TPU v7x, 128 devices: a whole 4x4x4 slice. The times are simulated.
128 devices in a mesh: gx: 8 (over z_hi, y), gy: 8 (over x, z_lo), gz: 2 (over core).
Axes of the slice: x: 4, y: 4, z: 4 (z_hi: 2, z_lo: 2; z = z_hi * 2 + z_lo), core: 2. Of those that a mesh axis runs over, the one named last changes fastest.
Arguments:
- diag_blocks: bfloat16 [8, 32, 4, 128, 128], P('gx', 'gy', 'gz'), as said below
- face_blocks: bfloat16 [6, 8, 32, 4, 128, 128], P(None, 'gx', 'gy', 'gz'), may hold values from -1.796875 to 1.796875
- split: int32 [8, 32, 4], P('gx', 'gy', 'gz'), may hold values from 0 to 1, as said below
Outputs:
- interp: bfloat16 [6, 8, 32, 4, 128, 128], P(None, 'gx', 'gy', 'gz')
- coarse: float32 [8, 32, 4, 128, 128], P('gx', 'gy', 'gz')
Inputs may be any that keep to these rules, and one draw needn't show every extreme that they name: `diag_blocks`: symmetric positive definite blocks. `split`: along the third dimension no two adjacent elements both have value 0, so every fine element has a coarse face neighbour.
All inputs are finite; a program needn't handle non-finite values.
Results may differ from a plain program's by a relative error of at most 0.00042.
Values may be sent and summed in bfloat16 or wider, within the bound.
No kernel may reach another device: no remote copies, remote signals or barrier semaphores. Data moves between devices by JAX's collectives and lax.ppermute only.
A program may use at most 128 MiB of HBM per device.

v0:
```python
import jax
import jax.numpy as jnp
from jax import lax
from jax.sharding import PartitionSpec as P


def with_halo(x, sides, width):
    edges = {}
    for axis, dim in sides:
        size, length = (lax.axis_size(axis), x.shape[dim])
        up = [(i, (i + 1) % size) for i in range(size - 1)]
        last = lax.slice_in_dim(x, length - width, length, axis=dim)
        initial = lax.slice_in_dim(x, 0, width, axis=dim)
        edges[dim] = (
            lax.ppermute(last, axis, up),
            lax.ppermute(initial, axis, [(b, a) for a, b in up]),
        )
    done = []
    for _, dim in sides:
        low, high = edges[dim]
        around = [(width, width) if d in done else (0, 0) for d in range(x.ndim)]
        x = jnp.concatenate([jnp.pad(low, around), x, jnp.pad(high, around)], axis=dim)
        done.append(dim)
    return x


def extended(block, sides, width):
    for axis, dim in sides:
        count = lax.axis_size(axis)
        forward = [(i, i + 1) for i in range(count - 1)]
        backward = [(target, source) for source, target in forward]
        low = lax.ppermute(
            lax.slice_in_dim(block, block.shape[dim] - width, None, axis=dim), axis, forward
        )
        high = lax.ppermute(lax.slice_in_dim(block, 0, width, axis=dim), axis, backward)
        block = jnp.concatenate([low, block, high], axis=dim)
    return block


def beside(padded, dimension, offset, leading):
    index = [slice(None)] * leading + [slice(1, -1)] * 3
    index = index + [slice(None)] * (padded.ndim - leading - 3)
    length = padded.shape[leading + dimension]
    index[leading + dimension] = slice(1 + offset, length - 1 + offset)
    return padded[tuple(index)]


def cho_apply(factor, right_side):
    forward = lax.linalg.triangular_solve(factor, right_side, left_side=True, lower=True)
    return lax.linalg.triangular_solve(
        factor, forward, left_side=True, lower=True, transpose_a=True
    )


def edge_rims(records, dimension):
    size = records.shape[2 + dimension]
    lower_rim = lax.slice_in_dim(records[2 * dimension], 0, 1, axis=1 + dimension)
    upper_rim = lax.slice_in_dim(records[2 * dimension + 1], size - 1, size, axis=1 + dimension)
    return jnp.concatenate([lower_rim, upper_rim], axis=1 + dimension)


def arrivals(records, padded, dimension):
    size = records.shape[2 + dimension]
    from_below = jnp.concatenate(
        [
            lax.slice_in_dim(padded, 0, 1, axis=1 + dimension),
            lax.slice_in_dim(records[2 * dimension + 1], 0, size - 1, axis=1 + dimension),
        ],
        axis=1 + dimension,
    )
    from_above = jnp.concatenate(
        [
            lax.slice_in_dim(records[2 * dimension], 1, size, axis=1 + dimension),
            lax.slice_in_dim(padded, 3, 4, axis=1 + dimension),
        ],
        axis=1 + dimension,
    )
    return (from_below, from_above)


def on_device(diag_blocks, face_blocks, split):
    grid = split.shape
    order = diag_blocks.shape[-1]
    number = grid[0] * grid[1] * grid[2]
    coords = (
        lax.axis_index("gx") * grid[0] + lax.broadcasted_iota(jnp.int32, grid, 0),
        lax.axis_index("gy") * grid[1] + lax.broadcasted_iota(jnp.int32, grid, 1),
        lax.axis_index("gz") * grid[2] + lax.broadcasted_iota(jnp.int32, grid, 2),
    )
    extent = (
        lax.axis_size("gx") * grid[0],
        lax.axis_size("gy") * grid[1],
        lax.axis_size("gz") * grid[2],
    )
    dense = diag_blocks.astype(jnp.float32)
    diag_norm = jnp.sqrt(jnp.sum(dense * dense, axis=(-2, -1)))
    facts = jnp.stack([diag_norm, split.astype(jnp.float32)])
    facts_pad = with_halo(facts, (("gx", 1), ("gy", 2), ("gz", 3)), 1)
    factor = jnp.linalg.cholesky(dense.reshape(number, order, order))
    is_coarse = split == 1
    total = jnp.zeros(grid, jnp.float32)
    denom = jnp.zeros(grid, jnp.float32)
    links = []
    for direction in range(6):
        dimension = direction // 2
        offset = 1 if direction % 2 else -1
        target = coords[dimension] + offset
        present = (target >= 0) & (target < extent[dimension])
        neighbour = beside(facts_pad, dimension, offset, 1)
        face = face_blocks[direction].astype(jnp.float32)
        face_norm = jnp.sqrt(jnp.sum(face * face, axis=(-2, -1)))
        other_norm = jnp.where(present, neighbour[0], 1.0)
        strength = jnp.where(present, face_norm / jnp.sqrt(diag_norm * other_norm), 0.0)
        linked = present & (neighbour[1] > 0.5)
        total = total + strength
        denom = denom + jnp.where(linked, strength, 0.0)
        links.append(linked)
    ratio = total / jnp.where(is_coarse, 1.0, denom)
    flat_diag = diag_blocks.reshape(number, order, order)
    interps = []
    contribs = []
    for direction in range(6):
        weight = jnp.where(links[direction] & ~is_coarse, -ratio, 0.0).reshape(number, 1, 1)
        right_side = face_blocks[direction].reshape(number, order, order).astype(jnp.float32)
        solved = cho_apply(factor, right_side)
        interp = (weight * solved).astype(jnp.bfloat16)
        mixed = (
            jnp.einsum("mab,mbc->mac", flat_diag, interp, preferred_element_type=jnp.float32)
            + right_side
        )
        contrib = jnp.einsum(
            "mba,mbc->mac", interp.astype(jnp.float32), mixed, precision=lax.Precision.HIGHEST
        )
        interps.append(interp)
        contribs.append(contrib.astype(jnp.bfloat16))
    interp_all = jnp.stack(interps).reshape((6,) + grid + (order, order))
    contrib_all = jnp.stack(contribs).reshape((6,) + grid + (order, order))
    records = jnp.stack([interp_all, contrib_all], axis=1)
    incoming = [None] * 6
    padded_x = extended(edge_rims(records, 0), (("gx", 1),), 1)
    incoming[0], incoming[1] = arrivals(records, padded_x, 0)
    padded_y = extended(edge_rims(records, 1), (("gy", 2),), 1)
    incoming[2], incoming[3] = arrivals(records, padded_y, 1)
    padded_z = extended(edge_rims(records, 2), (("gz", 3),), 1)
    incoming[4], incoming[5] = arrivals(records, padded_z, 2)
    summed = dense
    for direction in range(6):
        arrive = incoming[direction]
        product = jnp.einsum(
            "xyzab,xyzbc->xyzac",
            face_blocks[direction],
            arrive[0],
            preferred_element_type=jnp.float32,
        )
        summed = summed + arrive[1].astype(jnp.float32) + product
    coarse = jnp.where(is_coarse[..., None, None], summed, 0.0)
    return (interp_all, coarse)


def solution(mesh):
    in_specs = (
        P("gx", "gy", "gz", None, None),
        P(None, "gx", "gy", "gz", None, None),
        P("gx", "gy", "gz"),
    )
    out_specs = (P(None, "gx", "gy", "gz", None, None), P("gx", "gy", "gz", None, None))
    return jax.shard_map(
        on_device, mesh=mesh, in_specs=in_specs, out_specs=out_specs, check_vma=False
    )
```

profile of v0, /device:TPU:24, one launch (start us, length us, event | category | flops | bytes accessed | tf_op | source)
XLA Modules:
  0.0 294.0 jit_solution(17129066625924420973)
XLA Ops:
  0.6 0.8 convert_bitcast_fusion
  1.4 1.1 copy.205
  2.8 2.6 collective-permute-start.1
  5.5 6.8 %collective-permute-start = (f32[2,1,4,2]{2,3,1,0:T(2,128)S(1)}, f32[2,1,4,2]{2,3,1,0:T(2,128)S(1)}, u32[]{:S(2)}, u32[]{:S(2)}) collective-permute-start(f32[2,1,4,2]{2,3,1,0:T(2,128)S(1)} %pad_maximum_fusion.5), channel_id=1, source_target_pairs={{0,16},{16,32},{32,48},{48,64},{64,80},{80,96},{96,112},{1,17},{17... | collective-permute-start | bytes 200 | tf_op jit(solution)/shard_map/ppermute | solution.py:15
  12.3 1.3 collective-permute-start.4
  13.6 1.3 collective-permute-start.5
  15.0 3.8 %collective-permute-start.2 = (f32[2,1,1,2]{2,3,1,0:T(2,128)S(1)}, f32[2,1,1,2]{2,3,1,0:T(2,128)S(1)}, u32[]{:S(2)}, u32[]{:S(2)}) collective-permute-start(f32[2,1,1,2]{2,3,1,0:T(2,128)S(1)} %get-tuple-element.54), channel_id=1, source_target_pairs={{0,2},{2,4},{4,6},{6,8},{8,10},{10,12},{12,14},{1,3},{3,5},{5,7},{... | collective-permute-start | bytes 56 | tf_op jit(solution)/shard_map/ppermute | solution.py:15
  18.8 0.8 copy.208
  19.6 1.8 multiply_reduce_fusion.5
  21.4 1.5 slice_convert_fusion
  23.2 0.9 fusion.32
  24.1 94.6 %custom-call.10 = f32[8,128,128]{2,1,0:T(8,128)S(1)} custom-call(f32[8,128,128]{2,1,0:T(8,128)} %fusion.32), custom_call_target="Cholesky" | custom-call | tf_op jit(solution)/shard_map/jit(cholesky)/cholesky | solution.py:99
  118.8 0.9 select_bitcast_fusion
  119.8 79.6 %custom-call.22 = f32[8,1,128,128]{2,3,1,0:T(8,128)S(1)} custom-call(f32[8,1,128,128]{3,2,1,0:T(8,128)} %select_bitcast_fusion), custom_call_target="InvertDiagBlocksLowerTriangular" | custom-call | tf_op jit(solution)/shard_map/triangular_solve/custom-call.2 | solution.py:50
  199.4 2.9 fusion.39
  202.3 2.9 fusion.33
  205.2 1.8 fusion.42
  207.0 1.8 fusion.45
  208.9 1.8 fusion.48
  210.7 1.8 fusion.36
  212.6 1.6 collective-permute-start.3
  214.2 3.9 %collective-permute-done.3 = f32[2,1,1,2]{2,3,1,0:T(2,128)S(1)} collective-permute-done((f32[2,1,1,2]{2,3,1,0:T(2,128)S(1)}, f32[2,1,1,2]{2,3,1,0:T(2,128)S(1)}, u32[]{:S(2)}, u32[]{:S(2)}) %collective-permute-start.3) | collective-permute-done | bytes 48 | tf_op jit(solution)/shard_map/ppermute | solution.py:16
  220.5 1.7 fusion.15
  222.4 0.4 convolution_convert_fusion.2
  222.9 0.8 copy.284
  223.8 0.9 copy.260
  224.6 1.7 fusion.17
  226.3 1.3 fusion.5
  227.6 0.4 convolution_convert_fusion
  228.0 0.9 copy.286
  228.9 0.9 copy.262
  229.8 1.7 fusion.14
  231.7 1.2 convolution_convert_fusion.3
  232.9 1.8 copy.283
  234.7 0.8 copy.259
  235.5 1.7 fusion.13
  237.5 0.5 copy-done.2
  238.0 1.2 convolution_convert_fusion.4
  239.2 1.8 copy.282
  240.9 1.8 copy.258
  242.7 1.7 fusion.12
  244.7 0.5 copy-done.6
  245.2 1.2 convolution_convert_fusion.5
  246.4 1.8 copy.281
  248.2 1.8 copy.257
  250.0 1.7 fusion.16
  252.0 0.5 copy-done.4
  252.9 0.9 copy.285
  253.7 1.8 copy.261
  255.6 1.0 constant_dynamic-update-slice_fusion.11
  256.6 1.0 constant_dynamic-update-slice_fusion.10
  257.7 1.0 constant_dynamic-update-slice_fusion.9
  259.1 0.6 copy-done.23
  260.2 4.0 %collective-permute-start.8 = (bf16[2,1,1,2,128,128]{4,5,3,2,0,1:T(8,128)(2,1)S(1)}, bf16[2,1,1,2,128,128]{4,5,3,2,0,1:T(8,128)(2,1)S(1)}, u32[]{:S(2)}, u32[]{:S(2)}) collective-permute-start(bf16[2,1,1,2,128,128]{4,5,3,2,0,1:T(8,128)(2,1)S(1)} %slice.260), channel_id=1, source_target_pairs={{0,2},{2,4},{4,6},{6,8},{8,10},{10,12},{12,14},{1,3},{3,5},{5,7},{... | collective-permute-start | bytes 393224 | tf_op jit(solution)/shard_map/ppermute | solution.py:32
  264.2 1.3 collective-permute-start.9
  265.6 1.3 collective-permute-start.11
  266.9 3.2 %collective-permute-start.10 = (bf16[2,1,4,1,128,128]{4,5,3,2,0,1:T(8,128)(2,1)S(1)}, bf16[2,1,4,1,128,128]{4,5,3,2,0,1:T(8,128)(2,1)S(1)}, u32[]{:S(2)}, u32[]{:S(2)}) collective-permute-start(bf16[2,1,4,1,128,128]{4,5,3,2,0,1:T(8,128)(2,1)S(1)} %get-tuple-element.33), channel_id=1, source_target_pairs={{0,1},{2,3},{4,5},{6,7},{8,9},{10,11},{12,13},{14,15},{16,17},{18,... | collective-permute-start | bytes 786440 | tf_op jit(solution)/shard_map/ppermute | solution.py:32
  270.1 2.1 collective-permute-start.6
  272.5 1.1 copy-done.26
  273.6 3.7 %collective-permute-start.7 = (bf16[2,1,4,2,128,128]{4,5,3,2,0,1:T(8,128)(2,1)S(1)}, bf16[2,1,4,2,128,128]{4,5,3,2,0,1:T(8,128)(2,1)S(1)}, u32[]{:S(2)}, u32[]{:S(2)}) collective-permute-start(bf16[2,1,4,2,128,128]{4,5,3,2,0,1:T(8,128)(2,1)S(1)} %get-tuple-element.23), channel_id=1, source_target_pairs={{16,0},{32,16},{48,32},{64,48},{80,64},{96,80},{112,96},{17,1},{33... | collective-permute-start | bytes 1572872 | tf_op jit(solution)/shard_map/ppermute | solution.py:35
  278.3 6.9 %collective-permute-done.6 = bf16[2,1,4,2,128,128]{4,5,3,2,1,0:T(8,128)(2,1)S(1)} collective-permute-done((bf16[2,1,4,2,128,128]{4,5,3,2,1,0:T(8,128)(2,1)S(1)}, bf16[2,1,4,2,128,128]{4,5,3,2,1,0:T(8,128)(2,1)S(1)}, u32[]{:S(2)}, u32[]{:S(2)}) %collective-permute-start.6) | collective-permute-done | bytes 524320 | tf_op jit(solution)/shard_map/ppermute | solution.py:32
  285.5 6.7 %collective-permute-done.7 = bf16[2,1,4,2,128,128]{4,5,3,2,0,1:T(8,128)(2,1)S(1)} collective-permute-done((bf16[2,1,4,2,128,128]{4,5,3,2,0,1:T(8,128)(2,1)S(1)}, bf16[2,1,4,2,128,128]{4,5,3,2,0,1:T(8,128)(2,1)S(1)}, u32[]{:S(2)}, u32[]{:S(2)}) %collective-permute-start.7) | collective-permute-done | bytes 524320 | tf_op jit(solution)/shard_map/ppermute | solution.py:35
  292.5 0.5 fusion.11
  293.0 1.0 copy.288
  (132 shorter events, 7.2 us)
Async XLA Ops:
  0.6 20.8 %copy-start = (bf16[6,1,4,2,128,128]{5,4,3,2,1,0:T(8,128)(2,1)S(1)}, bf16[6,1,4,2,128,128]{5,4,3,2,1,0:T(8,128)(2,1)}, u32[]{:S(2)}) copy-start(bf16[6,1,4,2,128,128]{5,4,3,2,1,0:T(8,128)(2,1)} %param.8) | copy-start | bytes 4718596
  2.8 215.4 %collective-permute-start.1 = (f32[2,1,4,2]{2,3,1,0:T(2,128)S(1)}, f32[2,1,4,2]{2,3,1,0:T(2,128)S(1)}, u32[]{:S(2)}, u32[]{:S(2)}) collective-permute-start(f32[2,1,4,2]{2,3,1,0:T(2,128)S(1)} %pad_maximum_fusion.5), channel_id=1, source_target_pairs={{16,0},{32,16},{48,32},{64,48},{80,64},{96,80},{112,96},{17,1},{33... | collective-permute-start | bytes 200 | tf_op jit(solution)/shard_map/ppermute | solution.py:16
  5.5 212.7 %collective-permute-start = (f32[2,1,4,2]{2,3,1,0:T(2,128)S(1)}, f32[2,1,4,2]{2,3,1,0:T(2,128)S(1)}, u32[]{:S(2)}, u32[]{:S(2)}) collective-permute-start(f32[2,1,4,2]{2,3,1,0:T(2,128)S(1)} %pad_maximum_fusion.5), channel_id=1, source_target_pairs={{0,16},{16,32},{32,48},{48,64},{64,80},{80,96},{96,112},{1,17},{17... | collective-permute-start | bytes 200 | tf_op jit(solution)/shard_map/ppermute | solution.py:15
  12.3 205.9 %collective-permute-start.4 = (f32[2,1,4,1]{2,3,1,0:T(1,128)S(1)}, f32[2,1,4,1]{2,3,1,0:T(1,128)S(1)}, u32[]{:S(2)}, u32[]{:S(2)}) collective-permute-start(f32[2,1,4,1]{2,3,1,0:T(1,128)S(1)} %get-tuple-element.52), channel_id=1, source_target_pairs={{0,1},{2,3},{4,5},{6,7},{8,9},{10,11},{12,13},{14,15},{16,17},{18,... | collective-permute-start | bytes 104 | tf_op jit(solution)/shard_map/ppermute | solution.py:15
  13.6 204.6 %collective-permute-start.5 = (f32[2,1,4,1]{2,3,1,0:T(1,128)S(1)}, f32[2,1,4,1]{2,3,1,0:T(1,128)S(1)}, u32[]{:S(2)}, u32[]{:S(2)}) collective-permute-start(f32[2,1,4,1]{2,3,1,0:T(1,128)S(1)} %get-tuple-element.53), channel_id=1, source_target_pairs={{1,0},{3,2},{5,4},{7,6},{9,8},{11,10},{13,12},{15,14},{17,16},{19,... | collective-permute-start | bytes 104 | tf_op jit(solution)/shard_map/ppermute | solution.py:16
  15.0 197.6 %collective-permute-start.2 = (f32[2,1,1,2]{2,3,1,0:T(2,128)S(1)}, f32[2,1,1,2]{2,3,1,0:T(2,128)S(1)}, u32[]{:S(2)}, u32[]{:S(2)}) collective-permute-start(f32[2,1,1,2]{2,3,1,0:T(2,128)S(1)} %get-tuple-element.54), channel_id=1, source_target_pairs={{0,2},{2,4},{4,6},{6,8},{8,10},{10,12},{12,14},{1,3},{3,5},{5,7},{... | collective-permute-start | bytes 56 | tf_op jit(solution)/shard_map/ppermute | solution.py:15
  23.0 187.8 %copy-start.8 = (f32[1,1,4,2,128,128]{5,4,3,2,1,0:T(8,128)}, f32[1,1,4,2,128,128]{5,4,3,2,1,0:T(8,128)S(1)}, u32[]{:S(2)}) copy-start(f32[1,1,4,2,128,128]{5,4,3,2,1,0:T(8,128)S(1)} %get-tuple-element.32) | copy-start | bytes 1572868
  199.4 5.8 %copy-start.14 = (f32[1,1,4,2,128,128]{5,4,3,2,1,0:T(8,128)S(1)}, f32[1,1,4,2,128,128]{5,4,3,2,1,0:T(8,128)}, u32[]{:S(2)}) copy-start(f32[1,1,4,2,128,128]{5,4,3,2,1,0:T(8,128)} %get-tuple-element.29) | copy-start | bytes 1572868
  202.3 4.8 %copy-start.12 = (f32[1,1,4,2,128,128]{5,4,3,2,1,0:T(8,128)S(1)}, f32[1,1,4,2,128,128]{5,4,3,2,1,0:T(8,128)}, u32[]{:S(2)}) copy-start(f32[1,1,4,2,128,128]{5,4,3,2,1,0:T(8,128)} %get-tuple-element.30) | copy-start | bytes 1572868
  205.2 3.7 %copy-start.10 = (f32[1,1,4,2,128,128]{5,4,3,2,1,0:T(8,128)S(1)}, f32[1,1,4,2,128,128]{5,4,3,2,1,0:T(8,128)}, u32[]{:S(2)}) copy-start(f32[1,1,4,2,128,128]{5,4,3,2,1,0:T(8,128)} %get-tuple-element.31) | copy-start | bytes 1572868
  210.7 11.5 %copy-start.1 = (bf16[1,4,2,128,128]{4,3,2,1,0:T(8,128)(2,1)S(1)}, bf16[1,4,2,128,128]{4,3,2,1,0:T(8,128)(2,1)}, u32[]{:S(2)}) copy-start(bf16[1,4,2,128,128]{4,3,2,1,0:T(8,128)(2,1)} %param.7) | copy-start | bytes 786436
  212.6 9.6 %copy-start.16 = (f32[1,1,4,2,128,128]{5,4,3,2,1,0:T(8,128)S(1)}, f32[1,1,4,2,128,128]{5,4,3,2,1,0:T(8,128)}, u32[]{:S(2)}) copy-start(f32[1,1,4,2,128,128]{5,4,3,2,1,0:T(8,128)} %get-tuple-element.28) | copy-start | bytes 1572868
  212.6 5.6 %collective-permute-start.3 = (f32[2,1,1,2]{2,3,1,0:T(2,128)S(1)}, f32[2,1,1,2]{2,3,1,0:T(2,128)S(1)}, u32[]{:S(2)}, u32[]{:S(2)}) collective-permute-start(f32[2,1,1,2]{2,3,1,0:T(2,128)S(1)} %get-tuple-element.55), channel_id=1, source_target_pairs={{2,0},{4,2},{6,4},{8,6},{10,8},{12,10},{14,12},{3,1},{5,3},{7,5},{... | collective-permute-start | bytes 56 | tf_op jit(solution)/shard_map/ppermute | solution.py:16
  229.7 1.7 copy-start.15
  235.5 1.7 copy-start.13
  237.3 0.7 copy-start.2
  242.7 1.7 copy-start.11
  244.5 0.7 copy-start.6
  250.0 1.7 copy-start.9
  251.7 0.7 copy-start.4
  252.4 4.2 %copy-start.24 = (bf16[1,1,1,4,2,128,128]{5,6,4,3,1,2,0:T(8,128)(2,1)S(1)}, bf16[1,1,1,4,2,128,128]{5,6,4,3,1,2,0:T(8,128)(2,1)}, u32[]{:S(2)}) copy-start(bf16[1,1,1,4,2,128,128]{5,6,4,3,1,2,0:T(8,128)(2,1)} %copy.281) | copy-start | bytes 786436
  252.9 5.8 %copy-start.19 = (bf16[1,1,1,4,2,128,128]{5,6,4,3,1,2,0:T(8,128)(2,1)S(1)}, bf16[1,1,1,4,2,128,128]{5,6,4,3,1,2,0:T(8,128)(2,1)}, u32[]{:S(2)}) copy-start(bf16[1,1,1,4,2,128,128]{5,6,4,3,1,2,0:T(8,128)(2,1)} %copy.260) | copy-start | bytes 786436
  255.5 3.2 %copy-start.25 = (bf16[1,1,1,4,2,128,128]{5,6,4,3,1,2,0:T(8,128)(2,1)S(1)}, bf16[1,1,1,4,2,128,128]{5,6,4,3,1,2,0:T(8,128)(2,1)}, u32[]{:S(2)}) copy-start(bf16[1,1,1,4,2,128,128]{5,6,4,3,1,2,0:T(8,128)(2,1)} %copy.261) | copy-start | bytes 786436
  255.6 3.3 %copy-start.20 = (bf16[1,1,1,4,2,128,128]{5,6,4,3,1,2,0:T(8,128)(2,1)S(1)}, bf16[1,1,1,4,2,128,128]{5,6,4,3,1,2,0:T(8,128)(2,1)}, u32[]{:S(2)}) copy-start(bf16[1,1,1,4,2,128,128]{5,6,4,3,1,2,0:T(8,128)(2,1)} %copy.262) | copy-start | bytes 786436
  256.6 2.3 copy-start.22
  256.6 2.3 copy-start.21
  257.7 1.3 copy-start.17
  258.7 1.0 copy-start.23
  258.8 1.0 copy-start.18
  260.2 12.1 %copy-start.7 = (bf16[8,128,128]{2,1,0:T(8,128)(2,1)S(1)}, bf16[8,128,128]{2,1,0:T(8,128)(2,1)}, u32[]{:S(2)}) copy-start(bf16[8,128,128]{2,1,0:T(8,128)(2,1)} %copy-done.6) | copy-start | bytes 786436
  260.2 12.1 %copy-start.3 = (bf16[8,128,128]{2,1,0:T(8,128)(2,1)S(1)}, bf16[8,128,128]{2,1,0:T(8,128)(2,1)}, u32[]{:S(2)}) copy-start(bf16[8,128,128]{2,1,0:T(8,128)(2,1)} %copy-done.2) | copy-start | bytes 786436
  260.2 12.3 %collective-permute-start.8 = (bf16[2,1,1,2,128,128]{4,5,3,2,0,1:T(8,128)(2,1)S(1)}, bf16[2,1,1,2,128,128]{4,5,3,2,0,1:T(8,128)(2,1)S(1)}, u32[]{:S(2)}, u32[]{:S(2)}) collective-permute-start(bf16[2,1,1,2,128,128]{4,5,3,2,0,1:T(8,128)(2,1)S(1)} %slice.260), channel_id=1, source_target_pairs={{0,2},{2,4},{4,6},{6,8},{8,10},{10,12},{12,14},{1,3},{3,5},{5,7},{... | collective-permute-start | bytes 393224 | tf_op jit(solution)/shard_map/ppermute | solution.py:32
  264.2 28.3 %collective-permute-start.9 = (bf16[2,1,1,2,128,128]{4,5,3,2,0,1:T(8,128)(2,1)S(1)}, bf16[2,1,1,2,128,128]{4,5,3,2,0,1:T(8,128)(2,1)S(1)}, u32[]{:S(2)}, u32[]{:S(2)}) collective-permute-start(bf16[2,1,1,2,128,128]{4,5,3,2,0,1:T(8,128)(2,1)S(1)} %slice.267), channel_id=1, source_target_pairs={{2,0},{4,2},{6,4},{8,6},{10,8},{12,10},{14,12},{3,1},{5,3},{7,5},{... | collective-permute-start | bytes 393224 | tf_op jit(solution)/shard_map/ppermute | solution.py:35
  265.6 12.1 %collective-permute-start.11 = (bf16[2,1,4,1,128,128]{4,5,3,2,1,0:T(8,128)(2,1)S(1)}, bf16[2,1,4,1,128,128]{4,5,3,2,1,0:T(8,128)(2,1)S(1)}, u32[]{:S(2)}, u32[]{:S(2)}) collective-permute-start(bf16[2,1,4,1,128,128]{4,5,3,2,1,0:T(8,128)(2,1)S(1)} %get-tuple-element.36), channel_id=1, source_target_pairs={{1,0},{3,2},{5,4},{7,6},{9,8},{11,10},{13,12},{15,14},{17,16},{19,... | collective-permute-start | bytes 786440 | tf_op jit(solution)/shard_map/ppermute | solution.py:35
  266.9 5.5 %copy-start.5 = (bf16[8,128,128]{2,1,0:T(8,128)(2,1)S(1)}, bf16[8,128,128]{2,1,0:T(8,128)(2,1)}, u32[]{:S(2)}) copy-start(bf16[8,128,128]{2,1,0:T(8,128)(2,1)} %copy-done.4) | copy-start | bytes 786436
  266.9 11.1 %collective-permute-start.10 = (bf16[2,1,4,1,128,128]{4,5,3,2,0,1:T(8,128)(2,1)S(1)}, bf16[2,1,4,1,128,128]{4,5,3,2,0,1:T(8,128)(2,1)S(1)}, u32[]{:S(2)}, u32[]{:S(2)}) collective-permute-start(bf16[2,1,4,1,128,128]{4,5,3,2,0,1:T(8,128)(2,1)S(1)} %get-tuple-element.33), channel_id=1, source_target_pairs={{0,1},{2,3},{4,5},{6,7},{8,9},{10,11},{12,13},{14,15},{16,17},{18,... | collective-permute-start | bytes 786440 | tf_op jit(solution)/shard_map/ppermute | solution.py:32
  270.1 15.1 %collective-permute-start.6 = (bf16[2,1,4,2,128,128]{4,5,3,2,1,0:T(8,128)(2,1)S(1)}, bf16[2,1,4,2,128,128]{4,5,3,2,1,0:T(8,128)(2,1)S(1)}, u32[]{:S(2)}, u32[]{:S(2)}) collective-permute-start(bf16[2,1,4,2,128,128]{4,5,3,2,1,0:T(8,128)(2,1)S(1)} %get-tuple-element.22), channel_id=1, source_target_pairs={{0,16},{16,32},{32,48},{48,64},{64,80},{80,96},{96,112},{1,17},{17... | collective-permute-start | bytes 1572872 | tf_op jit(solution)/shard_map/ppermute | solution.py:32
  272.5 1.1 copy-start.26
  273.6 18.5 %collective-permute-start.7 = (bf16[2,1,4,2,128,128]{4,5,3,2,0,1:T(8,128)(2,1)S(1)}, bf16[2,1,4,2,128,128]{4,5,3,2,0,1:T(8,128)(2,1)S(1)}, u32[]{:S(2)}, u32[]{:S(2)}) collective-permute-start(bf16[2,1,4,2,128,128]{4,5,3,2,0,1:T(8,128)(2,1)S(1)} %get-tuple-element.23), channel_id=1, source_target_pairs={{16,0},{32,16},{48,32},{64,48},{80,64},{96,80},{112,96},{17,1},{33... | collective-permute-start | bytes 1572872 | tf_op jit(solution)/shard_map/ppermute | solution.py:35
where the time goes:
time: 297 us; the launch traced here: 294 us
  other arithmetic  181 us (61%)
  starting transfers between devices  33.1 us (11%)
  matrix products  32.7 us (11%)
  local copies, waits for them, and re-layouts  28 us (9%)
  waiting for transfers between devices  17.5 us (6%)
    another operation x4, other arithmetic, on_device(): factor = jnp.linalg.cholesky(dense.reshape(number, order, order))  94.7 us
    another operation x3, other arithmetic, cho_apply(): lax.linalg.triangular_solve(factor, forward, left_side=True, lower=True,...  80.5 us
    another operation x6, matrix products, cho_apply(): lax.linalg.triangular_solve(factor, right_side, left_side=True, lower=True)  13.2 us
    ppermute x3, starting transfers between devices, with_halo(): lax.ppermute(last, axis, up)  11.9 us
    another operation x6, matrix products, cho_apply(): lax.linalg.triangular_solve(factor, forward, left_side=True, lower=True,...  10.3 us
    unnamed x72, local copies, waits for them, and re-layouts  9.67 us
    ppermute x3, starting transfers between devices, extended(): lax.ppermute(lax.slice_in_dim(block, block.shape[dim] - width, None, axis...  9.26 us
    another operation x8, local copies, waits for them, and re-layouts, on_device(): interp_all = jnp.stack(interps).reshape((6,) + grid + (order, order))  8.04 us
  transfers between devices with their start and end apart: 12, of which 3 were waited for; matrix products, arithmetic and copies ran while one was open for 67% of the time, Pallas kernels for 0%

commit v1 on v0

v1 whole, which is shorter than its diff:
```python
import jax
import jax.numpy as jnp
from jax import lax
from jax.experimental import pallas as pl
from jax.experimental.pallas import tpu as pltpu
from jax.sharding import PartitionSpec as P

B = 128
F32 = jnp.float32
BF16 = jnp.bfloat16
VMEM = pl.BlockSpec(memory_space=pltpu.VMEM)
SMEM = pl.BlockSpec(memory_space=pltpu.SMEM)
LIMIT = 24 * 1024 * 1024


def mm(a, b):
    return jnp.dot(a, b, preferred_element_type=F32)


def mm32(a, b):
    return jnp.dot(a, b, preferred_element_type=F32, precision=lax.Precision.HIGHEST)


def mm_t(a, b):
    return lax.dot_general(a, b, (((0,), (0,)), ((), ())), preferred_element_type=F32)


def halves(x):
    hi = x.astype(BF16)
    return hi, (x - hi.astype(F32)).astype(BF16)


def thirds(x):
    hi = x.astype(BF16)
    rest = x - hi.astype(F32)
    mid = rest.astype(BF16)
    return hi, mid, (rest - mid.astype(F32)).astype(BF16)


def wide(x):
    return jnp.concatenate([x, x], axis=0)


def fine_of(split_ref, column):
    return jnp.where(split_ref[2 * column] == 0, 0, 1)


def block_norms(load, rows):
    for e in range(8):
        x = load(e).astype(F32)
        rows[pl.ds(e, 1), :] = jnp.sum(x * x, axis=0, keepdims=True)
    total = jnp.sum(rows[...], axis=1, keepdims=True)
    return jnp.broadcast_to(jnp.sqrt(total), (8, B))


def facts_kernel(split_ref, diag_ref, facts_ref, rows):
    facts_ref[pl.ds(0, 8), :] = block_norms(lambda e: diag_ref[e], rows)
    for e in range(8):
        facts_ref[pl.ds(8 + e, 1), :] = jnp.full((1, B), split_ref[e].astype(F32), F32)


def inverse_kernel(split_ref, diag_ref, face_ref, inv_ref, fnorm_ref, rows, work):
    cols = range(4)
    eye = (
        lax.broadcasted_iota(jnp.int32, (B, B), 0) == lax.broadcasted_iota(jnp.int32, (B, B), 1)
    )
    one = jnp.where(eye, 1.0, 0.0).astype(F32)
    mats = [diag_ref[2 * c + fine_of(split_ref, c)] for c in cols]
    scaled, starts, scales = [], [], []
    for c in cols:
        a = mats[c].astype(F32)
        picked = jnp.where(eye, a, 0.0)
        down = lax.rsqrt(jnp.sum(picked, axis=1, keepdims=True))
        along = lax.rsqrt(jnp.sum(picked, axis=0, keepdims=True))
        a = a * down * along
        bound = jnp.max(jnp.sum(jnp.abs(a), axis=0, keepdims=True), axis=1, keepdims=True)
        scaled.append(a)
        starts.append(1.9 / bound)
        scales.append((down, along))
    powers = [one - starts[c] * scaled[c] for c in cols]
    sums = [one + powers[c] for c in cols]
    powers = [p.astype(BF16) for p in powers]
    for _ in range(4):
        powers = [mm(p, p).astype(BF16) for p in powers]
        sums = [s + mm(s.astype(BF16), p) for s, p in zip(sums, powers)]
    guess = [
        (sums[c] * (starts[c] * scales[c][0]) * scales[c][1]).astype(BF16) for c in cols
    ]
    left = [one - mm(mats[c], guess[c]) for c in cols]
    small = [r.astype(BF16) for r in left]
    left = [r + mm(b, b) for r, b in zip(left, small)]
    better = []
    for c in cols:
        hi, lo = halves(left[c])
        better.append(guess[c].astype(F32) + (mm(guess[c], hi) + mm(guess[c], lo)))
    pairs = [halves(x) for x in better]
    left = [one - (mm(mats[c], pairs[c][0]) + mm(mats[c], pairs[c][1])) for c in cols]
    worst = jnp.zeros((1, B), F32)
    for c in cols:
        hi, lo = pairs[c]
        rhi, rlo = halves(left[c])
        fixed = (hi.astype(F32) + lo.astype(F32)) + (mm(hi, rhi) + (mm(hi, rlo) + mm(lo, rhi)))
        inv_ref[0, c], inv_ref[1, c], inv_ref[2, c] = thirds(fixed)
        worst = worst + jnp.sum(jnp.abs(left[c]), axis=0, keepdims=True)
    reached = jnp.max(worst) <= 1e-3

    @pl.when(jnp.logical_not(reached))
    def _():
        for c in cols:
            a = mats[c].astype(F32)
            picked = jnp.where(eye, a, 0.0)
            down = lax.rsqrt(jnp.sum(picked, axis=1, keepdims=True))
            along = lax.rsqrt(jnp.sum(picked, axis=0, keepdims=True))
            a = a * down * along
            bound = jnp.max(jnp.sum(jnp.abs(a), axis=0, keepdims=True), axis=1, keepdims=True)
            work[0] = a
            work[1] = one * (1.9 / bound)

            @pl.loop(0, 48)
            def _(_):
                x = work[1]
                work[1] = x + mm32(x, one - mm32(work[0], x))

            inv_ref[0, c], inv_ref[1, c], inv_ref[2, c] = thirds(work[1] * down * along)

    for d in range(6):
        fnorm_ref[d] = block_norms(lambda e: face_ref[d, e], rows)


def shifted(own, beyond, step, edge):
    return jnp.where(edge, pltpu.roll(beyond, step, 0), pltpu.roll(own, step, 0))


def weights_of(facts_ref, halo_refs, fnorm_ref, weight_ref):
    gx, gy, gz = lax.axis_index("gx"), lax.axis_index("gy"), lax.axis_index("gz")
    ha, hb, hc, hd, hz = halo_refs
    row = lax.broadcasted_iota(jnp.int32, (8, B), 0)
    depth = row % 2
    even_x, even_y = gx % 2 == 0, gy % 2 == 0

    def pick(test, first, second, part):
        rows = pl.ds(8 * part, 8)
        return jnp.where(test, first[rows, :], second[rows, :])

    def neighbours(part):
        own = facts_ref[pl.ds(8 * part, 8), :]
        z = hz[pl.ds(8 * part, 8), :]
        return (
            pick(even_x, hb, ha, part),
            pick(even_x, ha, hb, part),
            shifted(own, pick(even_y, hd, hc, part), 2, row < 2),
            shifted(own, pick(even_y, hc, hd, part), 6, row >= 6),
            jnp.where(depth == 0, pltpu.roll(z, 7, 0), pltpu.roll(own, 1, 0)),
            jnp.where(depth == 1, pltpu.roll(z, 1, 0), pltpu.roll(own, 7, 0)),
        )

    present = (
        jnp.broadcast_to(gx > 0, (8, B)),
        jnp.broadcast_to(gx < lax.axis_size("gx") - 1, (8, B)),
        (row >= 2) | (gy > 0),
        (row < 6) | (gy < lax.axis_size("gy") - 1),
        (depth == 1) | (gz > 0),
        (depth == 0) | (gz < lax.axis_size("gz") - 1),
    )
    own_norm = facts_ref[pl.ds(0, 8), :]
    fine = facts_ref[pl.ds(8, 8), :] < 0.5
    norms, splits = neighbours(0), neighbours(1)
    total = jnp.zeros((8, B), F32)
    denom = jnp.zeros((8, B), F32)
    links = []
    for d in range(6):
        other = jnp.where(present[d], norms[d], 1.0)
        strength = jnp.where(present[d], fnorm_ref[d] / jnp.sqrt(own_norm * other), 0.0)
        linked = present[d] & (splits[d] > 0.5)
        total = total + strength
        denom = denom + jnp.where(linked, strength, 0.0)
        links.append(linked)
    ratio = total / jnp.where(fine, denom, 1.0)
    for d in range(6):
        weight_ref[d] = jnp.where(links[d] & fine, -ratio, 0.0)


def interp_kernel(
    split_ref, diag_ref, face_ref, inv_ref, fnorm_ref, facts_ref, ha, hb, hc, hd, hz,
    interp_ref, near_ref, code_ref, xa_ref, xb_ref, ya_ref, yb_ref, z_ref, weight_ref,
):
    weights_of(facts_ref, (ha, hb, hc, hd, hz), fnorm_ref, weight_ref)
    gx, gy, gz = lax.axis_index("gx"), lax.axis_index("gy"), lax.axis_index("gz")
    row = lax.broadcasted_iota(jnp.int32, (8, B), 0)
    lane = lax.broadcasted_iota(jnp.int32, (8, B), 1)
    bit = jnp.where((row % 2 == 0) & (lane == 0), 1, 0) * lax.shift_left(1, row // 2)
    code = jnp.zeros((8, B), F32)
    for place, ref in enumerate((ha, hb, hc, hd)):
        code = code + ref[pl.ds(8, 8), :] * (bit * (1 << (4 * place))).astype(F32)
    code_ref[0] = jnp.sum(code).astype(jnp.int32)
    zero = jnp.zeros((B, B), BF16)
    for c in range(4):
        z = fine_of(split_ref, c)
        e = 2 * c + z
        a = diag_ref[e]
        inv = jnp.concatenate([inv_ref[0, c], inv_ref[1, c]], axis=1)
        last = inv_ref[2, c]
        for d in range(6):
            face = face_ref[d, e]
            solved = mm(inv, wide(face)) + mm(last, face)
            interp = (weight_ref[d, pl.ds(e, 1), :] * solved).astype(BF16)
            interp_ref[d, e] = interp
            interp_ref[d, 2 * c + 1 - z] = zero
            hi, lo = halves(mm(a, interp) + face.astype(F32))
            contrib = (mm_t(interp, hi) + mm_t(interp, lo)).astype(BF16)
            if d < 2:
                first = gx % 2 == 1 - d

                @pl.when(first)
                def _():
                    xa_ref[0, c], xa_ref[1, c] = interp, contrib

                @pl.when(jnp.logical_not(first))
                def _():
                    xb_ref[0, c], xb_ref[1, c] = interp, contrib
            elif d < 4:
                if c == (0, 3)[d - 2]:
                    first = gy % 2 == 3 - d

                    @pl.when(first)
                    def _():
                        ya_ref[0, 0], ya_ref[1, 0] = interp, contrib

                    @pl.when(jnp.logical_not(first))
                    def _():
                        yb_ref[0, 0], yb_ref[1, 0] = interp, contrib
                else:
                    near_ref[d - 2, c] = contrib
            else:
                inside = z == 5 - d

                @pl.when(inside)
                def _():
                    near_ref[2, c] = contrib

                @pl.when(jnp.logical_not(inside) & (gz == 5 - d))
                def _():
                    z_ref[0, c], z_ref[1, c] = interp, contrib

        @pl.when(z == gz)
        def _():
            z_ref[0, c], z_ref[1, c] = zero, zero


def coarse_kernel(
    split_ref, code_ref, diag_ref, face_ref, interp_ref, near_ref,
    xa_ref, xb_ref, ya_ref, yb_ref, z_ref, coarse_ref,
):
    gx, gy, gz = lax.axis_index("gx"), lax.axis_index("gy"), lax.axis_index("gz")
    code = code_ref[0]
    for e in range(8):
        coarse_ref[e] = diag_ref[e].astype(F32)

    def add(target, d, interp, contrib):
        coarse_ref[target] = coarse_ref[target] + (
            contrib.astype(F32) + mm(face_ref[d, target], interp)
        )

    def bit_at(place):
        return lax.shift_right_logical(code, place) & 1

    for c in range(4):
        add(2 * c + bit_at(c), jnp.where(gx % 2 == 0, 1, 0), xa_ref[0, c], xa_ref[1, c])
        add(2 * c + bit_at(4 + c), jnp.where(gx % 2 == 0, 0, 1), xb_ref[0, c], xb_ref[1, c])
        if c > 0:
            z = fine_of(split_ref, c - 1)
            add(2 * c + z, 2, interp_ref[3, 2 * (c - 1) + z], near_ref[1, c - 1])
        if c < 3:
            z = fine_of(split_ref, c + 1)
            add(2 * c + z, 3, interp_ref[2, 2 * (c + 1) + z], near_ref[0, c + 1])
        z = fine_of(split_ref, c)
        add(2 * c + 1 - z, 4 + z, interp_ref[5 - z, 2 * c + z], near_ref[2, c])
        add(2 * c + 1 - gz, 5 - gz, z_ref[0, c], z_ref[1, c])
    up = gy % 2 == 0
    code_a = jnp.where(up, bit_at(8), bit_at(11))
    code_b = jnp.where(up, bit_at(15), bit_at(12))
    add(jnp.where(up, 6, 0) + code_a, jnp.where(up, 3, 2), ya_ref[0, 0], ya_ref[1, 0])
    add(jnp.where(up, 0, 6) + code_b, jnp.where(up, 2, 3), yb_ref[0, 0], yb_ref[1, 0])
    for e in range(8):
        coarse_ref[e] = jnp.where(split_ref[e] == 1, coarse_ref[e], 0.0)


def matching(size, start):
    pairs = [(i, i + 1) for i in range(start, size - 1, 2)]
    return pairs + [(b, a) for a, b in pairs]


def swap(x, axis, start):
    return lax.ppermute(x, axis, matching(lax.axis_size(axis), start))


def call(body, out_shape, in_specs, out_specs, scratch, flops, name):
    return pl.pallas_call(
        body,
        out_shape=out_shape,
        in_specs=in_specs,
        out_specs=out_specs,
        scratch_shapes=scratch,
        compiler_params=pltpu.CompilerParams(vmem_limit_bytes=LIMIT),
        cost_estimate=pl.CostEstimate(flops=flops, bytes_accessed=2 << 20, transcendentals=0),
        name=name,
    )


def on_device(diag_blocks, face_blocks, split):
    diag = diag_blocks.reshape(8, B, B)
    face = face_blocks.reshape(6, 8, B, B)
    split = split.reshape(8)
    sds = jax.ShapeDtypeStruct
    facts = call(
        facts_kernel, sds((16, B), F32), [SMEM, VMEM], VMEM,
        [pltpu.VMEM((8, B), F32)], 1 << 20, "facts",
    )(split, diag)
    halo = (
        swap(facts, "gx", 0), swap(facts, "gx", 1),
        swap(facts, "gy", 0), swap(facts, "gy", 1), swap(facts, "gz", 0),
    )
    inv, fnorm = call(
        inverse_kernel, (sds((3, 4, B, B), BF16), sds((6, 8, B), F32)),
        [SMEM, VMEM, VMEM], (VMEM, VMEM),
        [pltpu.VMEM((8, B), F32), pltpu.VMEM((2, B, B), F32)], 1 << 30, "inverse",
    )(split, diag, face)
    blocks = lambda *lead: sds(lead + (B, B), BF16)
    interp, near, code, xa, xb, ya, yb, z = call(
        interp_kernel,
        (
            blocks(6, 8), blocks(3, 4), sds((1,), jnp.int32),
            blocks(2, 4), blocks(2, 4), blocks(2, 1), blocks(2, 1), blocks(2, 4),
        ),
        [SMEM] + [VMEM] * 10,
        (VMEM, VMEM, SMEM) + (VMEM,) * 5,
        [pltpu.VMEM((6, 8, B), F32)], 1 << 30, "interp",
    )(split, diag, face, inv, fnorm, facts, *halo)
    xa, xb = swap(xa, "gx", 0), swap(xb, "gx", 1)
    ya, yb = swap(ya, "gy", 0), swap(yb, "gy", 1)
    z = swap(z, "gz", 0)
    coarse = call(
        coarse_kernel, sds((8, B, B), F32), [SMEM, SMEM] + [VMEM] * 9, VMEM, [], 1 << 30, "coarse",
    )(split, code, diag, face, interp, near, xa, xb, ya, yb, z)
    return interp.reshape(face_blocks.shape), coarse.reshape(diag_blocks.shape)


def solution(mesh):
    in_specs = (
        P("gx", "gy", "gz", None, None),
        P(None, "gx", "gy", "gz", None, None),
        P("gx", "gy", "gz"),
    )
    out_specs = (P(None, "gx", "gy", "gz", None, None), P("gx", "gy", "gz", None, None))
    return jax.shard_map(
        on_device, mesh=mesh, in_specs=in_specs, out_specs=out_specs, check_vma=False
    )
```

time: 297 us -> 49 us (0.16)
  other arithmetic: 181 us -> 0 us
  matrix products: 32.7 us -> 0 us
  local copies, waits for them, and re-layouts: 28 us -> 4.61 us
  Pallas kernels: 0 us -> 17.7 us
  starting transfers between devices: 33.1 us -> 17.4 us
  waiting for transfers between devices: 17.5 us -> 8.19 us
    another operation x11 -> x0, other arithmetic: 176 us -> none  [the longest x4 94.7 us: on_device(): factor = jnp.linalg.cholesky(dense.reshape(number, order, order))]
    another operation x12 -> x0, matrix products: 23.5 us -> none  [the longest x6 13.2 us: cho_apply(): lax.linalg.triangular_solve(factor, right_side, left_side=True, lower=True)]
    pallas_call x0 -> x4, Pallas kernels: none -> 17.7 us  [the longest x1 11.3 us: on_device(): call(interp_kernel, (blocks(6, 8), blocks(3, 4), sds((1,), jnp.int32), bl...]
    another operation x15 -> x0, local copies, waits for them, and re-layouts: 16 us -> none  [the longest x8 8.04 us: on_device(): interp_all = jnp.stack(interps).reshape((6,) + grid + (order, order))]
    ppermute x12 -> x10, starting transfers between devices: 33.1 us -> 17.4 us  [swap(): return lax.ppermute(x, axis, matching(lax.axis_size(axis), start))]
    ppermute x12 -> x10, waiting for transfers between devices: 17.5 us -> 8.19 us  [swap(): return lax.ppermute(x, axis, matching(lax.axis_size(axis), start))]
    dot_general x18 -> x0, matrix products: 9.22 us -> none  [the longest x6 4.82 us: on_device(): jnp.einsum('mba,mbc->mac', interp.astype(jnp.float32), mixed, precision=l...]
    unnamed x72 -> x7, local copies, waits for them, and re-layouts: 9.67 us -> 4.53 us
  transfers between devices with their start and end apart: 12 -> 10, of which waited for: 3 -> 2; matrix products, arithmetic and copies ran while one was open for 67% -> 0% of each run, Pallas kernels for 0% -> 6%
where the time goes in v1:
time: 49 us; the launch traced here: 48.7 us
  Pallas kernels  17.7 us (36%)
  starting transfers between devices  17.4 us (36%)
  waiting for transfers between devices  8.19 us (17%)
  local copies, waits for them, and re-layouts  4.61 us (9%)
  between operations  0.74 us (2%)
    ppermute x10, starting transfers between devices, swap(): return lax.ppermute(x, axis, matching(lax.axis_size(axis), start))  17.4 us
    pallas_call x1, Pallas kernels, on_device(): call(interp_kernel, (blocks(6, 8), blocks(3, 4), sds((1,), jnp.int32), bl...  11.3 us
    ppermute x10, waiting for transfers between devices, swap(): return lax.ppermute(x, axis, matching(lax.axis_size(axis), start))  8.19 us
    unnamed x7, local copies, waits for them, and re-layouts  4.53 us
    pallas_call x1, Pallas kernels, on_device(): call(inverse_kernel, (sds((3, 4, B, B), BF16), sds((6, 8, B), F32)), [SME...  2.99 us
    pallas_call x1, Pallas kernels, on_device(): call(coarse_kernel, sds((8, B, B), F32), [SMEM, SMEM] + [VMEM] * 9, VMEM,...  2.7 us
  transfers between devices with their start and end apart: 10, of which 2 were waited for; matrix products, arithmetic and copies ran while one was open for 0% of the time, Pallas kernels for 6%

profile of v1, /device:TPU:24, one launch (start us, length us, event | category | flops | bytes accessed | tf_op | source)
XLA Modules:
  0.0 48.7 jit_solution(1734585739513509344)
XLA Ops:
  0.6 0.8 %copy.7 = s32[1,4,2]{2,1,0:T(4,128)S(1)} copy(s32[1,4,2]{1,2,0:T(2,128)} %param.5) | data formatting | bytes 64 | tf_op args[2]
  1.4 0.1 reshape.19.split_ref
  1.5 0.0 copy-start.2
  1.5 0.9 %copy-done.2 = bf16[1,4,2,128,128]{4,3,2,1,0:T(8,128)(2,1)S(1)} copy-done((bf16[1,4,2,128,128]{4,3,2,1,0:T(8,128)(2,1)S(1)}, bf16[1,4,2,128,128]{4,3,2,1,0:T(8,128)(2,1)}, u32[]{:S(2)}) %copy-start.2) | copy-done | bytes 262168
  2.4 0.7 %facts.1.facts_ref = f32[16,128]{1,0:T(8,128)S(1)} custom-call(s32[8]{0:T(128)S(1)} %reshape.19.split_ref, bf16[8,128,128]{2,1,0:T(8,128)(2,1)S(1)} %bitcast.10), custom_call_target="tpu_custom_call" | custom-call | flops 1048576 | bytes 2097152 | tf_op jit(solution)/shard_map/facts/pallas_call | solution.py:315
  3.1 0.0 collective-permute-start.4
  3.1 0.7 %collective-permute-start.3 = (f32[16,128]{1,0:T(8,128)S(1)}, f32[16,128]{1,0:T(8,128)S(1)}, u32[]{:S(2)}, u32[]{:S(2)}) collective-permute-start(f32[16,128]{1,0:T(8,128)S(1)} %facts.1.facts_ref), channel_id=1, source_target_pairs={{2,4},{6,8},{10,12},{4,2},{8,6},{12,10},{3,5},{7,9},{11,13},{5,3},... | collective-permute-start | bytes 24584 | tf_op jit(solution)/shard_map/ppermute | solution.py:294
  3.8 4.3 %collective-permute-start.2 = (f32[16,128]{1,0:T(8,128)S(1)}, f32[16,128]{1,0:T(8,128)S(1)}, u32[]{:S(2)}, u32[]{:S(2)}) collective-permute-start(f32[16,128]{1,0:T(8,128)S(1)} %facts.1.facts_ref), channel_id=1, source_target_pairs={{0,2},{4,6},{8,10},{12,14},{2,0},{6,4},{10,8},{14,12},{1,3},{5,7},... | collective-permute-start | bytes 24584 | tf_op jit(solution)/shard_map/ppermute | solution.py:294
  8.1 5.4 %collective-permute-start.1 = (f32[16,128]{1,0:T(8,128)S(1)}, f32[16,128]{1,0:T(8,128)S(1)}, u32[]{:S(2)}, u32[]{:S(2)}) collective-permute-start(f32[16,128]{1,0:T(8,128)S(1)} %facts.1.facts_ref), channel_id=1, source_target_pairs={{16,32},{48,64},{80,96},{32,16},{64,48},{96,80},{17,33},{49,65},{8... | collective-permute-start | bytes 24584 | tf_op jit(solution)/shard_map/ppermute | solution.py:294
  13.5 0.1 collective-permute-start
  13.6 0.0 copy-start
  13.6 1.4 %copy-done = bf16[6,1,4,2,128,128]{5,4,3,2,1,0:T(8,128)(2,1)S(1)} copy-done((bf16[6,1,4,2,128,128]{5,4,3,2,1,0:T(8,128)(2,1)S(1)}, bf16[6,1,4,2,128,128]{5,4,3,2,1,0:T(8,128)(2,1)}, u32[]{:S(2)}) %copy-start) | copy-done | bytes 1572888
  15.0 3.0 %inverse.1 = (bf16[3,4,128,128]{3,2,1,0:T(8,128)(2,1)S(1)}, f32[6,8,128]{2,1,0:T(8,128)S(1)}) custom-call(s32[8]{0:T(128)S(1)} %reshape.19.split_ref, bf16[8,128,128]{2,1,0:T(8,128)(2,1)S(1)} %bitcast.11, bf16[6,8,128,128]{3,2,1,0:T(8,128)(2,1)S(1)} %bitcast.6), custom_call_target="tpu_custom_call" | custom-call | flops 1073741824 | bytes 2097152 | tf_op jit(solution)/shard_map/inverse/pallas_call | solution.py:323
  18.0 0.0 collective-permute-done.4.hz
  18.0 0.0 collective-permute-done.3.hd
  18.0 0.0 collective-permute-done.2.hc
  18.1 0.0 collective-permute-done.1.hb
  18.1 0.0 collective-permute-done.ha
  18.1 11.3 %interp.1 = (bf16[6,8,128,128]{3,2,1,0:T(8,128)(2,1)}, bf16[3,4,128,128]{3,2,1,0:T(8,128)(2,1)S(1)}, s32[1]{0:T(128)}, bf16[2,4,128,128]{3,2,1,0:T(8,128)(2,1)S(...) custom-call(s32[8]{0:T(128)S(1)} %reshape.19.split_ref, ...), custom_call_target="tpu_custom_call" | custom-call | flops 1073741824 | bytes 2097152 | tf_op jit(solution)/shard_map/interp/pallas_call | solution.py:329
  29.4 2.1 %collective-permute-start.5 = (bf16[2,4,128,128]{3,2,1,0:T(8,128)(2,1)S(1)}, bf16[2,4,128,128]{3,2,1,0:T(8,128)(2,1)S(1)}, u32[]{:S(2)}, u32[]{:S(2)}) collective-permute-start(bf16[2,4,128,128]{3,2,1,0:T(8,128)(2,1)S(1)} %get-tuple-element.17), channel_id=1, source_target_pairs={{0,16},{32,48},{64,80},{96,112},{16,0},{48,32},{80,64},{112,96},{1... | collective-permute-start | bytes 786440 | tf_op jit(solution)/shard_map/ppermute | solution.py:294
  31.5 4.0 %collective-permute-start.6 = (bf16[2,4,128,128]{3,2,1,0:T(8,128)(2,1)S(1)}, bf16[2,4,128,128]{3,2,1,0:T(8,128)(2,1)S(1)}, u32[]{:S(2)}, u32[]{:S(2)}) collective-permute-start(bf16[2,4,128,128]{3,2,1,0:T(8,128)(2,1)S(1)} %get-tuple-element.18), channel_id=1, source_target_pairs={{16,32},{48,64},{80,96},{32,16},{64,48},{96,80},{17,33},{49,65},{8... | collective-permute-start | bytes 786440 | tf_op jit(solution)/shard_map/ppermute | solution.py:294
  35.5 0.1 collective-permute-start.9
  35.6 0.1 collective-permute-start.7
  35.7 0.7 %collective-permute-start.8 = (bf16[2,1,128,128]{3,2,1,0:T(8,128)(2,1)S(1)}, bf16[2,1,128,128]{3,2,1,0:T(8,128)(2,1)S(1)}, u32[]{:S(2)}, u32[]{:S(2)}) collective-permute-start(bf16[2,1,128,128]{3,2,1,0:T(8,128)(2,1)S(1)} %get-tuple-element.20), channel_id=1, source_target_pairs={{2,4},{6,8},{10,12},{4,2},{8,6},{12,10},{3,5},{7,9},{11,13},{5,3},... | collective-permute-start | bytes 196616 | tf_op jit(solution)/shard_map/ppermute | solution.py:294
  36.4 3.7 %collective-permute-done.7.ya_ref = bf16[2,1,128,128]{3,2,1,0:T(8,128)(2,1)S(1)} collective-permute-done((bf16[2,1,128,128]{3,2,1,0:T(8,128)(2,1)S(1)}, bf16[2,1,128,128]{3,2,1,0:T(8,128)(2,1)S(1)}, u32[]{:S(2)}, u32[]{:S(2)}) %collective-permute-start.7) | collective-permute-done | bytes 65568 | tf_op jit(solution)/shard_map/ppermute | solution.py:294
  40.1 0.0 collective-permute-done.8.yb_ref
  40.1 0.0 collective-permute-done.5.xa_ref
  40.1 4.4 %collective-permute-done.6.xb_ref = bf16[2,4,128,128]{3,2,1,0:T(8,128)(2,1)S(1)} collective-permute-done((bf16[2,4,128,128]{3,2,1,0:T(8,128)(2,1)S(1)}, bf16[2,4,128,128]{3,2,1,0:T(8,128)(2,1)S(1)}, u32[]{:S(2)}, u32[]{:S(2)}) %collective-permute-start.6) | collective-permute-done | bytes 262176 | tf_op jit(solution)/shard_map/ppermute | solution.py:294
  44.5 0.0 collective-permute-done.9.z_ref
  44.5 0.0 copy-start.1
  44.6 1.4 %copy-done.1 = bf16[6,8,128,128]{3,2,1,0:T(8,128)(2,1)S(1)} copy-done((bf16[6,8,128,128]{3,2,1,0:T(8,128)(2,1)S(1)}, bf16[6,8,128,128]{3,2,1,0:T(8,128)(2,1)}, u32[]{:S(2)}) %copy-start.1) | copy-done | bytes 1572888
  46.0 2.7 %coarse.1 = f32[8,128,128]{2,1,0:T(8,128)} custom-call(s32[8]{0:T(128)S(1)} %reshape.19.split_ref, s32[1]{0:T(128)} %get-tuple-element.15.code_ref, bf16[8,128,128]{2,1,0:T(8,128)(2,1)S(1)} %bitcast.13, bf16[6,8,128,128]{3,2,1,0:T(8,128)(2,1)S(1)} %bitcast.8, bf16[6,8,128,128]{3,2,1,0:T(8,128)(2,1)S(1)} %copy-done.1, ...), custom_call_target="tpu_custom_call" | custom-call | flops 1073741824 | bytes 2097152 | tf_op jit(solution)/shard_map/coarse/pallas_call | solution.py:342
Async XLA Ops:
  1.5 1.0 %copy-start.2 = (bf16[1,4,2,128,128]{4,3,2,1,0:T(8,128)(2,1)S(1)}, bf16[1,4,2,128,128]{4,3,2,1,0:T(8,128)(2,1)}, u32[]{:S(2)}) copy-start(bf16[1,4,2,128,128]{4,3,2,1,0:T(8,128)(2,1)} %param.3) | copy-start | bytes 786436
  3.1 14.9 %collective-permute-start.4 = (f32[16,128]{1,0:T(8,128)S(1)}, f32[16,128]{1,0:T(8,128)S(1)}, u32[]{:S(2)}, u32[]{:S(2)}) collective-permute-start(f32[16,128]{1,0:T(8,128)S(1)} %facts.1.facts_ref), channel_id=1, source_target_pairs={{0,1},{1,0},{2,3},{3,2},{4,5},{5,4},{6,7},{7,6},{8,9},{9,8},{10,11... | collective-permute-start | bytes 24584 | tf_op jit(solution)/shard_map/ppermute | solution.py:294
  3.1 14.9 %collective-permute-start.3 = (f32[16,128]{1,0:T(8,128)S(1)}, f32[16,128]{1,0:T(8,128)S(1)}, u32[]{:S(2)}, u32[]{:S(2)}) collective-permute-start(f32[16,128]{1,0:T(8,128)S(1)} %facts.1.facts_ref), channel_id=1, source_target_pairs={{2,4},{6,8},{10,12},{4,2},{8,6},{12,10},{3,5},{7,9},{11,13},{5,3},... | collective-permute-start | bytes 24584 | tf_op jit(solution)/shard_map/ppermute | solution.py:294
  3.8 14.2 %collective-permute-start.2 = (f32[16,128]{1,0:T(8,128)S(1)}, f32[16,128]{1,0:T(8,128)S(1)}, u32[]{:S(2)}, u32[]{:S(2)}) collective-permute-start(f32[16,128]{1,0:T(8,128)S(1)} %facts.1.facts_ref), channel_id=1, source_target_pairs={{0,2},{4,6},{8,10},{12,14},{2,0},{6,4},{10,8},{14,12},{1,3},{5,7},... | collective-permute-start | bytes 24584 | tf_op jit(solution)/shard_map/ppermute | solution.py:294
  8.1 10.0 %collective-permute-start.1 = (f32[16,128]{1,0:T(8,128)S(1)}, f32[16,128]{1,0:T(8,128)S(1)}, u32[]{:S(2)}, u32[]{:S(2)}) collective-permute-start(f32[16,128]{1,0:T(8,128)S(1)} %facts.1.facts_ref), channel_id=1, source_target_pairs={{16,32},{48,64},{80,96},{32,16},{64,48},{96,80},{17,33},{49,65},{8... | collective-permute-start | bytes 24584 | tf_op jit(solution)/shard_map/ppermute | solution.py:294
  13.5 4.5 %collective-permute-start = (f32[16,128]{1,0:T(8,128)S(1)}, f32[16,128]{1,0:T(8,128)S(1)}, u32[]{:S(2)}, u32[]{:S(2)}) collective-permute-start(f32[16,128]{1,0:T(8,128)S(1)} %facts.1.facts_ref), channel_id=1, source_target_pairs={{0,16},{32,48},{64,80},{96,112},{16,0},{48,32},{80,64},{112,96},{1... | collective-permute-start | bytes 24584 | tf_op jit(solution)/shard_map/ppermute | solution.py:294
  13.6 1.4 %copy-start = (bf16[6,1,4,2,128,128]{5,4,3,2,1,0:T(8,128)(2,1)S(1)}, bf16[6,1,4,2,128,128]{5,4,3,2,1,0:T(8,128)(2,1)}, u32[]{:S(2)}) copy-start(bf16[6,1,4,2,128,128]{5,4,3,2,1,0:T(8,128)(2,1)} %param.4) | copy-start | bytes 4718596
  29.4 10.7 %collective-permute-start.5 = (bf16[2,4,128,128]{3,2,1,0:T(8,128)(2,1)S(1)}, bf16[2,4,128,128]{3,2,1,0:T(8,128)(2,1)S(1)}, u32[]{:S(2)}, u32[]{:S(2)}) collective-permute-start(bf16[2,4,128,128]{3,2,1,0:T(8,128)(2,1)S(1)} %get-tuple-element.17), channel_id=1, source_target_pairs={{0,16},{32,48},{64,80},{96,112},{16,0},{48,32},{80,64},{112,96},{1... | collective-permute-start | bytes 786440 | tf_op jit(solution)/shard_map/ppermute | solution.py:294
  31.5 13.0 %collective-permute-start.6 = (bf16[2,4,128,128]{3,2,1,0:T(8,128)(2,1)S(1)}, bf16[2,4,128,128]{3,2,1,0:T(8,128)(2,1)S(1)}, u32[]{:S(2)}, u32[]{:S(2)}) collective-permute-start(bf16[2,4,128,128]{3,2,1,0:T(8,128)(2,1)S(1)} %get-tuple-element.18), channel_id=1, source_target_pairs={{16,32},{48,64},{80,96},{32,16},{64,48},{96,80},{17,33},{49,65},{8... | collective-permute-start | bytes 786440 | tf_op jit(solution)/shard_map/ppermute | solution.py:294
  35.5 9.0 %collective-permute-start.9 = (bf16[2,4,128,128]{3,2,1,0:T(8,128)(2,1)S(1)}, bf16[2,4,128,128]{3,2,1,0:T(8,128)(2,1)S(1)}, u32[]{:S(2)}, u32[]{:S(2)}) collective-permute-start(bf16[2,4,128,128]{3,2,1,0:T(8,128)(2,1)S(1)} %get-tuple-element.21), channel_id=1, source_target_pairs={{0,1},{1,0},{2,3},{3,2},{4,5},{5,4},{6,7},{7,6},{8,9},{9,8},{10,11... | collective-permute-start | bytes 786440 | tf_op jit(solution)/shard_map/ppermute | solution.py:294
  35.6 4.5 %collective-permute-start.7 = (bf16[2,1,128,128]{3,2,1,0:T(8,128)(2,1)S(1)}, bf16[2,1,128,128]{3,2,1,0:T(8,128)(2,1)S(1)}, u32[]{:S(2)}, u32[]{:S(2)}) collective-permute-start(bf16[2,1,128,128]{3,2,1,0:T(8,128)(2,1)S(1)} %get-tuple-element.19), channel_id=1, source_target_pairs={{0,2},{4,6},{8,10},{12,14},{2,0},{6,4},{10,8},{14,12},{1,3},{5,7},... | collective-permute-start | bytes 196616 | tf_op jit(solution)/shard_map/ppermute | solution.py:294
  35.7 4.4 %collective-permute-start.8 = (bf16[2,1,128,128]{3,2,1,0:T(8,128)(2,1)S(1)}, bf16[2,1,128,128]{3,2,1,0:T(8,128)(2,1)S(1)}, u32[]{:S(2)}, u32[]{:S(2)}) collective-permute-start(bf16[2,1,128,128]{3,2,1,0:T(8,128)(2,1)S(1)} %get-tuple-element.20), channel_id=1, source_target_pairs={{2,4},{6,8},{10,12},{4,2},{8,6},{12,10},{3,5},{7,9},{11,13},{5,3},... | collective-permute-start | bytes 196616 | tf_op jit(solution)/shard_map/ppermute | solution.py:294
  44.5 1.4 %copy-start.1 = (bf16[6,8,128,128]{3,2,1,0:T(8,128)(2,1)S(1)}, bf16[6,8,128,128]{3,2,1,0:T(8,128)(2,1)}, u32[]{:S(2)}) copy-start(bf16[6,8,128,128]{3,2,1,0:T(8,128)(2,1)} %get-tuple-element.14.interp_ref) | copy-start | bytes 4718596

commit v2 on v1

v2 whole, which is shorter than its diff:
```python
import jax
import jax.numpy as jnp
from jax import lax
from jax.experimental import pallas as pl
from jax.experimental.pallas import tpu as pltpu
from jax.sharding import PartitionSpec as P

B = 128
F32 = jnp.float32
BF16 = jnp.bfloat16
VMEM = pl.BlockSpec(memory_space=pltpu.VMEM)
SMEM = pl.BlockSpec(memory_space=pltpu.SMEM)
HBM = pl.BlockSpec(memory_space=pltpu.HBM)
LIMIT = 24 * 1024 * 1024


def mm(a, b):
    return jnp.dot(a, b, preferred_element_type=F32)


def mm32(a, b):
    return jnp.dot(a, b, preferred_element_type=F32, precision=lax.Precision.HIGHEST)


def halves(x):
    hi = x.astype(BF16)
    return hi, (x - hi.astype(F32)).astype(BF16)


def thirds(x):
    hi = x.astype(BF16)
    rest = x - hi.astype(F32)
    mid = rest.astype(BF16)
    return hi, mid, (rest - mid.astype(F32)).astype(BF16)


def wide(x):
    return jnp.concatenate([x, x], axis=0)


def split_at(split_ref, c, z):
    return split_ref[0, z, c]


def fine_of(split_ref, c):
    return jnp.where(split_at(split_ref, c, 0) == 0, 0, 1)


def square_sums(x):
    x = x.astype(F32)
    return jnp.sum(x * x, axis=0, keepdims=True)


def norms_of(rows):
    return jnp.broadcast_to(jnp.sqrt(jnp.sum(rows, axis=1, keepdims=True)), rows.shape)


def facts_kernel(split_ref, diag_ref, facts_ref, rows):
    for e in range(8):
        rows[pl.ds(e, 1), :] = square_sums(diag_ref[e])
        part = split_at(split_ref, e // 2, e % 2).astype(F32)
        facts_ref[pl.ds(8 + e, 1), :] = jnp.full((1, B), part, F32)
    facts_ref[pl.ds(0, 8), :] = norms_of(rows[...])


def scaling(a, eye):
    picked = jnp.where(eye, a, 0.0)
    down = lax.rsqrt(jnp.sum(picked, axis=1, keepdims=True))
    along = lax.rsqrt(jnp.sum(picked, axis=0, keepdims=True))
    a = a * down * along
    bound = jnp.max(jnp.sum(jnp.abs(a), axis=0, keepdims=True), axis=1, keepdims=True)
    return a, down, along, 1.9 / bound


def inverse_kernel(split_ref, diag_ref, face_ref, inv_ref, fnorm_ref, fine_ref, rows, work, sems):
    cols = range(4)
    copies = []
    for c in cols:
        e = 2 * c + fine_of(split_ref, c)
        for d in range(6):
            copies.append(
                pltpu.make_async_copy(face_ref.at[d, e], fine_ref.at[d, c], sems.at[6 * c + d])
            )
            copies[-1].start()
    eye = (
        lax.broadcasted_iota(jnp.int32, (B, B), 0) == lax.broadcasted_iota(jnp.int32, (B, B), 1)
    )
    one = jnp.where(eye, 1.0, 0.0).astype(F32)
    mats = [diag_ref[2 * c + fine_of(split_ref, c)] for c in cols]
    parts = [scaling(m.astype(F32), eye) for m in mats]
    powers = [one - start * a for a, _, _, start in parts]
    sums = [one + p for p in powers]
    powers = [p.astype(BF16) for p in powers]
    for _ in range(4):
        powers = [mm(p, p).astype(BF16) for p in powers]
        sums = [s + mm(s.astype(BF16), p) for s, p in zip(sums, powers)]
    guess = [
        (s * (start * down) * along).astype(BF16) for s, (_, down, along, start) in zip(sums, parts)
    ]
    left = [one - mm(mats[c], guess[c]) for c in cols]
    small = [r.astype(BF16) for r in left]
    left = [r + mm(b, b) for r, b in zip(left, small)]
    better = []
    for c in cols:
        hi, lo = halves(left[c])
        better.append(guess[c].astype(F32) + (mm(guess[c], hi) + mm(guess[c], lo)))
    pairs = [halves(x) for x in better]
    left = [one - (mm(mats[c], pairs[c][0]) + mm(mats[c], pairs[c][1])) for c in cols]
    worst = jnp.zeros((1, B), F32)
    for c in cols:
        hi, lo = pairs[c]
        rhi, rlo = halves(left[c])
        fixed = (hi.astype(F32) + lo.astype(F32)) + (mm(hi, rhi) + (mm(hi, rlo) + mm(lo, rhi)))
        inv_ref[0, c], inv_ref[1, c], inv_ref[2, c] = thirds(fixed)
        worst = worst + jnp.sum(jnp.abs(left[c]), axis=0, keepdims=True)
    for c in cols:
        for d in range(6):
            copies[6 * c + d].wait()
    for d in range(6):
        for c in cols:
            sums = square_sums(fine_ref[d, c])
            rows[pl.ds(8 * d + 2 * c, 1), :] = sums
            rows[pl.ds(8 * d + 2 * c + 1, 1), :] = sums
    fnorm_ref[...] = norms_of(rows[...])
    reached = jnp.max(worst) <= 1e-3

    @pl.when(jnp.logical_not(reached))
    def _():
        for c in cols:
            a, down, along, start = scaling(mats[c].astype(F32), eye)
            work[0] = a
            work[1] = one * start

            @pl.loop(0, 48)
            def _(_):
                x = work[1]
                work[1] = x + mm32(x, one - mm32(work[0], x))

            inv_ref[0, c], inv_ref[1, c], inv_ref[2, c] = thirds(work[1] * down * along)


def shifted(own, beyond, step, edge):
    return jnp.where(edge, pltpu.roll(beyond, step, 0), pltpu.roll(own, step, 0))


def weights_of(facts_ref, halo_refs, fnorm_ref, weight_ref):
    gx, gy, gz = lax.axis_index("gx"), lax.axis_index("gy"), lax.axis_index("gz")
    ha, hb, hc, hd, hz = halo_refs
    row = lax.broadcasted_iota(jnp.int32, (8, B), 0)
    depth = row % 2
    even_x, even_y = gx % 2 == 0, gy % 2 == 0

    def pick(test, first, second, part):
        rows = pl.ds(8 * part, 8)
        return jnp.where(test, first[rows, :], second[rows, :])

    def neighbours(part):
        own = facts_ref[pl.ds(8 * part, 8), :]
        z = hz[pl.ds(8 * part, 8), :]
        return (
            pick(even_x, hb, ha, part),
            pick(even_x, ha, hb, part),
            shifted(own, pick(even_y, hd, hc, part), 2, row < 2),
            shifted(own, pick(even_y, hc, hd, part), 6, row >= 6),
            jnp.where(depth == 0, pltpu.roll(z, 7, 0), pltpu.roll(own, 1, 0)),
            jnp.where(depth == 1, pltpu.roll(z, 1, 0), pltpu.roll(own, 7, 0)),
        )

    present = (
        jnp.broadcast_to(gx > 0, (8, B)),
        jnp.broadcast_to(gx < lax.axis_size("gx") - 1, (8, B)),
        (row >= 2) | (gy > 0),
        (row < 6) | (gy < lax.axis_size("gy") - 1),
        (depth == 1) | (gz > 0),
        (depth == 0) | (gz < lax.axis_size("gz") - 1),
    )
    own_norm = facts_ref[pl.ds(0, 8), :]
    fine = facts_ref[pl.ds(8, 8), :] < 0.5
    norms, splits = neighbours(0), neighbours(1)
    total = jnp.zeros((8, B), F32)
    denom = jnp.zeros((8, B), F32)
    links = []
    for d in range(6):
        other = jnp.where(present[d], norms[d], 1.0)
        strength = jnp.where(present[d], fnorm_ref[pl.ds(8 * d, 8), :] / jnp.sqrt(own_norm * other), 0.0)
        linked = present[d] & (splits[d] > 0.5)
        total = total + strength
        denom = denom + jnp.where(linked, strength, 0.0)
        links.append(linked)
    ratio = total / jnp.where(fine, denom, 1.0)
    for d in range(6):
        weight_ref[d] = jnp.where(links[d] & fine, -ratio, 0.0)


def interp_kernel(
    split_ref, diag_ref, fine_ref, inv_ref, fnorm_ref, facts_ref, ha, hb, hc, hd, hz,
    interp_ref, code_ref, xa_ref, xb_ref, ya_ref, yb_ref, z_ref, near_ref, inside_ref,
    weight_ref, mixed_ref, zero_ref, sems,
):
    zero_ref[...] = jnp.zeros((B, B), BF16)
    gx, gy = lax.axis_index("gx"), lax.axis_index("gy")
    fines = [fine_of(split_ref, c) for c in range(4)]
    weights_of(facts_ref, (ha, hb, hc, hd, hz), fnorm_ref, weight_ref)
    copies = []

    def send(block, d, e):
        copies.append(pltpu.make_async_copy(block, interp_ref.at[d, e], sems.at[len(copies)]))
        copies[-1].start()

    def slots(c):
        return (
            (1 - gx % 2, xa_ref.at[0, c], xa_ref.at[1, c]),
            (gx % 2, xb_ref.at[0, c], xb_ref.at[1, c]),
            (2, near_ref.at[0, 0, c], near_ref.at[0, 1, c]),
            (3, near_ref.at[1, 0, c], near_ref.at[1, 1, c]),
            (5 - fines[c], inside_ref.at[0, c], inside_ref.at[1, c]),
            (4 + fines[c], z_ref.at[0, c], z_ref.at[1, c]),
        )

    def send_column(c):
        for d, interp, _ in slots(c):
            send(interp, d, 2 * c + fines[c])

    for c in range(4):
        e = 2 * c + fines[c]
        inv = jnp.concatenate([inv_ref[0, c], inv_ref[1, c]], axis=1)
        last = inv_ref[2, c]
        here = slots(c)
        for s in (0, 2, 4):
            two = [here[s], here[s + 1]]
            face = jnp.concatenate([fine_ref[d, c] for d, _, _ in two], axis=1)
            weight = jnp.concatenate([weight_ref[d, pl.ds(e, 1), :] for d, _, _ in two], axis=1)
            interp = (weight * (mm(inv, wide(face)) + mm(last, face))).astype(BF16)
            two[0][1][...] = interp[:, :B]
            two[1][1][...] = interp[:, B:]
        for d in range(6):
            send(zero_ref, d, 2 * c + 1 - fines[c])
        if c > 0:
            send_column(c - 1)
    row = lax.broadcasted_iota(jnp.int32, (8, B), 0)
    lane = lax.broadcasted_iota(jnp.int32, (8, B), 1)
    bit = jnp.where((row % 2 == 0) & (lane == 0), 1, 0) * lax.shift_left(1, row // 2)
    code = jnp.zeros((8, B), F32)
    for place, ref in enumerate((ha, hb, hc, hd)):
        code = code + ref[pl.ds(8, 8), :] * (bit * (1 << (4 * place))).astype(F32)
    code_ref[0] = jnp.sum(code).astype(jnp.int32)
    for c in range(4):
        a = diag_ref[2 * c + fines[c]]
        here = slots(c)
        for s in (0, 2, 4):
            two = [here[s], here[s + 1]]
            face = jnp.concatenate([fine_ref[d, c] for d, _, _ in two], axis=1)
            interp = jnp.concatenate([block[...] for _, block, _ in two], axis=1)
            hi, lo = halves(mm(a, interp) + face.astype(F32))
            for t in range(2):
                lanes = slice(B * t, B * t + B)
                mixed_ref[c, s + t, pl.ds(0, B), :] = hi[:, lanes]
                mixed_ref[c, s + t, pl.ds(B, B), :] = lo[:, lanes]
        if c == 1:
            send_column(3)
    for c in range(4):
        for s, (_, interp, contrib) in enumerate(slots(c)):
            turned = jnp.transpose(interp[...])
            both = jnp.concatenate([turned, turned], axis=1)
            contrib[...] = mm(both, mixed_ref[c, s]).astype(BF16)
    up = gy % 2 == 0
    for k in range(2):
        low, high = near_ref[0, k, 0], near_ref[1, k, 3]
        ya_ref[k, 0] = jnp.where(up, high, low)
        yb_ref[k, 0] = jnp.where(up, low, high)
    for copy in copies:
        copy.wait()


def near_kernel(
    split_ref, code_ref, diag_ref, face_ref, near_ref, inside_ref,
    sum_ref, far_ref, held_ref, sems,
):
    gx, gy, gz = lax.axis_index("gx"), lax.axis_index("gy"), lax.axis_index("gz")
    fines = [fine_of(split_ref, c) for c in range(4)]
    local = []
    for c in range(4):
        if c > 0:
            local.append((2 * c + fines[c - 1], 2, near_ref.at[1, 0, c - 1], near_ref.at[1, 1, c - 1]))
        if c < 3:
            local.append((2 * c + fines[c + 1], 3, near_ref.at[0, 0, c + 1], near_ref.at[0, 1, c + 1]))
        local.append((2 * c + 1 - fines[c], 4 + fines[c], inside_ref.at[0, c], inside_ref.at[1, c]))
    copies = []

    def fetch(target, d, into):
        copies.append(pltpu.make_async_copy(face_ref.at[d, target], into, sems.at[len(copies)]))
        copies[-1].start()

    for k, (target, d, _, _) in enumerate(local):
        fetch(target, d, held_ref.at[k])
    for k, (target, d) in enumerate(far_targets(code_ref[0], gx, gy, gz)):
        fetch(target, d, far_ref.at[k])
    for e in range(8):
        sum_ref[e] = diag_ref[e].astype(F32)
    for copy in copies:
        copy.wait()
    for k, (target, _, interp, contrib) in enumerate(local):
        sum_ref[target] = sum_ref[target] + (contrib[...].astype(F32) + mm(held_ref[k], interp[...]))


def far_targets(code, gx, gy, gz):
    def bit_at(place):
        return lax.shift_right_logical(code, place) & 1

    up = gy % 2 == 0
    found = [(2 * c + bit_at(c), 1 - gx % 2) for c in range(4)]
    found += [(2 * c + bit_at(4 + c), gx % 2) for c in range(4)]
    code_a = jnp.where(up, bit_at(8), bit_at(11))
    code_b = jnp.where(up, bit_at(15), bit_at(12))
    found.append((jnp.where(up, 6, 0) + code_a, jnp.where(up, 3, 2)))
    found.append((jnp.where(up, 0, 6) + code_b, jnp.where(up, 2, 3)))
    return found + [(2 * c + 1 - gz, 5 - gz) for c in range(4)]


def coarse_kernel(
    split_ref, code_ref, sum_ref, far_ref, xa_ref, xb_ref, ya_ref, yb_ref, z_ref, coarse_ref
):
    gx, gy, gz = lax.axis_index("gx"), lax.axis_index("gy"), lax.axis_index("gz")
    arrived = [(ref, c) for ref in (xa_ref, xb_ref) for c in range(4)]
    arrived += [(ya_ref, 0), (yb_ref, 0)] + [(z_ref, c) for c in range(4)]
    for e in range(8):
        coarse_ref[e] = sum_ref[e]
    targets = far_targets(code_ref[0], gx, gy, gz)
    for k, ((target, _), (ref, c)) in enumerate(zip(targets, arrived)):
        coarse_ref[target] = coarse_ref[target] + (
            ref[1, c].astype(F32) + mm(far_ref[k], ref[0, c])
        )
    for e in range(8):
        keep = split_at(split_ref, e // 2, e % 2) == 1
        coarse_ref[e] = jnp.where(keep, coarse_ref[e], 0.0)


def matching(size, start):
    pairs = [(i, i + 1) for i in range(start, size - 1, 2)]
    return pairs + [(b, a) for a, b in pairs]


def swap(x, axis, start):
    return lax.ppermute(x, axis, matching(lax.axis_size(axis), start))


def call(body, out_shape, in_specs, out_specs, scratch, flops, name):
    return pl.pallas_call(
        body,
        out_shape=out_shape,
        in_specs=in_specs,
        out_specs=out_specs,
        scratch_shapes=scratch,
        compiler_params=pltpu.CompilerParams(vmem_limit_bytes=LIMIT),
        cost_estimate=pl.CostEstimate(flops=flops, bytes_accessed=2 << 20, transcendentals=0),
        name=name,
    )


def on_device(diag_blocks, face_blocks, split):
    diag = diag_blocks.reshape(8, B, B)
    face = face_blocks.reshape(6, 8, B, B)
    split = jnp.transpose(split, (0, 2, 1))
    sds = jax.ShapeDtypeStruct
    dma = pltpu.SemaphoreType.DMA
    facts = call(
        facts_kernel, sds((16, B), F32), [SMEM, VMEM], VMEM,
        [pltpu.VMEM((8, B), F32)], 1 << 20, "facts",
    )(split, diag)
    halo = (
        swap(facts, "gx", 0), swap(facts, "gx", 1),
        swap(facts, "gy", 0), swap(facts, "gy", 1), swap(facts, "gz", 0),
    )
    blocks = lambda *lead: sds(lead + (B, B), BF16)
    inv, fnorm, fine = call(
        inverse_kernel, (blocks(3, 4), sds((48, B), F32), blocks(6, 4)),
        [SMEM, VMEM, HBM], (VMEM, VMEM, VMEM),
        [pltpu.VMEM((48, B), F32), pltpu.VMEM((2, B, B), F32), dma((24,))], 1 << 30, "inverse",
    )(split, diag, face)
    interp, code, xa, xb, ya, yb, z, near, inside = call(
        interp_kernel,
        (
            blocks(6, 8), sds((1,), jnp.int32), blocks(2, 4), blocks(2, 4), blocks(2, 1),
            blocks(2, 1), blocks(2, 4), blocks(2, 2, 4), blocks(2, 4),
        ),
        [SMEM] + [VMEM] * 10,
        (HBM, SMEM) + (VMEM,) * 7,
        [
            pltpu.VMEM((6, 8, B), F32), pltpu.VMEM((4, 6, 2 * B, B), BF16),
            pltpu.VMEM((B, B), BF16), dma((48,)),
        ],
        1 << 30, "interp",
    )(split, diag, fine, inv, fnorm, facts, *halo)
    xa, xb = swap(xa, "gx", 0), swap(xb, "gx", 1)
    ya, yb = swap(ya, "gy", 0), swap(yb, "gy", 1)
    z = swap(z, "gz", 0)
    total, far = call(
        near_kernel, (sds((8, B, B), F32), blocks(14)),
        [SMEM, SMEM, VMEM, HBM, VMEM, VMEM], (VMEM, VMEM),
        [pltpu.VMEM((10, B, B), BF16), dma((24,))], 1 << 30, "near",
    )(split, code, diag, face, near, inside)
    coarse = call(
        coarse_kernel, sds((8, B, B), F32), [SMEM, SMEM] + [VMEM] * 7, VMEM, [], 1 << 30, "coarse",
    )(split, code, total, far, xa, xb, ya, yb, z)
    return interp.reshape(face_blocks.shape), coarse.reshape(diag_blocks.shape)


def solution(mesh):
    in_specs = (
        P("gx", "gy", "gz", None, None),
        P(None, "gx", "gy", "gz", None, None),
        P("gx", "gy", "gz"),
    )
    out_specs = (P(None, "gx", "gy", "gz", None, None), P("gx", "gy", "gz", None, None))
    return jax.shard_map(
        on_device, mesh=mesh, in_specs=in_specs, out_specs=out_specs, check_vma=False
    )
```

time: 49 us -> 40.1 us (0.82)
  Pallas kernels: 17.7 us -> 13.3 us
  waiting for transfers between devices: 8.19 us -> 5.28 us
  local copies, waits for them, and re-layouts: 4.61 us -> 3.03 us
    pallas_call x3 -> x4, Pallas kernels: 17 us -> 12.6 us  [the longest x1 4.15 us: on_device(): call(inverse_kernel, (blocks(3, 4), sds((48, B), F32), blocks(6, 4)), [SM...]
    ppermute x10, waiting for transfers between devices: 8.19 us -> 5.28 us  [swap(): return lax.ppermute(x, axis, matching(lax.axis_size(axis), start))]
    unnamed x7 -> x8, local copies, waits for them, and re-layouts: 4.53 us -> 3.03 us
  transfers between devices with their start and end apart: 10 -> 10, of which waited for: 2 -> 2; matrix products, arithmetic and copies ran while one was open for 0% -> 0% of each run, Pallas kernels for 6% -> 18%
where the time goes in v2:
time: 40.1 us; the launch traced here: 39.8 us
  starting transfers between devices  17.4 us (43%)
  Pallas kernels  13.3 us (33%)
  waiting for transfers between devices  5.28 us (13%)
  local copies, waits for them, and re-layouts  3.03 us (8%)
  between operations  0.79 us (2%)
    ppermute x10, starting transfers between devices, swap(): return lax.ppermute(x, axis, matching(lax.axis_size(axis), start))  17.4 us
    ppermute x10, waiting for transfers between devices, swap(): return lax.ppermute(x, axis, matching(lax.axis_size(axis), start))  5.28 us
    pallas_call x1, Pallas kernels, on_device(): call(inverse_kernel, (blocks(3, 4), sds((48, B), F32), blocks(6, 4)), [SM...  4.15 us
    pallas_call x1, Pallas kernels, on_device(): call(interp_kernel, (blocks(6, 8), sds((1,), jnp.int32), blocks(2, 4), bl...  3.09 us
    unnamed x8, local copies, waits for them, and re-layouts  3.03 us
    pallas_call x1, Pallas kernels, on_device(): call(near_kernel, (sds((8, B, B), F32), blocks(14)), [SMEM, SMEM, VMEM, H...  2.9 us
    pallas_call x1, Pallas kernels, on_device(): call(coarse_kernel, sds((8, B, B), F32), [SMEM, SMEM] + [VMEM] * 7, VMEM,...  2.48 us
  transfers between devices with their start and end apart: 10, of which 2 were waited for; matrix products, arithmetic and copies ran while one was open for 0% of the time, Pallas kernels for 18%

profile of v2, /device:TPU:24, one launch (start us, length us, event | category | flops | bytes accessed | tf_op | source)
XLA Modules:
  0.0 39.8 jit_solution(760250165159884595)
XLA Ops:
  0.6 0.0 copy-start
  0.6 0.9 %copy-done = bf16[1,4,2,128,128]{4,3,2,1,0:T(8,128)(2,1)S(1)} copy-done((bf16[1,4,2,128,128]{4,3,2,1,0:T(8,128)(2,1)S(1)}, bf16[1,4,2,128,128]{4,3,2,1,0:T(8,128)(2,1)}, u32[]{:S(2)}) %copy-start) | copy-done | bytes 262168
  1.6 0.0 copy-start.1
  1.6 0.7 %copy-done.1 = s32[1,4,2]{1,2,0:T(2,128)S(1)} copy-done((s32[1,4,2]{1,2,0:T(2,128)S(1)}, s32[1,4,2]{1,2,0:T(2,128)}, u32[]{:S(2)}) %copy-start.1) | copy-done | bytes 56
  2.3 0.7 %facts.1.facts_ref = f32[16,128]{1,0:T(8,128)S(1)} custom-call(s32[1,2,4]{2,1,0:T(2,128)S(1)} %bitcast.11, bf16[8,128,128]{2,1,0:T(8,128)(2,1)S(1)} %bitcast.7), custom_call_target="tpu_custom_call" | custom-call | flops 1048576 | bytes 2097152 | tf_op jit(solution)/shard_map/facts/pallas_call | solution.py:366
  3.0 0.0 collective-permute-start.4
  3.0 0.7 %collective-permute-start.3 = (f32[16,128]{1,0:T(8,128)S(1)}, f32[16,128]{1,0:T(8,128)S(1)}, u32[]{:S(2)}, u32[]{:S(2)}) collective-permute-start(f32[16,128]{1,0:T(8,128)S(1)} %facts.1.facts_ref), channel_id=1, source_target_pairs={{2,4},{6,8},{10,12},{4,2},{8,6},{12,10},{3,5},{7,9},{11,13},{5,3},... | collective-permute-start | bytes 24584 | tf_op jit(solution)/shard_map/ppermute | solution.py:344
  3.6 4.3 %collective-permute-start.2 = (f32[16,128]{1,0:T(8,128)S(1)}, f32[16,128]{1,0:T(8,128)S(1)}, u32[]{:S(2)}, u32[]{:S(2)}) collective-permute-start(f32[16,128]{1,0:T(8,128)S(1)} %facts.1.facts_ref), channel_id=1, source_target_pairs={{0,2},{4,6},{8,10},{12,14},{2,0},{6,4},{10,8},{14,12},{1,3},{5,7},... | collective-permute-start | bytes 24584 | tf_op jit(solution)/shard_map/ppermute | solution.py:344
  7.9 5.4 %collective-permute-start.1 = (f32[16,128]{1,0:T(8,128)S(1)}, f32[16,128]{1,0:T(8,128)S(1)}, u32[]{:S(2)}, u32[]{:S(2)}) collective-permute-start(f32[16,128]{1,0:T(8,128)S(1)} %facts.1.facts_ref), channel_id=1, source_target_pairs={{16,32},{48,64},{80,96},{32,16},{64,48},{96,80},{17,33},{49,65},{8... | collective-permute-start | bytes 24584 | tf_op jit(solution)/shard_map/ppermute | solution.py:344
  13.4 0.1 collective-permute-start
  13.5 0.0 copy-start.2
  13.5 1.4 %copy-done.2 = bf16[6,1,4,2,128,128]{5,4,3,2,1,0:T(8,128)(2,1)S(1)} copy-done((bf16[6,1,4,2,128,128]{5,4,3,2,1,0:T(8,128)(2,1)S(1)}, bf16[6,1,4,2,128,128]{5,4,3,2,1,0:T(8,128)(2,1)}, u32[]{:S(2)}) %copy-start.2) | copy-done | bytes 1572888
  14.9 4.1 %inverse.1 = (bf16[3,4,128,128]{3,2,1,0:T(8,128)(2,1)S(1)}, f32[48,128]{1,0:T(8,128)S(1)}, bf16[6,4,128,128]{3,2,1,0:T(8,128)(2,1)S(1)}) custom-call(s32[1,2,4]{2,1,0:T(2,128)S(1)} %bitcast.12, bf16[8,128,128]{2,1,0:T(8,128)(2,1)S(1)} %bitcast.8, bf16[6,8,128,128]{3,2,1,0:T(8,128)(2,1)S(1)} %bitcast.16), custom_call_target="tpu_custom_call" | custom-call | flops 1073741824 | bytes 2097152 | tf_op jit(solution)/shard_map/inverse/pallas_call | solution.py:375
  19.0 0.0 collective-permute-done.4.hz
  19.0 0.0 collective-permute-done.3.hd
  19.1 0.0 collective-permute-done.2.hc
  19.1 0.0 collective-permute-done.1.hb
  19.1 0.0 collective-permute-done.ha
  19.1 0.0 copy-start.3
  19.1 3.1 %interp.1 = (bf16[6,8,128,128]{3,2,1,0:T(8,128)(2,1)}, s32[1]{0:T(128)}, bf16[2,4,128,128]{3,2,1,0:T(8,128)(2,1)S(1)}, bf16[2,4,128,128]{3,2,1,0:T(8,128)(2,1)S(...) custom-call(s32[1,2,4]{2,1,0:T(2,128)S(1)} %bitcast.13, ...), custom_call_target="tpu_custom_call" | custom-call | flops 1073741824 | bytes 2097152 | tf_op jit(solution)/shard_map/interp/pallas_call | solution.py:380
  22.2 2.1 %collective-permute-start.5 = (bf16[2,4,128,128]{3,2,1,0:T(8,128)(2,1)S(1)}, bf16[2,4,128,128]{3,2,1,0:T(8,128)(2,1)S(1)}, u32[]{:S(2)}, u32[]{:S(2)}) collective-permute-start(bf16[2,4,128,128]{3,2,1,0:T(8,128)(2,1)S(1)} %get-tuple-element.25), channel_id=1, source_target_pairs={{0,16},{32,48},{64,80},{96,112},{16,0},{48,32},{80,64},{112,96},{1... | collective-permute-start | bytes 786440 | tf_op jit(solution)/shard_map/ppermute | solution.py:344
  24.3 4.0 %collective-permute-start.6 = (bf16[2,4,128,128]{3,2,1,0:T(8,128)(2,1)S(1)}, bf16[2,4,128,128]{3,2,1,0:T(8,128)(2,1)S(1)}, u32[]{:S(2)}, u32[]{:S(2)}) collective-permute-start(bf16[2,4,128,128]{3,2,1,0:T(8,128)(2,1)S(1)} %get-tuple-element.26), channel_id=1, source_target_pairs={{16,32},{48,64},{80,96},{32,16},{64,48},{96,80},{17,33},{49,65},{8... | collective-permute-start | bytes 786440 | tf_op jit(solution)/shard_map/ppermute | solution.py:344
  28.3 0.1 collective-permute-start.9
  28.4 0.1 collective-permute-start.7
  28.5 0.7 %collective-permute-start.8 = (bf16[2,1,128,128]{3,2,1,0:T(8,128)(2,1)S(1)}, bf16[2,1,128,128]{3,2,1,0:T(8,128)(2,1)S(1)}, u32[]{:S(2)}, u32[]{:S(2)}) collective-permute-start(bf16[2,1,128,128]{3,2,1,0:T(8,128)(2,1)S(1)} %get-tuple-element.28), channel_id=1, source_target_pairs={{2,4},{6,8},{10,12},{4,2},{8,6},{12,10},{3,5},{7,9},{11,13},{5,3},... | collective-permute-start | bytes 196616 | tf_op jit(solution)/shard_map/ppermute | solution.py:344
  29.2 0.0 copy-done.3
  29.2 2.9 %near.1 = (f32[8,128,128]{2,1,0:T(8,128)S(1)}, bf16[14,128,128]{2,1,0:T(8,128)(2,1)S(1)}) custom-call(s32[1,2,4]{2,1,0:T(2,128)S(1)} %bitcast.14, s32[1]{0:T(128)} %get-tuple-element.20.code_ref, bf16[8,128,128]{2,1,0:T(8,128)(2,1)S(1)} %bitcast.10, bf16[6,8,128,128]{3,2,1,0:T(8,128)(2,1)S(1)} %bitcast.17, ...), custom_call_target="tpu_custom_call" | custom-call | flops 1073741824 | bytes 2097152 | tf_op jit(solution)/shard_map/near/pallas_call | solution.py:397
  32.1 0.8 %collective-permute-done.7.ya_ref = bf16[2,1,128,128]{3,2,1,0:T(8,128)(2,1)S(1)} collective-permute-done((bf16[2,1,128,128]{3,2,1,0:T(8,128)(2,1)S(1)}, bf16[2,1,128,128]{3,2,1,0:T(8,128)(2,1)S(1)}, u32[]{:S(2)}, u32[]{:S(2)}) %collective-permute-start.7) | collective-permute-done | bytes 65568 | tf_op jit(solution)/shard_map/ppermute | solution.py:344
  32.9 0.0 collective-permute-done.8.yb_ref
  32.9 0.0 collective-permute-done.5.xa_ref
  32.9 4.5 %collective-permute-done.6.xb_ref = bf16[2,4,128,128]{3,2,1,0:T(8,128)(2,1)S(1)} collective-permute-done((bf16[2,4,128,128]{3,2,1,0:T(8,128)(2,1)S(1)}, bf16[2,4,128,128]{3,2,1,0:T(8,128)(2,1)S(1)}, u32[]{:S(2)}, u32[]{:S(2)}) %collective-permute-start.6) | collective-permute-done | bytes 262176 | tf_op jit(solution)/shard_map/ppermute | solution.py:344
  37.3 0.0 collective-permute-done.9.z_ref
  37.3 2.5 %coarse.1 = f32[8,128,128]{2,1,0:T(8,128)} custom-call(s32[1,2,4]{2,1,0:T(2,128)S(1)} %bitcast.15, s32[1]{0:T(128)} %get-tuple-element.20.code_ref, f32[8,128,128]{2,1,0:T(8,128)S(1)} %get-tuple-element.23.sum_ref, bf16[14,128,128]{2,1,0:T(8,128)(2,1)S(1)} %get-tuple-element.24.far_ref, bf16[2,4,128,128]{3,2,1,0:T(8,128)(2,1)S(1)} %collective-permute-done.5.xa_ref, ...), custom_call_target="tpu_custom_call" | custom-call | flops 1073741824 | bytes 2097152 | tf_op jit(solution)/shard_map/coarse/pallas_call | solution.py:402
Async XLA Ops:
  0.6 1.0 %copy-start = (bf16[1,4,2,128,128]{4,3,2,1,0:T(8,128)(2,1)S(1)}, bf16[1,4,2,128,128]{4,3,2,1,0:T(8,128)(2,1)}, u32[]{:S(2)}) copy-start(bf16[1,4,2,128,128]{4,3,2,1,0:T(8,128)(2,1)} %param.3) | copy-start | bytes 786436
  1.6 0.7 %copy-start.1 = (s32[1,4,2]{1,2,0:T(2,128)S(1)}, s32[1,4,2]{1,2,0:T(2,128)}, u32[]{:S(2)}) copy-start(s32[1,4,2]{1,2,0:T(2,128)} %param.5) | copy-start | bytes 100
  3.0 16.1 %collective-permute-start.4 = (f32[16,128]{1,0:T(8,128)S(1)}, f32[16,128]{1,0:T(8,128)S(1)}, u32[]{:S(2)}, u32[]{:S(2)}) collective-permute-start(f32[16,128]{1,0:T(8,128)S(1)} %facts.1.facts_ref), channel_id=1, source_target_pairs={{0,1},{1,0},{2,3},{3,2},{4,5},{5,4},{6,7},{7,6},{8,9},{9,8},{10,11... | collective-permute-start | bytes 24584 | tf_op jit(solution)/shard_map/ppermute | solution.py:344
  3.0 16.1 %collective-permute-start.3 = (f32[16,128]{1,0:T(8,128)S(1)}, f32[16,128]{1,0:T(8,128)S(1)}, u32[]{:S(2)}, u32[]{:S(2)}) collective-permute-start(f32[16,128]{1,0:T(8,128)S(1)} %facts.1.facts_ref), channel_id=1, source_target_pairs={{2,4},{6,8},{10,12},{4,2},{8,6},{12,10},{3,5},{7,9},{11,13},{5,3},... | collective-permute-start | bytes 24584 | tf_op jit(solution)/shard_map/ppermute | solution.py:344
  3.6 15.4 %collective-permute-start.2 = (f32[16,128]{1,0:T(8,128)S(1)}, f32[16,128]{1,0:T(8,128)S(1)}, u32[]{:S(2)}, u32[]{:S(2)}) collective-permute-start(f32[16,128]{1,0:T(8,128)S(1)} %facts.1.facts_ref), channel_id=1, source_target_pairs={{0,2},{4,6},{8,10},{12,14},{2,0},{6,4},{10,8},{14,12},{1,3},{5,7},... | collective-permute-start | bytes 24584 | tf_op jit(solution)/shard_map/ppermute | solution.py:344
  7.9 11.1 %collective-permute-start.1 = (f32[16,128]{1,0:T(8,128)S(1)}, f32[16,128]{1,0:T(8,128)S(1)}, u32[]{:S(2)}, u32[]{:S(2)}) collective-permute-start(f32[16,128]{1,0:T(8,128)S(1)} %facts.1.facts_ref), channel_id=1, source_target_pairs={{16,32},{48,64},{80,96},{32,16},{64,48},{96,80},{17,33},{49,65},{8... | collective-permute-start | bytes 24584 | tf_op jit(solution)/shard_map/ppermute | solution.py:344
  13.4 5.7 %collective-permute-start = (f32[16,128]{1,0:T(8,128)S(1)}, f32[16,128]{1,0:T(8,128)S(1)}, u32[]{:S(2)}, u32[]{:S(2)}) collective-permute-start(f32[16,128]{1,0:T(8,128)S(1)} %facts.1.facts_ref), channel_id=1, source_target_pairs={{0,16},{32,48},{64,80},{96,112},{16,0},{48,32},{80,64},{112,96},{1... | collective-permute-start | bytes 24584 | tf_op jit(solution)/shard_map/ppermute | solution.py:344
  13.5 1.4 %copy-start.2 = (bf16[6,1,4,2,128,128]{5,4,3,2,1,0:T(8,128)(2,1)S(1)}, bf16[6,1,4,2,128,128]{5,4,3,2,1,0:T(8,128)(2,1)}, u32[]{:S(2)}) copy-start(bf16[6,1,4,2,128,128]{5,4,3,2,1,0:T(8,128)(2,1)} %param.4) | copy-start | bytes 4718596
  19.1 10.1 %copy-start.3 = (bf16[6,1,4,2,128,128]{5,4,3,2,1,0:T(8,128)(2,1)S(1)}, bf16[6,1,4,2,128,128]{5,4,3,2,1,0:T(8,128)(2,1)}, u32[]{:S(2)}) copy-start(bf16[6,1,4,2,128,128]{5,4,3,2,1,0:T(8,128)(2,1)} %param.4) | copy-start | bytes 4718596
  22.2 10.7 %collective-permute-start.5 = (bf16[2,4,128,128]{3,2,1,0:T(8,128)(2,1)S(1)}, bf16[2,4,128,128]{3,2,1,0:T(8,128)(2,1)S(1)}, u32[]{:S(2)}, u32[]{:S(2)}) collective-permute-start(bf16[2,4,128,128]{3,2,1,0:T(8,128)(2,1)S(1)} %get-tuple-element.25), channel_id=1, source_target_pairs={{0,16},{32,48},{64,80},{96,112},{16,0},{48,32},{80,64},{112,96},{1... | collective-permute-start | bytes 786440 | tf_op jit(solution)/shard_map/ppermute | solution.py:344
  24.3 13.1 %collective-permute-start.6 = (bf16[2,4,128,128]{3,2,1,0:T(8,128)(2,1)S(1)}, bf16[2,4,128,128]{3,2,1,0:T(8,128)(2,1)S(1)}, u32[]{:S(2)}, u32[]{:S(2)}) collective-permute-start(bf16[2,4,128,128]{3,2,1,0:T(8,128)(2,1)S(1)} %get-tuple-element.26), channel_id=1, source_target_pairs={{16,32},{48,64},{80,96},{32,16},{64,48},{96,80},{17,33},{49,65},{8... | collective-permute-start | bytes 786440 | tf_op jit(solution)/shard_map/ppermute | solution.py:344
  28.3 9.0 %collective-permute-start.9 = (bf16[2,4,128,128]{3,2,1,0:T(8,128)(2,1)S(1)}, bf16[2,4,128,128]{3,2,1,0:T(8,128)(2,1)S(1)}, u32[]{:S(2)}, u32[]{:S(2)}) collective-permute-start(bf16[2,4,128,128]{3,2,1,0:T(8,128)(2,1)S(1)} %get-tuple-element.29), channel_id=1, source_target_pairs={{0,1},{1,0},{2,3},{3,2},{4,5},{5,4},{6,7},{7,6},{8,9},{9,8},{10,11... | collective-permute-start | bytes 786440 | tf_op jit(solution)/shard_map/ppermute | solution.py:344
  28.4 4.5 %collective-permute-start.7 = (bf16[2,1,128,128]{3,2,1,0:T(8,128)(2,1)S(1)}, bf16[2,1,128,128]{3,2,1,0:T(8,128)(2,1)S(1)}, u32[]{:S(2)}, u32[]{:S(2)}) collective-permute-start(bf16[2,1,128,128]{3,2,1,0:T(8,128)(2,1)S(1)} %get-tuple-element.27), channel_id=1, source_target_pairs={{0,2},{4,6},{8,10},{12,14},{2,0},{6,4},{10,8},{14,12},{1,3},{5,7},... | collective-permute-start | bytes 196616 | tf_op jit(solution)/shard_map/ppermute | solution.py:344
  28.5 4.4 %collective-permute-start.8 = (bf16[2,1,128,128]{3,2,1,0:T(8,128)(2,1)S(1)}, bf16[2,1,128,128]{3,2,1,0:T(8,128)(2,1)S(1)}, u32[]{:S(2)}, u32[]{:S(2)}) collective-permute-start(bf16[2,1,128,128]{3,2,1,0:T(8,128)(2,1)S(1)} %get-tuple-element.28), channel_id=1, source_target_pairs={{2,4},{6,8},{10,12},{4,2},{8,6},{12,10},{3,5},{7,9},{11,13},{5,3},... | collective-permute-start | bytes 196616 | tf_op jit(solution)/shard_map/ppermute | solution.py:344

commit v3 on v2

--- a/solution.py
+++ b/solution.py
@@ -39,7 +39,7 @@
 
 
 def split_at(split_ref, c, z):
-    return split_ref[0, z, c]
+    return split_ref[2 * c + z, 0]
 
 
 def fine_of(split_ref, c):
@@ -55,11 +55,21 @@
     return jnp.broadcast_to(jnp.sqrt(jnp.sum(rows, axis=1, keepdims=True)), rows.shape)
 
 
-def facts_kernel(split_ref, diag_ref, facts_ref, rows):
+def facts_kernel(split_ref, diag_ref, facts_ref, flags_ref, kept_ref, rows, held, sems):
+    copies = [
+        pltpu.make_async_copy(diag_ref.at[e], kept_ref.at[e], sems.at[e]) for e in range(8)
+    ]
+    copies.append(pltpu.make_async_copy(split_ref, held, sems.at[8]))
+    for copy in copies[::-1]:
+        copy.start()
+    copies[8].wait()
     for e in range(8):
-        rows[pl.ds(e, 1), :] = square_sums(diag_ref[e])
-        part = split_at(split_ref, e // 2, e % 2).astype(F32)
-        facts_ref[pl.ds(8 + e, 1), :] = jnp.full((1, B), part, F32)
+        part = held[0, e % 2, e // 2]
+        flags_ref[pl.ds(e, 1), :] = jnp.full((1, B), part, jnp.int32)
+    facts_ref[pl.ds(8, 8), :] = flags_ref[...].astype(F32)
+    for e in range(8):
+        copies[e].wait()
+        rows[pl.ds(e, 1), :] = square_sums(kept_ref[e])
     facts_ref[pl.ds(0, 8), :] = norms_of(rows[...])
 
 
@@ -243,7 +253,8 @@
     code = jnp.zeros((8, B), F32)
     for place, ref in enumerate((ha, hb, hc, hd)):
         code = code + ref[pl.ds(8, 8), :] * (bit * (1 << (4 * place))).astype(F32)
-    code_ref[0] = jnp.sum(code).astype(jnp.int32)
+    code = jnp.sum(jnp.sum(code, axis=0, keepdims=True), axis=1, keepdims=True)
+    code_ref[...] = jnp.broadcast_to(code, (8, B)).astype(jnp.int32)
     for c in range(4):
         a = diag_ref[2 * c + fines[c]]
         here = slots(c)
@@ -272,67 +283,70 @@
         copy.wait()
 
 
-def near_kernel(
-    split_ref, code_ref, diag_ref, face_ref, near_ref, inside_ref,
-    sum_ref, far_ref, held_ref, sems,
+def near_kernel(split_ref, diag_ref, face_ref, near_ref, inside_ref, sum_ref):
+    fines = [fine_of(split_ref, c) for c in range(4)]
+    for c in range(4):
+        arrived = []
+        if c > 0:
+            arrived.append((fines[c - 1], 2, near_ref.at[1, 0, c - 1], near_ref.at[1, 1, c - 1]))
+        if c < 3:
+            arrived.append((fines[c + 1], 3, near_ref.at[0, 0, c + 1], near_ref.at[0, 1, c + 1]))
+        arrived.append((1 - fines[c], 4 + fines[c], inside_ref.at[0, c], inside_ref.at[1, c]))
+        gather(c, arrived, face_ref, lambda e: diag_ref[e].astype(F32), sum_ref)
+
+
+def gather(c, arrived, face_ref, start, out_ref):
+    totals = [start(2 * c), start(2 * c + 1)]
+    for z, d, interp, contrib in arrived:
+        part = contrib[...].astype(F32) + mm(face_ref[d, 2 * c + z], interp[...])
+        totals = [total + jnp.where(z == k, part, 0.0) for k, total in enumerate(totals)]
+    for k in range(2):
+        out_ref[2 * c + k] = totals[k]
+
+
+def coarse_kernel(
+    split_ref, code_ref, sum_ref, face_ref, xa_ref, xb_ref, ya_ref, yb_ref, z_ref,
+    coarse_ref, total_ref, sems,
 ):
     gx, gy, gz = lax.axis_index("gx"), lax.axis_index("gy"), lax.axis_index("gz")
-    fines = [fine_of(split_ref, c) for c in range(4)]
-    local = []
-    for c in range(4):
-        if c > 0:
-            local.append((2 * c + fines[c - 1], 2, near_ref.at[1, 0, c - 1], near_ref.at[1, 1, c - 1]))
-        if c < 3:
-            local.append((2 * c + fines[c + 1], 3, near_ref.at[0, 0, c + 1], near_ref.at[0, 1, c + 1]))
-        local.append((2 * c + 1 - fines[c], 4 + fines[c], inside_ref.at[0, c], inside_ref.at[1, c]))
+    code = code_ref[0, 0]
+    up = gy % 2 == 0
+
+    def bit_at(place):
+        return lax.shift_right_logical(code, place) & 1
+
     copies = []
-
-    def fetch(target, d, into):
-        copies.append(pltpu.make_async_copy(face_ref.at[d, target], into, sems.at[len(copies)]))
-        copies[-1].start()
-
-    for k, (target, d, _, _) in enumerate(local):
-        fetch(target, d, held_ref.at[k])
-    for k, (target, d) in enumerate(far_targets(code_ref[0], gx, gy, gz)):
-        fetch(target, d, far_ref.at[k])
-    for e in range(8):
-        sum_ref[e] = diag_ref[e].astype(F32)
+    for c in (1, 2, 0, 3):
+        arrived = [
+            (bit_at(c), 1 - gx % 2, xa_ref.at[0, c], xa_ref.at[1, c]),
+            (bit_at(4 + c), gx % 2, xb_ref.at[0, c], xb_ref.at[1, c]),
+            (1 - gz, 5 - gz, z_ref.at[0, c], z_ref.at[1, c]),
+        ]
+        extra = None
+        if c in (0, 3):
+            first = up if c == 3 else jnp.logical_not(up)
+            edge = 0 if c == 3 else 3
+            z = jnp.where(first, bit_at(8 + edge), bit_at(12 + edge))
+            pair = [jnp.where(first, ya_ref[k, 0], yb_ref[k, 0]) for k in range(2)]
+            extra = (z, 3 if c == 3 else 2, pair)
+        totals = [sum_ref[2 * c], sum_ref[2 * c + 1]]
+        parts = [
+            (z, contrib[...].astype(F32) + mm(face_ref[d, 2 * c + z], interp[...]))
+            for z, d, interp, contrib in arrived
+        ]
+        if extra:
+            z, d, (interp, contrib) = extra
+            parts.append((z, contrib.astype(F32) + mm(face_ref[d, 2 * c + z], interp)))
+        for k in range(2):
+            e = 2 * c + k
+            keep = split_at(split_ref, c, k) == 1
+            for z, part in parts:
+                totals[k] = totals[k] + jnp.where(z == k, part, 0.0)
+            total_ref[e] = jnp.where(keep, totals[k], 0.0)
+            copies.append(pltpu.make_async_copy(total_ref.at[e], coarse_ref.at[e], sems.at[e]))
+            copies[-1].start()
     for copy in copies:
         copy.wait()
-    for k, (target, _, interp, contrib) in enumerate(local):
-        sum_ref[target] = sum_ref[target] + (contrib[...].astype(F32) + mm(held_ref[k], interp[...]))
-
-
-def far_targets(code, gx, gy, gz):
-    def bit_at(place):
-        return lax.shift_right_logical(code, place) & 1
-
-    up = gy % 2 == 0
-    found = [(2 * c + bit_at(c), 1 - gx % 2) for c in range(4)]
-    found += [(2 * c + bit_at(4 + c), gx % 2) for c in range(4)]
-    code_a = jnp.where(up, bit_at(8), bit_at(11))
-    code_b = jnp.where(up, bit_at(15), bit_at(12))
-    found.append((jnp.where(up, 6, 0) + code_a, jnp.where(up, 3, 2)))
-    found.append((jnp.where(up, 0, 6) + code_b, jnp.where(up, 2, 3)))
-    return found + [(2 * c + 1 - gz, 5 - gz) for c in range(4)]
-
-
-def coarse_kernel(
-    split_ref, code_ref, sum_ref, far_ref, xa_ref, xb_ref, ya_ref, yb_ref, z_ref, coarse_ref
-):
-    gx, gy, gz = lax.axis_index("gx"), lax.axis_index("gy"), lax.axis_index("gz")
-    arrived = [(ref, c) for ref in (xa_ref, xb_ref) for c in range(4)]
-    arrived += [(ya_ref, 0), (yb_ref, 0)] + [(z_ref, c) for c in range(4)]
-    for e in range(8):
-        coarse_ref[e] = sum_ref[e]
-    targets = far_targets(code_ref[0], gx, gy, gz)
-    for k, ((target, _), (ref, c)) in enumerate(zip(targets, arrived)):
-        coarse_ref[target] = coarse_ref[target] + (
-            ref[1, c].astype(F32) + mm(far_ref[k], ref[0, c])
-        )
-    for e in range(8):
-        keep = split_at(split_ref, e // 2, e % 2) == 1
-        coarse_ref[e] = jnp.where(keep, coarse_ref[e], 0.0)
 
 
 def matching(size, start):
@@ -363,45 +377,47 @@
     split = jnp.transpose(split, (0, 2, 1))
     sds = jax.ShapeDtypeStruct
     dma = pltpu.SemaphoreType.DMA
-    facts = call(
-        facts_kernel, sds((16, B), F32), [SMEM, VMEM], VMEM,
-        [pltpu.VMEM((8, B), F32)], 1 << 20, "facts",
-    )(split, diag)
+    in_hbm = lambda x: pltpu.with_memory_space_constraint(x, pltpu.HBM)
+    blocks = lambda *lead: sds(lead + (B, B), BF16)
+    facts, flags, diag = call(
+        facts_kernel, (sds((16, B), F32), sds((8, B), jnp.int32), blocks(8)),
+        [HBM, HBM], (VMEM, VMEM, VMEM),
+        [pltpu.VMEM((8, B), F32), pltpu.SMEM((1, 2, 4), jnp.int32), dma((9,))], 1 << 20, "facts",
+    )(in_hbm(split), in_hbm(diag))
     halo = (
         swap(facts, "gx", 0), swap(facts, "gx", 1),
         swap(facts, "gy", 0), swap(facts, "gy", 1), swap(facts, "gz", 0),
     )
-    blocks = lambda *lead: sds(lead + (B, B), BF16)
     inv, fnorm, fine = call(
         inverse_kernel, (blocks(3, 4), sds((48, B), F32), blocks(6, 4)),
         [SMEM, VMEM, HBM], (VMEM, VMEM, VMEM),
         [pltpu.VMEM((48, B), F32), pltpu.VMEM((2, B, B), F32), dma((24,))], 1 << 30, "inverse",
-    )(split, diag, face)
+    )(flags, diag, in_hbm(face))
     interp, code, xa, xb, ya, yb, z, near, inside = call(
         interp_kernel,
         (
-            blocks(6, 8), sds((1,), jnp.int32), blocks(2, 4), blocks(2, 4), blocks(2, 1),
+            blocks(6, 8), sds((8, B), jnp.int32), blocks(2, 4), blocks(2, 4), blocks(2, 1),
             blocks(2, 1), blocks(2, 4), blocks(2, 2, 4), blocks(2, 4),
         ),
         [SMEM] + [VMEM] * 10,
-        (HBM, SMEM) + (VMEM,) * 7,
+        (HBM,) + (VMEM,) * 8,
         [
             pltpu.VMEM((6, 8, B), F32), pltpu.VMEM((4, 6, 2 * B, B), BF16),
             pltpu.VMEM((B, B), BF16), dma((48,)),
         ],
         1 << 30, "interp",
-    )(split, diag, fine, inv, fnorm, facts, *halo)
-    xa, xb = swap(xa, "gx", 0), swap(xb, "gx", 1)
-    ya, yb = swap(ya, "gy", 0), swap(yb, "gy", 1)
+    )(flags, diag, fine, inv, fnorm, facts, *halo)
+    xb = swap(xb, "gx", 1)
+    xa = swap(xa, "gx", 0)
+    yb, ya = swap(yb, "gy", 1), swap(ya, "gy", 0)
     z = swap(z, "gz", 0)
-    total, far = call(
-        near_kernel, (sds((8, B, B), F32), blocks(14)),
-        [SMEM, SMEM, VMEM, HBM, VMEM, VMEM], (VMEM, VMEM),
-        [pltpu.VMEM((10, B, B), BF16), dma((24,))], 1 << 30, "near",
-    )(split, code, diag, face, near, inside)
+    total = call(
+        near_kernel, sds((8, B, B), F32), [SMEM] + [VMEM] * 4, VMEM, [], 1 << 30, "near",
+    )(flags, diag, face, near, inside)
     coarse = call(
-        coarse_kernel, sds((8, B, B), F32), [SMEM, SMEM] + [VMEM] * 7, VMEM, [], 1 << 30, "coarse",
-    )(split, code, total, far, xa, xb, ya, yb, z)
+        coarse_kernel, sds((8, B, B), F32), [SMEM, SMEM] + [VMEM] * 7, HBM,
+        [pltpu.VMEM((8, B, B), F32), dma((8,))], 1 << 30, "coarse",
+    )(flags, code, total, face, xa, xb, ya, yb, z)
     return interp.reshape(face_blocks.shape), coarse.reshape(diag_blocks.shape)
 
 

time: 40.1 us -> 36 us (0.90)
  Pallas kernels: 13.3 us -> 9.78 us
  local copies, waits for them, and re-layouts: 3.03 us -> 0.01 us
  waiting for transfers between devices: 5.28 us -> 7.88 us
    unnamed x8 -> x2, local copies, waits for them, and re-layouts: 3.03 us -> 0.01 us
    pallas_call x4, Pallas kernels: 9.17 us -> 6.51 us  [the longest x1 2.61 us: on_device(): call(interp_kernel, (blocks(6, 8), sds((8, B), jnp.int32), blocks(2, 4),...]
    ppermute x10, waiting for transfers between devices: 5.28 us -> 7.88 us  [swap(): return lax.ppermute(x, axis, matching(lax.axis_size(axis), start))]
    pallas_call x1, Pallas kernels: 4.15 us -> 3.27 us  [on_device(): call(inverse_kernel, (blocks(3, 4), sds((48, B), F32), blocks(6, 4)), [SM...]
  transfers between devices with their start and end apart: 10 -> 10, of which waited for: 2 -> 3; matrix products, arithmetic and copies ran while one was open for 0% -> 0% of each run, Pallas kernels for 18% -> 12%
where the time goes in v3:
time: 36 us; the launch traced here: 35.6 us
  starting transfers between devices  17.2 us (48%)
  Pallas kernels  9.78 us (27%)
  waiting for transfers between devices  7.88 us (22%)
  between operations  0.75 us (2%)
    ppermute x10, starting transfers between devices, swap(): return lax.ppermute(x, axis, matching(lax.axis_size(axis), start))  17.2 us
    ppermute x10, waiting for transfers between devices, swap(): return lax.ppermute(x, axis, matching(lax.axis_size(axis), start))  7.88 us
    pallas_call x1, Pallas kernels, on_device(): call(inverse_kernel, (blocks(3, 4), sds((48, B), F32), blocks(6, 4)), [SM...  3.27 us
    pallas_call x1, Pallas kernels, on_device(): call(interp_kernel, (blocks(6, 8), sds((8, B), jnp.int32), blocks(2, 4),...  2.61 us
    pallas_call x1, Pallas kernels, on_device(): call(coarse_kernel, sds((8, B, B), F32), [SMEM, SMEM] + [VMEM] * 7, HBM,...  1.76 us
    pallas_call x1, Pallas kernels, on_device(): call(facts_kernel, (sds((16, B), F32), sds((8, B), jnp.int32), blocks(8))...  1.25 us
    pallas_call x1, Pallas kernels, on_device(): call(near_kernel, sds((8, B, B), F32), [SMEM] + [VMEM] * 4, VMEM, [], 1 <...  0.89 us
  transfers between devices with their start and end apart: 10, of which 3 were waited for; matrix products, arithmetic and copies ran while one was open for 0% of the time, Pallas kernels for 12%

profile of v3, /device:TPU:24, one launch (start us, length us, event | category | flops | bytes accessed | tf_op | source)
XLA Modules:
  0.0 35.6 jit_solution(13702737307436672103)
XLA Ops:
  0.6 1.3 %facts.1 = (f32[16,128]{1,0:T(8,128)S(1)}, s32[8,128]{1,0:T(8,128)S(1)}, bf16[8,128,128]{2,1,0:T(8,128)(2,1)S(1)}) custom-call(s32[1,2,4]{2,1,0:T(2,128)} %bitcast.11, bf16[8,128,128]{2,1,0:T(8,128)(2,1)} %bitcast.10), custom_call_target="tpu_custom_call" | custom-call | flops 1048576 | bytes 2097152 | tf_op jit(solution)/shard_map/facts/pallas_call | solution.py:382
  1.9 0.1 collective-permute-start.4
  2.0 0.7 %collective-permute-start.3 = (f32[16,128]{1,0:T(8,128)S(1)}, f32[16,128]{1,0:T(8,128)S(1)}, u32[]{:S(2)}, u32[]{:S(2)}) collective-permute-start(f32[16,128]{1,0:T(8,128)S(1)} %get-tuple-element.22.facts_ref), channel_id=1, source_target_pairs={{2,4},{6,8},{10,12},{4,2},{8,6},{12,10},{3,5},{7,9},{11,13},{5,3},... | collective-permute-start | bytes 24584 | tf_op jit(solution)/shard_map/ppermute | solution.py:358
  2.6 4.3 %collective-permute-start.2 = (f32[16,128]{1,0:T(8,128)S(1)}, f32[16,128]{1,0:T(8,128)S(1)}, u32[]{:S(2)}, u32[]{:S(2)}) collective-permute-start(f32[16,128]{1,0:T(8,128)S(1)} %get-tuple-element.22.facts_ref), channel_id=1, source_target_pairs={{0,2},{4,6},{8,10},{12,14},{2,0},{6,4},{10,8},{14,12},{1,3},{5,7},... | collective-permute-start | bytes 24584 | tf_op jit(solution)/shard_map/ppermute | solution.py:358
  6.9 5.4 %collective-permute-start.1 = (f32[16,128]{1,0:T(8,128)S(1)}, f32[16,128]{1,0:T(8,128)S(1)}, u32[]{:S(2)}, u32[]{:S(2)}) collective-permute-start(f32[16,128]{1,0:T(8,128)S(1)} %get-tuple-element.22.facts_ref), channel_id=1, source_target_pairs={{16,32},{48,64},{80,96},{32,16},{64,48},{96,80},{17,33},{49,65},{8... | collective-permute-start | bytes 24584 | tf_op jit(solution)/shard_map/ppermute | solution.py:358
  12.4 0.1 collective-permute-start
  12.5 3.3 %inverse.1 = (bf16[3,4,128,128]{3,2,1,0:T(8,128)(2,1)S(1)}, f32[48,128]{1,0:T(8,128)S(1)}, bf16[6,4,128,128]{3,2,1,0:T(8,128)(2,1)S(1)}) custom-call(s32[8,128]{1,0:T(8,128)S(1)} %get-tuple-element.17.split_ref, bf16[8,128,128]{2,1,0:T(8,128)(2,1)S(1)} %get-tuple-element.18.diag_ref, bf16[6,8,128,128]{3,2,1,0:T(8,128)(2,1)} %bitcast.7), custom_call_target="tpu_custom_call" | custom-call | flops 1073741824 | bytes 2097152 | tf_op jit(solution)/shard_map/inverse/pallas_call | solution.py:391
  15.7 0.0 collective-permute-done.4.hz
  15.8 0.0 collective-permute-done.3.hd
  15.8 0.0 collective-permute-done.2.hc
  15.8 0.3 collective-permute-done.1.hb
  16.1 0.0 collective-permute-done.ha
  16.1 0.0 copy-start
  16.1 2.6 %interp.1 = (bf16[6,8,128,128]{3,2,1,0:T(8,128)(2,1)}, s32[8,128]{1,0:T(8,128)S(1)}, bf16[2,4,128,128]{3,2,1,0:T(8,128)(2,1)S(1)}, bf16[2,4,128,128]{3,2,1,0:T(8...) custom-call(s32[8,128]{1,0:T(8,128)S(1)} %get-tuple-element.17.split, ...), custom_call_target="tpu_custom_call" | custom-call | flops 1073741824 | bytes 2097152 | tf_op jit(solution)/shard_map/interp/pallas_call | solution.py:396
  18.7 1.8 %collective-permute-start.5 = (bf16[2,4,128,128]{3,2,1,0:T(8,128)(2,1)S(1)}, bf16[2,4,128,128]{3,2,1,0:T(8,128)(2,1)S(1)}, u32[]{:S(2)}, u32[]{:S(2)}) collective-permute-start(bf16[2,4,128,128]{3,2,1,0:T(8,128)(2,1)S(1)} %get-tuple-element.27), channel_id=1, source_target_pairs={{0,16},{32,48},{64,80},{96,112},{16,0},{48,32},{80,64},{112,96},{1... | collective-permute-start | bytes 786440 | tf_op jit(solution)/shard_map/ppermute | solution.py:358
  20.5 4.0 %collective-permute-start.6 = (bf16[2,4,128,128]{3,2,1,0:T(8,128)(2,1)S(1)}, bf16[2,4,128,128]{3,2,1,0:T(8,128)(2,1)S(1)}, u32[]{:S(2)}, u32[]{:S(2)}) collective-permute-start(bf16[2,4,128,128]{3,2,1,0:T(8,128)(2,1)S(1)} %get-tuple-element.28), channel_id=1, source_target_pairs={{16,32},{48,64},{80,96},{32,16},{64,48},{96,80},{17,33},{49,65},{8... | collective-permute-start | bytes 786440 | tf_op jit(solution)/shard_map/ppermute | solution.py:358
  24.5 0.1 collective-permute-start.9
  24.6 0.1 collective-permute-start.7
  24.7 0.7 %collective-permute-start.8 = (bf16[2,1,128,128]{3,2,1,0:T(8,128)(2,1)S(1)}, bf16[2,1,128,128]{3,2,1,0:T(8,128)(2,1)S(1)}, u32[]{:S(2)}, u32[]{:S(2)}) collective-permute-start(bf16[2,1,128,128]{3,2,1,0:T(8,128)(2,1)S(1)} %get-tuple-element.30), channel_id=1, source_target_pairs={{2,4},{6,8},{10,12},{4,2},{8,6},{12,10},{3,5},{7,9},{11,13},{5,3},... | collective-permute-start | bytes 196616 | tf_op jit(solution)/shard_map/ppermute | solution.py:358
  25.4 0.0 copy-done
  25.4 0.9 %near.1.sum_ref = f32[8,128,128]{2,1,0:T(8,128)S(1)} custom-call(s32[8,128]{1,0:T(8,128)S(1)} %get-tuple-element.17.split_ref, bf16[8,128,128]{2,1,0:T(8,128)(2,1)S(1)} %get-tuple-element.18.diag_ref, bf16[6,8,128,128]{3,2,1,0:T(8,128)(2,1)S(1)} %bitcast.8, bf16[2,2,4,128,128]{4,3,2,1,0:T(8,128)(2,1)S(1)} %get-tuple-element.25.near_ref, ...), custom_call_target="tpu_custom_call" | custom-call | flops 1073741824 | bytes 2097152 | tf_op jit(solution)/shard_map/near/pallas_call | solution.py:414
  26.3 2.8 %collective-permute-done.7.ya_ref = bf16[2,1,128,128]{3,2,1,0:T(8,128)(2,1)S(1)} collective-permute-done((bf16[2,1,128,128]{3,2,1,0:T(8,128)(2,1)S(1)}, bf16[2,1,128,128]{3,2,1,0:T(8,128)(2,1)S(1)}, u32[]{:S(2)}, u32[]{:S(2)}) %collective-permute-start.7) | collective-permute-done | bytes 65568 | tf_op jit(solution)/shard_map/ppermute | solution.py:358
  29.1 0.0 collective-permute-done.8.yb_ref
  29.1 0.0 collective-permute-done.5.xa_ref
  29.1 4.7 %collective-permute-done.6.xb_ref = bf16[2,4,128,128]{3,2,1,0:T(8,128)(2,1)S(1)} collective-permute-done((bf16[2,4,128,128]{3,2,1,0:T(8,128)(2,1)S(1)}, bf16[2,4,128,128]{3,2,1,0:T(8,128)(2,1)S(1)}, u32[]{:S(2)}, u32[]{:S(2)}) %collective-permute-start.6) | collective-permute-done | bytes 262176 | tf_op jit(solution)/shard_map/ppermute | solution.py:358
  33.8 0.0 collective-permute-done.9.z_ref
  33.8 1.8 %coarse.1 = f32[8,128,128]{2,1,0:T(8,128)} custom-call(s32[8,128]{1,0:T(8,128)S(1)} %get-tuple-element.17.split_ref, s32[8,128]{1,0:T(8,128)S(1)} %get-tuple-element.24.code_ref, f32[8,128,128]{2,1,0:T(8,128)S(1)} %near.1.sum_ref, bf16[6,8,128,128]{3,2,1,0:T(8,128)(2,1)S(1)} %bitcast.9, bf16[2,4,128,128]{3,2,1,0:T(8,128)(2,1)S(1)} %collective-permute-done.5.xa_ref, ...), custom_call_target="tpu_custom_call" | custom-call | flops 1073741824 | bytes 2097152 | tf_op jit(solution)/shard_map/coarse/pallas_call | solution.py:417
Async XLA Ops:
  1.9 13.9 %collective-permute-start.4 = (f32[16,128]{1,0:T(8,128)S(1)}, f32[16,128]{1,0:T(8,128)S(1)}, u32[]{:S(2)}, u32[]{:S(2)}) collective-permute-start(f32[16,128]{1,0:T(8,128)S(1)} %get-tuple-element.22.facts_ref), channel_id=1, source_target_pairs={{0,1},{1,0},{2,3},{3,2},{4,5},{5,4},{6,7},{7,6},{8,9},{9,8},{10,11... | collective-permute-start | bytes 24584 | tf_op jit(solution)/shard_map/ppermute | solution.py:358
  2.0 13.8 %collective-permute-start.3 = (f32[16,128]{1,0:T(8,128)S(1)}, f32[16,128]{1,0:T(8,128)S(1)}, u32[]{:S(2)}, u32[]{:S(2)}) collective-permute-start(f32[16,128]{1,0:T(8,128)S(1)} %get-tuple-element.22.facts_ref), channel_id=1, source_target_pairs={{2,4},{6,8},{10,12},{4,2},{8,6},{12,10},{3,5},{7,9},{11,13},{5,3},... | collective-permute-start | bytes 24584 | tf_op jit(solution)/shard_map/ppermute | solution.py:358
  2.6 13.1 %collective-permute-start.2 = (f32[16,128]{1,0:T(8,128)S(1)}, f32[16,128]{1,0:T(8,128)S(1)}, u32[]{:S(2)}, u32[]{:S(2)}) collective-permute-start(f32[16,128]{1,0:T(8,128)S(1)} %get-tuple-element.22.facts_ref), channel_id=1, source_target_pairs={{0,2},{4,6},{8,10},{12,14},{2,0},{6,4},{10,8},{14,12},{1,3},{5,7},... | collective-permute-start | bytes 24584 | tf_op jit(solution)/shard_map/ppermute | solution.py:358
  6.9 9.1 %collective-permute-start.1 = (f32[16,128]{1,0:T(8,128)S(1)}, f32[16,128]{1,0:T(8,128)S(1)}, u32[]{:S(2)}, u32[]{:S(2)}) collective-permute-start(f32[16,128]{1,0:T(8,128)S(1)} %get-tuple-element.22.facts_ref), channel_id=1, source_target_pairs={{16,32},{48,64},{80,96},{32,16},{64,48},{96,80},{17,33},{49,65},{8... | collective-permute-start | bytes 24584 | tf_op jit(solution)/shard_map/ppermute | solution.py:358
  12.4 3.7 %collective-permute-start = (f32[16,128]{1,0:T(8,128)S(1)}, f32[16,128]{1,0:T(8,128)S(1)}, u32[]{:S(2)}, u32[]{:S(2)}) collective-permute-start(f32[16,128]{1,0:T(8,128)S(1)} %get-tuple-element.22.facts_ref), channel_id=1, source_target_pairs={{0,16},{32,48},{64,80},{96,112},{16,0},{48,32},{80,64},{112,96},{1... | collective-permute-start | bytes 24584 | tf_op jit(solution)/shard_map/ppermute | solution.py:358
  16.1 9.3 %copy-start = (bf16[6,1,4,2,128,128]{5,4,3,2,1,0:T(8,128)(2,1)S(1)}, bf16[6,1,4,2,128,128]{5,4,3,2,1,0:T(8,128)(2,1)}, u32[]{:S(2)}) copy-start(bf16[6,1,4,2,128,128]{5,4,3,2,1,0:T(8,128)(2,1)} %param.4) | copy-start | bytes 4718596
  18.7 10.4 %collective-permute-start.5 = (bf16[2,4,128,128]{3,2,1,0:T(8,128)(2,1)S(1)}, bf16[2,4,128,128]{3,2,1,0:T(8,128)(2,1)S(1)}, u32[]{:S(2)}, u32[]{:S(2)}) collective-permute-start(bf16[2,4,128,128]{3,2,1,0:T(8,128)(2,1)S(1)} %get-tuple-element.27), channel_id=1, source_target_pairs={{0,16},{32,48},{64,80},{96,112},{16,0},{48,32},{80,64},{112,96},{1... | collective-permute-start | bytes 786440 | tf_op jit(solution)/shard_map/ppermute | solution.py:358
  20.5 13.3 %collective-permute-start.6 = (bf16[2,4,128,128]{3,2,1,0:T(8,128)(2,1)S(1)}, bf16[2,4,128,128]{3,2,1,0:T(8,128)(2,1)S(1)}, u32[]{:S(2)}, u32[]{:S(2)}) collective-permute-start(bf16[2,4,128,128]{3,2,1,0:T(8,128)(2,1)S(1)} %get-tuple-element.28), channel_id=1, source_target_pairs={{16,32},{48,64},{80,96},{32,16},{64,48},{96,80},{17,33},{49,65},{8... | collective-permute-start | bytes 786440 | tf_op jit(solution)/shard_map/ppermute | solution.py:358
  24.5 9.3 %collective-permute-start.9 = (bf16[2,4,128,128]{3,2,1,0:T(8,128)(2,1)S(1)}, bf16[2,4,128,128]{3,2,1,0:T(8,128)(2,1)S(1)}, u32[]{:S(2)}, u32[]{:S(2)}) collective-permute-start(bf16[2,4,128,128]{3,2,1,0:T(8,128)(2,1)S(1)} %get-tuple-element.31), channel_id=1, source_target_pairs={{0,1},{1,0},{2,3},{3,2},{4,5},{5,4},{6,7},{7,6},{8,9},{9,8},{10,11... | collective-permute-start | bytes 786440 | tf_op jit(solution)/shard_map/ppermute | solution.py:358
  24.6 4.5 %collective-permute-start.7 = (bf16[2,1,128,128]{3,2,1,0:T(8,128)(2,1)S(1)}, bf16[2,1,128,128]{3,2,1,0:T(8,128)(2,1)S(1)}, u32[]{:S(2)}, u32[]{:S(2)}) collective-permute-start(bf16[2,1,128,128]{3,2,1,0:T(8,128)(2,1)S(1)} %get-tuple-element.29), channel_id=1, source_target_pairs={{0,2},{4,6},{8,10},{12,14},{2,0},{6,4},{10,8},{14,12},{1,3},{5,7},... | collective-permute-start | bytes 196616 | tf_op jit(solution)/shard_map/ppermute | solution.py:358
  24.7 4.4 %collective-permute-start.8 = (bf16[2,1,128,128]{3,2,1,0:T(8,128)(2,1)S(1)}, bf16[2,1,128,128]{3,2,1,0:T(8,128)(2,1)S(1)}, u32[]{:S(2)}, u32[]{:S(2)}) collective-permute-start(bf16[2,1,128,128]{3,2,1,0:T(8,128)(2,1)S(1)} %get-tuple-element.30), channel_id=1, source_target_pairs={{2,4},{6,8},{10,12},{4,2},{8,6},{12,10},{3,5},{7,9},{11,13},{5,3},... | collective-permute-start | bytes 196616 | tf_op jit(solution)/shard_map/ppermute | solution.py:358

commit v4 on v3

--- a/solution.py
+++ b/solution.py
@@ -4,6 +4,7 @@
 from jax.experimental import pallas as pl
 from jax.experimental.pallas import tpu as pltpu
 from jax.sharding import PartitionSpec as P
+
 
 B = 128
 F32 = jnp.float32
@@ -205,7 +206,7 @@
 def interp_kernel(
     split_ref, diag_ref, fine_ref, inv_ref, fnorm_ref, facts_ref, ha, hb, hc, hd, hz,
     interp_ref, code_ref, xa_ref, xb_ref, ya_ref, yb_ref, z_ref, near_ref, inside_ref,
-    weight_ref, mixed_ref, zero_ref, sems,
+    weight_ref, edge_ref, zero_ref, sems,
 ):
     zero_ref[...] = jnp.zeros((B, B), BF16)
     gx, gy = lax.axis_index("gx"), lax.axis_index("gy")
@@ -221,10 +222,10 @@
         return (
             (1 - gx % 2, xa_ref.at[0, c], xa_ref.at[1, c]),
             (gx % 2, xb_ref.at[0, c], xb_ref.at[1, c]),
-            (2, near_ref.at[0, 0, c], near_ref.at[0, 1, c]),
-            (3, near_ref.at[1, 0, c], near_ref.at[1, 1, c]),
-            (5 - fines[c], inside_ref.at[0, c], inside_ref.at[1, c]),
             (4 + fines[c], z_ref.at[0, c], z_ref.at[1, c]),
+            (2, near_ref.at[0, c], edge_ref.at[0] if c == 0 else None),
+            (3, near_ref.at[1, c], edge_ref.at[1] if c == 3 else None),
+            (5 - fines[c], inside_ref.at[c], None),
         )
 
     def send_column(c):
@@ -256,52 +257,60 @@
     code = jnp.sum(jnp.sum(code, axis=0, keepdims=True), axis=1, keepdims=True)
     code_ref[...] = jnp.broadcast_to(code, (8, B)).astype(jnp.int32)
     for c in range(4):
+        here = [slot for slot in slots(c) if slot[2] is not None]
         a = diag_ref[2 * c + fines[c]]
-        here = slots(c)
-        for s in (0, 2, 4):
-            two = [here[s], here[s + 1]]
-            face = jnp.concatenate([fine_ref[d, c] for d, _, _ in two], axis=1)
-            interp = jnp.concatenate([block[...] for _, block, _ in two], axis=1)
-            hi, lo = halves(mm(a, interp) + face.astype(F32))
-            for t in range(2):
-                lanes = slice(B * t, B * t + B)
-                mixed_ref[c, s + t, pl.ds(0, B), :] = hi[:, lanes]
-                mixed_ref[c, s + t, pl.ds(B, B), :] = lo[:, lanes]
-        if c == 1:
+        faces = [fine_ref[d, c] for d, _, _ in here]
+        found = contribs(a, faces, [block[...] for _, block, _ in here])
+        for (_, _, into), contrib in zip(here, found):
+            into[...] = contrib
+        if c == 0:
             send_column(3)
-    for c in range(4):
-        for s, (_, interp, contrib) in enumerate(slots(c)):
-            turned = jnp.transpose(interp[...])
-            both = jnp.concatenate([turned, turned], axis=1)
-            contrib[...] = mm(both, mixed_ref[c, s]).astype(BF16)
     up = gy % 2 == 0
-    for k in range(2):
-        low, high = near_ref[0, k, 0], near_ref[1, k, 3]
-        ya_ref[k, 0] = jnp.where(up, high, low)
-        yb_ref[k, 0] = jnp.where(up, low, high)
+    low, high = near_ref[0, 0], near_ref[1, 3]
+    ya_ref[0, 0], yb_ref[0, 0] = jnp.where(up, high, low), jnp.where(up, low, high)
+    low, high = edge_ref[0], edge_ref[1]
+    ya_ref[1, 0], yb_ref[1, 0] = jnp.where(up, high, low), jnp.where(up, low, high)
     for copy in copies:
         copy.wait()
 
 
-def near_kernel(split_ref, diag_ref, face_ref, near_ref, inside_ref, sum_ref):
+def contribs(a, faces, interps):
+    found = []
+    for s in range(0, len(faces), 2):
+        pair = interps[s:s + 2]
+        face = jnp.concatenate(faces[s:s + 2], axis=1)
+        hi, lo = halves(mm(a, jnp.concatenate(pair, axis=1)) + face.astype(F32))
+        for t, interp in enumerate(pair):
+            lanes = slice(B * t, B * t + B)
+            turned = jnp.transpose(interp)
+            both = jnp.concatenate([turned, turned], axis=1)
+            mixed = jnp.concatenate([hi[:, lanes], lo[:, lanes]], axis=0)
+            found.append(mm(both, mixed).astype(BF16))
+    return found
+
+
+def near_kernel(split_ref, diag_ref, face_ref, fine_ref, near_ref, inside_ref, sum_ref):
     fines = [fine_of(split_ref, c) for c in range(4)]
+    parts = [[] for _ in range(4)]
     for c in range(4):
-        arrived = []
+        z = fines[c]
+        here = [(c, 1 - z, 4 + z, 5 - z, inside_ref[c])]
         if c > 0:
-            arrived.append((fines[c - 1], 2, near_ref.at[1, 0, c - 1], near_ref.at[1, 1, c - 1]))
+            here.append((c - 1, z, 3, 2, near_ref[0, c]))
         if c < 3:
-            arrived.append((fines[c + 1], 3, near_ref.at[0, 0, c + 1], near_ref.at[0, 1, c + 1]))
-        arrived.append((1 - fines[c], 4 + fines[c], inside_ref.at[0, c], inside_ref.at[1, c]))
-        gather(c, arrived, face_ref, lambda e: diag_ref[e].astype(F32), sum_ref)
-
-
-def gather(c, arrived, face_ref, start, out_ref):
-    totals = [start(2 * c), start(2 * c + 1)]
-    for z, d, interp, contrib in arrived:
-        part = contrib[...].astype(F32) + mm(face_ref[d, 2 * c + z], interp[...])
-        totals = [total + jnp.where(z == k, part, 0.0) for k, total in enumerate(totals)]
-    for k in range(2):
-        out_ref[2 * c + k] = totals[k]
+            here.append((c + 1, z, 2, 3, near_ref[1, c]))
+        found = contribs(
+            diag_ref[2 * c + z], [fine_ref[d, c] for _, _, _, d, _ in here], [p for *_, p in here]
+        )
+        for (to, depth, back, _, interp), contrib in zip(here, found):
+            product = mm(face_ref[back, 2 * to + depth], interp)
+            parts[to].append((depth, contrib.astype(F32) + product))
+    for c in range(4):
+        for k in range(2):
+            total = diag_ref[2 * c + k].astype(F32)
+            for z, part in parts[c]:
+                total = total + jnp.where(z == k, part, 0.0)
+            sum_ref[2 * c + k] = total
 
 
 def coarse_kernel(
@@ -358,7 +367,7 @@
     return lax.ppermute(x, axis, matching(lax.axis_size(axis), start))
 
 
-def call(body, out_shape, in_specs, out_specs, scratch, flops, name):
+def call(body, out_shape, in_specs, out_specs, scratch, flops):
     return pl.pallas_call(
         body,
         out_shape=out_shape,
@@ -367,7 +376,6 @@
         scratch_shapes=scratch,
         compiler_params=pltpu.CompilerParams(vmem_limit_bytes=LIMIT),
         cost_estimate=pl.CostEstimate(flops=flops, bytes_accessed=2 << 20, transcendentals=0),
-        name=name,
     )
 
 
@@ -382,41 +390,41 @@
     facts, flags, diag = call(
         facts_kernel, (sds((16, B), F32), sds((8, B), jnp.int32), blocks(8)),
         [HBM, HBM], (VMEM, VMEM, VMEM),
-        [pltpu.VMEM((8, B), F32), pltpu.SMEM((1, 2, 4), jnp.int32), dma((9,))], 1 << 20, "facts",
+        [pltpu.VMEM((8, B), F32), pltpu.SMEM((1, 2, 4), jnp.int32), dma((9,))], 1 << 20,
     )(in_hbm(split), in_hbm(diag))
     halo = (
         swap(facts, "gx", 0), swap(facts, "gx", 1),
-        swap(facts, "gy", 0), swap(facts, "gy", 1), swap(facts, "gz", 0),
+        swap(facts, "gy", 0), swap(facts, "gy", 1),
+        swap(facts, "gz", 0),
     )
     inv, fnorm, fine = call(
         inverse_kernel, (blocks(3, 4), sds((48, B), F32), blocks(6, 4)),
         [SMEM, VMEM, HBM], (VMEM, VMEM, VMEM),
-        [pltpu.VMEM((48, B), F32), pltpu.VMEM((2, B, B), F32), dma((24,))], 1 << 30, "inverse",
+        [pltpu.VMEM((48, B), F32), pltpu.VMEM((2, B, B), F32), dma((24,))], 1 << 30,
     )(flags, diag, in_hbm(face))
     interp, code, xa, xb, ya, yb, z, near, inside = call(
         interp_kernel,
         (
             blocks(6, 8), sds((8, B), jnp.int32), blocks(2, 4), blocks(2, 4), blocks(2, 1),
-            blocks(2, 1), blocks(2, 4), blocks(2, 2, 4), blocks(2, 4),
+            blocks(2, 1), blocks(2, 4), blocks(2, 4), blocks(4),
         ),
         [SMEM] + [VMEM] * 10,
         (HBM,) + (VMEM,) * 8,
         [
-            pltpu.VMEM((6, 8, B), F32), pltpu.VMEM((4, 6, 2 * B, B), BF16),
+            pltpu.VMEM((6, 8, B), F32), pltpu.VMEM((2, B, B), BF16),
             pltpu.VMEM((B, B), BF16), dma((48,)),
         ],
-        1 << 30, "interp",
+        1 << 30,
     )(flags, diag, fine, inv, fnorm, facts, *halo)
-    xb = swap(xb, "gx", 1)
-    xa = swap(xa, "gx", 0)
-    yb, ya = swap(yb, "gy", 1), swap(ya, "gy", 0)
+    xa, xb = swap(xa, "gx", 0), swap(xb, "gx", 1)
+    ya, yb = swap(ya, "gy", 0), swap(yb, "gy", 1)
     z = swap(z, "gz", 0)
     total = call(
-        near_kernel, sds((8, B, B), F32), [SMEM] + [VMEM] * 4, VMEM, [], 1 << 30, "near",
-    )(flags, diag, face, near, inside)
+        near_kernel, sds((8, B, B), F32), [SMEM] + [VMEM] * 5, VMEM, [], 1 << 30,
+    )(flags, diag, face, fine, near, inside)
     coarse = call(
         coarse_kernel, sds((8, B, B), F32), [SMEM, SMEM] + [VMEM] * 7, HBM,
-        [pltpu.VMEM((8, B, B), F32), dma((8,))], 1 << 30, "coarse",
+        [pltpu.VMEM((8, B, B), F32), dma((8,))], 1 << 30,
     )(flags, code, total, face, xa, xb, ya, yb, z)
     return interp.reshape(face_blocks.shape), coarse.reshape(diag_blocks.shape)
 

time: 36 us -> 36.7 us (1.019)
  Pallas kernels: 9.78 us -> 11.3 us
  waiting for transfers between devices: 7.88 us -> 7.11 us
    pallas_call x1, Pallas kernels: 0.89 us -> 1.65 us  [on_device(): call(near_kernel, sds((8, B, B), F32), [SMEM] + [VMEM] * 5, VMEM, [], 1 <...]
    ppermute x10, waiting for transfers between devices: 7.88 us -> 7.11 us  [swap(): return lax.ppermute(x, axis, matching(lax.axis_size(axis), start))]
    pallas_call x1, Pallas kernels: 2.61 us -> 3.35 us  [on_device(): call(interp_kernel, (blocks(6, 8), sds((8, B), jnp.int32), blocks(2, 4),...]
  transfers between devices with their start and end apart: 10 -> 10, of which waited for: 3 -> 3; matrix products, arithmetic and copies ran while one was open for 0% -> 0% of each run, Pallas kernels for 12% -> 14%
where the time goes in v4:
time: 36.7 us; the launch traced here: 36.4 us
  starting transfers between devices  17.2 us (47%)
  Pallas kernels  11.3 us (31%)
  waiting for transfers between devices  7.11 us (19%)
  between operations  0.75 us (2%)
    ppermute x10, starting transfers between devices, swap(): return lax.ppermute(x, axis, matching(lax.axis_size(axis), start))  17.2 us
    ppermute x10, waiting for transfers between devices, swap(): return lax.ppermute(x, axis, matching(lax.axis_size(axis), start))  7.11 us
    pallas_call x1, Pallas kernels, on_device(): call(interp_kernel, (blocks(6, 8), sds((8, B), jnp.int32), blocks(2, 4),...  3.35 us
    pallas_call x1, Pallas kernels, on_device(): call(inverse_kernel, (blocks(3, 4), sds((48, B), F32), blocks(6, 4)), [SM...  3.27 us
    pallas_call x1, Pallas kernels, on_device(): call(coarse_kernel, sds((8, B, B), F32), [SMEM, SMEM] + [VMEM] * 7, HBM,...  1.76 us
    pallas_call x1, Pallas kernels, on_device(): call(near_kernel, sds((8, B, B), F32), [SMEM] + [VMEM] * 5, VMEM, [], 1 <...  1.65 us
    pallas_call x1, Pallas kernels, on_device(): call(facts_kernel, (sds((16, B), F32), sds((8, B), jnp.int32), blocks(8))...  1.25 us
  transfers between devices with their start and end apart: 10, of which 3 were waited for; matrix products, arithmetic and copies ran while one was open for 0% of the time, Pallas kernels for 14%

profile of v4, /device:TPU:24, one launch (start us, length us, event | category | flops | bytes accessed | tf_op | source)
XLA Modules:
  0.0 36.4 jit_solution(17667317854090540463)
XLA Ops:
  0.6 1.3 %shard_map.50 = (f32[16,128]{1,0:T(8,128)S(1)}, s32[8,128]{1,0:T(8,128)S(1)}, bf16[8,128,128]{2,1,0:T(8,128)(2,1)S(1)}) custom-call(s32[1,2,4]{2,1,0:T(2,128)} %bitcast.11, bf16[8,128,128]{2,1,0:T(8,128)(2,1)} %bitcast.10), custom_call_target="tpu_custom_call" | custom-call | flops 1048576 | bytes 2097152 | tf_op jit(solution)/shard_map/pallas_call | solution.py:390
  1.9 0.1 collective-permute-start.4
  2.0 0.7 %collective-permute-start.3 = (f32[16,128]{1,0:T(8,128)S(1)}, f32[16,128]{1,0:T(8,128)S(1)}, u32[]{:S(2)}, u32[]{:S(2)}) collective-permute-start(f32[16,128]{1,0:T(8,128)S(1)} %get-tuple-element.22.facts_ref), channel_id=1, source_target_pairs={{2,4},{6,8},{10,12},{4,2},{8,6},{12,10},{3,5},{7,9},{11,13},{5,3},... | collective-permute-start | bytes 24584 | tf_op jit(solution)/shard_map/ppermute | solution.py:367
  2.6 4.3 %collective-permute-start.2 = (f32[16,128]{1,0:T(8,128)S(1)}, f32[16,128]{1,0:T(8,128)S(1)}, u32[]{:S(2)}, u32[]{:S(2)}) collective-permute-start(f32[16,128]{1,0:T(8,128)S(1)} %get-tuple-element.22.facts_ref), channel_id=1, source_target_pairs={{0,2},{4,6},{8,10},{12,14},{2,0},{6,4},{10,8},{14,12},{1,3},{5,7},... | collective-permute-start | bytes 24584 | tf_op jit(solution)/shard_map/ppermute | solution.py:367
  6.9 5.4 %collective-permute-start.1 = (f32[16,128]{1,0:T(8,128)S(1)}, f32[16,128]{1,0:T(8,128)S(1)}, u32[]{:S(2)}, u32[]{:S(2)}) collective-permute-start(f32[16,128]{1,0:T(8,128)S(1)} %get-tuple-element.22.facts_ref), channel_id=1, source_target_pairs={{16,32},{48,64},{80,96},{32,16},{64,48},{96,80},{17,33},{49,65},{8... | collective-permute-start | bytes 24584 | tf_op jit(solution)/shard_map/ppermute | solution.py:367
  12.4 0.1 collective-permute-start
  12.5 3.3 %shard_map.51 = (bf16[3,4,128,128]{3,2,1,0:T(8,128)(2,1)S(1)}, f32[48,128]{1,0:T(8,128)S(1)}, bf16[6,4,128,128]{3,2,1,0:T(8,128)(2,1)S(1)}) custom-call(s32[8,128]{1,0:T(8,128)S(1)} %get-tuple-element.17.split_ref, bf16[8,128,128]{2,1,0:T(8,128)(2,1)S(1)} %get-tuple-element.18.diag_ref, bf16[6,8,128,128]{3,2,1,0:T(8,128)(2,1)} %bitcast.7), custom_call_target="tpu_custom_call" | custom-call | flops 1073741824 | bytes 2097152 | tf_op jit(solution)/shard_map/pallas_call | solution.py:400
  15.7 0.0 collective-permute-done.4.hz
  15.8 0.0 collective-permute-done.3.hd
  15.8 0.0 collective-permute-done.2.hc
  15.8 0.3 collective-permute-done.1.hb
  16.1 0.0 collective-permute-done.ha
  16.1 0.0 copy-start
  16.1 3.4 %shard_map.52 = (bf16[6,8,128,128]{3,2,1,0:T(8,128)(2,1)}, s32[8,128]{1,0:T(8,128)S(1)}, bf16[2,4,128,128]{3,2,1,0:T(8,128)(2,1)S(1)}, bf16[2,4,128,128]{3,2,1,0...) custom-call(s32[8,128]{1,0:T(8,128)S(1)} %get-tuple-element.17.split, ...), custom_call_target="tpu_custom_call" | custom-call | flops 1073741824 | bytes 2097152 | tf_op jit(solution)/shard_map/pallas_call | solution.py:405
  19.5 1.8 %collective-permute-start.5 = (bf16[2,4,128,128]{3,2,1,0:T(8,128)(2,1)S(1)}, bf16[2,4,128,128]{3,2,1,0:T(8,128)(2,1)S(1)}, u32[]{:S(2)}, u32[]{:S(2)}) collective-permute-start(bf16[2,4,128,128]{3,2,1,0:T(8,128)(2,1)S(1)} %get-tuple-element.27), channel_id=1, source_target_pairs={{0,16},{32,48},{64,80},{96,112},{16,0},{48,32},{80,64},{112,96},{1... | collective-permute-start | bytes 786440 | tf_op jit(solution)/shard_map/ppermute | solution.py:367
  21.3 4.0 %collective-permute-start.6 = (bf16[2,4,128,128]{3,2,1,0:T(8,128)(2,1)S(1)}, bf16[2,4,128,128]{3,2,1,0:T(8,128)(2,1)S(1)}, u32[]{:S(2)}, u32[]{:S(2)}) collective-permute-start(bf16[2,4,128,128]{3,2,1,0:T(8,128)(2,1)S(1)} %get-tuple-element.28), channel_id=1, source_target_pairs={{16,32},{48,64},{80,96},{32,16},{64,48},{96,80},{17,33},{49,65},{8... | collective-permute-start | bytes 786440 | tf_op jit(solution)/shard_map/ppermute | solution.py:367
  25.3 0.1 collective-permute-start.9
  25.4 0.1 collective-permute-start.7
  25.5 0.7 %collective-permute-start.8 = (bf16[2,1,128,128]{3,2,1,0:T(8,128)(2,1)S(1)}, bf16[2,1,128,128]{3,2,1,0:T(8,128)(2,1)S(1)}, u32[]{:S(2)}, u32[]{:S(2)}) collective-permute-start(bf16[2,1,128,128]{3,2,1,0:T(8,128)(2,1)S(1)} %get-tuple-element.30), channel_id=1, source_target_pairs={{2,4},{6,8},{10,12},{4,2},{8,6},{12,10},{3,5},{7,9},{11,13},{5,3},... | collective-permute-start | bytes 196616 | tf_op jit(solution)/shard_map/ppermute | solution.py:367
  26.1 0.0 copy-done
  26.2 1.7 %shard_map.53.sum_ref = f32[8,128,128]{2,1,0:T(8,128)S(1)} custom-call(s32[8,128]{1,0:T(8,128)S(1)} %get-tuple-element.17.split_ref, bf16[8,128,128]{2,1,0:T(8,128)(2,1)S(1)} %get-tuple-element.18.diag_ref, bf16[6,8,128,128]{3,2,1,0:T(8,128)(2,1)S(1)} %bitcast.8, bf16[6,4,128,128]{3,2,1,0:T(8,128)(2,1)S(1)} %get-tuple-element.19.fine_ref, ...), custom_call_target="tpu_custom_call" | custom-call | flops 1073741824 | bytes 2097152 | tf_op jit(solution)/shard_map/pallas_call | solution.py:422
  27.8 2.0 %collective-permute-done.7.ya_ref = bf16[2,1,128,128]{3,2,1,0:T(8,128)(2,1)S(1)} collective-permute-done((bf16[2,1,128,128]{3,2,1,0:T(8,128)(2,1)S(1)}, bf16[2,1,128,128]{3,2,1,0:T(8,128)(2,1)S(1)}, u32[]{:S(2)}, u32[]{:S(2)}) %collective-permute-start.7) | collective-permute-done | bytes 65568 | tf_op jit(solution)/shard_map/ppermute | solution.py:367
  29.9 0.0 collective-permute-done.8.yb_ref
  29.9 0.0 collective-permute-done.5.xa_ref
  29.9 4.7 %collective-permute-done.6.xb_ref = bf16[2,4,128,128]{3,2,1,0:T(8,128)(2,1)S(1)} collective-permute-done((bf16[2,4,128,128]{3,2,1,0:T(8,128)(2,1)S(1)}, bf16[2,4,128,128]{3,2,1,0:T(8,128)(2,1)S(1)}, u32[]{:S(2)}, u32[]{:S(2)}) %collective-permute-start.6) | collective-permute-done | bytes 262176 | tf_op jit(solution)/shard_map/ppermute | solution.py:367
  34.6 0.0 collective-permute-done.9.z_ref
  34.6 1.8 %shard_map.54 = f32[8,128,128]{2,1,0:T(8,128)} custom-call(s32[8,128]{1,0:T(8,128)S(1)} %get-tuple-element.17.split_ref, s32[8,128]{1,0:T(8,128)S(1)} %get-tuple-element.24.code_ref, f32[8,128,128]{2,1,0:T(8,128)S(1)} %shard_map.53.sum_ref, bf16[6,8,128,128]{3,2,1,0:T(8,128)(2,1)S(1)} %bitcast.9, bf16[2,4,128,128]{3,2,1,0:T(8,128)(2,1)S(1)} %collective-permute-done.5.xa_ref, ...), custom_call_target="tpu_custom_call" | custom-call | flops 1073741824 | bytes 2097152 | tf_op jit(solution)/shard_map/pallas_call | solution.py:425
Async XLA Ops:
  1.9 13.9 %collective-permute-start.4 = (f32[16,128]{1,0:T(8,128)S(1)}, f32[16,128]{1,0:T(8,128)S(1)}, u32[]{:S(2)}, u32[]{:S(2)}) collective-permute-start(f32[16,128]{1,0:T(8,128)S(1)} %get-tuple-element.22.facts_ref), channel_id=1, source_target_pairs={{0,1},{1,0},{2,3},{3,2},{4,5},{5,4},{6,7},{7,6},{8,9},{9,8},{10,11... | collective-permute-start | bytes 24584 | tf_op jit(solution)/shard_map/ppermute | solution.py:367
  2.0 13.8 %collective-permute-start.3 = (f32[16,128]{1,0:T(8,128)S(1)}, f32[16,128]{1,0:T(8,128)S(1)}, u32[]{:S(2)}, u32[]{:S(2)}) collective-permute-start(f32[16,128]{1,0:T(8,128)S(1)} %get-tuple-element.22.facts_ref), channel_id=1, source_target_pairs={{2,4},{6,8},{10,12},{4,2},{8,6},{12,10},{3,5},{7,9},{11,13},{5,3},... | collective-permute-start | bytes 24584 | tf_op jit(solution)/shard_map/ppermute | solution.py:367
  2.6 13.1 %collective-permute-start.2 = (f32[16,128]{1,0:T(8,128)S(1)}, f32[16,128]{1,0:T(8,128)S(1)}, u32[]{:S(2)}, u32[]{:S(2)}) collective-permute-start(f32[16,128]{1,0:T(8,128)S(1)} %get-tuple-element.22.facts_ref), channel_id=1, source_target_pairs={{0,2},{4,6},{8,10},{12,14},{2,0},{6,4},{10,8},{14,12},{1,3},{5,7},... | collective-permute-start | bytes 24584 | tf_op jit(solution)/shard_map/ppermute | solution.py:367
  6.9 9.1 %collective-permute-start.1 = (f32[16,128]{1,0:T(8,128)S(1)}, f32[16,128]{1,0:T(8,128)S(1)}, u32[]{:S(2)}, u32[]{:S(2)}) collective-permute-start(f32[16,128]{1,0:T(8,128)S(1)} %get-tuple-element.22.facts_ref), channel_id=1, source_target_pairs={{16,32},{48,64},{80,96},{32,16},{64,48},{96,80},{17,33},{49,65},{8... | collective-permute-start | bytes 24584 | tf_op jit(solution)/shard_map/ppermute | solution.py:367
  12.4 3.7 %collective-permute-start = (f32[16,128]{1,0:T(8,128)S(1)}, f32[16,128]{1,0:T(8,128)S(1)}, u32[]{:S(2)}, u32[]{:S(2)}) collective-permute-start(f32[16,128]{1,0:T(8,128)S(1)} %get-tuple-element.22.facts_ref), channel_id=1, source_target_pairs={{0,16},{32,48},{64,80},{96,112},{16,0},{48,32},{80,64},{112,96},{1... | collective-permute-start | bytes 24584 | tf_op jit(solution)/shard_map/ppermute | solution.py:367
  16.1 10.0 %copy-start = (bf16[6,1,4,2,128,128]{5,4,3,2,1,0:T(8,128)(2,1)S(1)}, bf16[6,1,4,2,128,128]{5,4,3,2,1,0:T(8,128)(2,1)}, u32[]{:S(2)}) copy-start(bf16[6,1,4,2,128,128]{5,4,3,2,1,0:T(8,128)(2,1)} %param.4) | copy-start | bytes 4718596
  19.5 10.4 %collective-permute-start.5 = (bf16[2,4,128,128]{3,2,1,0:T(8,128)(2,1)S(1)}, bf16[2,4,128,128]{3,2,1,0:T(8,128)(2,1)S(1)}, u32[]{:S(2)}, u32[]{:S(2)}) collective-permute-start(bf16[2,4,128,128]{3,2,1,0:T(8,128)(2,1)S(1)} %get-tuple-element.27), channel_id=1, source_target_pairs={{0,16},{32,48},{64,80},{96,112},{16,0},{48,32},{80,64},{112,96},{1... | collective-permute-start | bytes 786440 | tf_op jit(solution)/shard_map/ppermute | solution.py:367
  21.3 13.3 %collective-permute-start.6 = (bf16[2,4,128,128]{3,2,1,0:T(8,128)(2,1)S(1)}, bf16[2,4,128,128]{3,2,1,0:T(8,128)(2,1)S(1)}, u32[]{:S(2)}, u32[]{:S(2)}) collective-permute-start(bf16[2,4,128,128]{3,2,1,0:T(8,128)(2,1)S(1)} %get-tuple-element.28), channel_id=1, source_target_pairs={{16,32},{48,64},{80,96},{32,16},{64,48},{96,80},{17,33},{49,65},{8... | collective-permute-start | bytes 786440 | tf_op jit(solution)/shard_map/ppermute | solution.py:367
  25.3 9.3 %collective-permute-start.9 = (bf16[2,4,128,128]{3,2,1,0:T(8,128)(2,1)S(1)}, bf16[2,4,128,128]{3,2,1,0:T(8,128)(2,1)S(1)}, u32[]{:S(2)}, u32[]{:S(2)}) collective-permute-start(bf16[2,4,128,128]{3,2,1,0:T(8,128)(2,1)S(1)} %get-tuple-element.31), channel_id=1, source_target_pairs={{0,1},{1,0},{2,3},{3,2},{4,5},{5,4},{6,7},{7,6},{8,9},{9,8},{10,11... | collective-permute-start | bytes 786440 | tf_op jit(solution)/shard_map/ppermute | solution.py:367
  25.4 4.5 %collective-permute-start.7 = (bf16[2,1,128,128]{3,2,1,0:T(8,128)(2,1)S(1)}, bf16[2,1,128,128]{3,2,1,0:T(8,128)(2,1)S(1)}, u32[]{:S(2)}, u32[]{:S(2)}) collective-permute-start(bf16[2,1,128,128]{3,2,1,0:T(8,128)(2,1)S(1)} %get-tuple-element.29), channel_id=1, source_target_pairs={{0,2},{4,6},{8,10},{12,14},{2,0},{6,4},{10,8},{14,12},{1,3},{5,7},... | collective-permute-start | bytes 196616 | tf_op jit(solution)/shard_map/ppermute | solution.py:367
  25.5 4.4 %collective-permute-start.8 = (bf16[2,1,128,128]{3,2,1,0:T(8,128)(2,1)S(1)}, bf16[2,1,128,128]{3,2,1,0:T(8,128)(2,1)S(1)}, u32[]{:S(2)}, u32[]{:S(2)}) collective-permute-start(bf16[2,1,128,128]{3,2,1,0:T(8,128)(2,1)S(1)} %get-tuple-element.30), channel_id=1, source_target_pairs={{2,4},{6,8},{10,12},{4,2},{8,6},{12,10},{3,5},{7,9},{11,13},{5,3},... | collective-permute-start | bytes 196616 | tf_op jit(solution)/shard_map/ppermute | solution.py:367

commit v5 on v4

--- a/solution.py
+++ b/solution.py
@@ -56,22 +56,47 @@
     return jnp.broadcast_to(jnp.sqrt(jnp.sum(rows, axis=1, keepdims=True)), rows.shape)
 
 
-def facts_kernel(split_ref, diag_ref, facts_ref, flags_ref, kept_ref, rows, held, sems):
+def facts_kernel(
+    split_ref, diag_ref, face_ref, facts_ref, flags_ref, kept_ref, xa_ref, xb_ref, rows, held, sems
+):
+    gx = lax.axis_index("gx")
+    first = pltpu.make_async_copy(split_ref, held, sems.at[0])
+    first.start()
     copies = [
-        pltpu.make_async_copy(diag_ref.at[e], kept_ref.at[e], sems.at[e]) for e in range(8)
+        pltpu.make_async_copy(diag_ref.at[e], kept_ref.at[e], sems.at[1 + e]) for e in range(8)
     ]
-    copies.append(pltpu.make_async_copy(split_ref, held, sems.at[8]))
-    for copy in copies[::-1]:
+    for copy in copies:
         copy.start()
-    copies[8].wait()
+    first.wait()
+    for c in range(4):
+        e = 2 * c + jnp.where(held[0, 0, c] == 0, 0, 1)
+        for ref, d in ((xa_ref, 1 - gx % 2), (xb_ref, gx % 2)):
+            for block, place in ((diag_ref.at[e], c), (face_ref.at[d, e], 4 + c)):
+                into = ref.at[pl.ds(B * place, B), :]
+                copies.append(pltpu.make_async_copy(block, into, sems.at[1 + len(copies)]))
+                copies[-1].start()
     for e in range(8):
         part = held[0, e % 2, e // 2]
         flags_ref[pl.ds(e, 1), :] = jnp.full((1, B), part, jnp.int32)
-    facts_ref[pl.ds(8, 8), :] = flags_ref[...].astype(F32)
+    flags = flags_ref[...].astype(F32)
+    facts_ref[pl.ds(8, 8), :] = flags
     for e in range(8):
         copies[e].wait()
         rows[pl.ds(e, 1), :] = square_sums(kept_ref[e])
-    facts_ref[pl.ds(0, 8), :] = norms_of(rows[...])
+    norms = norms_of(rows[...])
+    facts_ref[pl.ds(0, 8), :] = norms
+    parts = [part.astype(F32) for part in thirds(norms)] + [flags]
+    for ref in (xa_ref, xb_ref):
+        for k in range(2):
+            both = jnp.concatenate(parts[2 * k:2 * k + 2], axis=0)
+            ref[pl.ds(8 * B + 16 * k, 16), :] = both.astype(BF16)
+    for copy in copies[8:]:
+        copy.wait()
+
+
+def facts_in(ref):
+    high, low = ref[pl.ds(8 * B, 16), :].astype(F32), ref[pl.ds(8 * B + 16, 16), :].astype(F32)
+    return high[:8] + high[8:] + low[:8], low[8:]
 
 
 def scaling(a, eye):
@@ -83,7 +108,9 @@
     return a, down, along, 1.9 / bound
 
 
-def inverse_kernel(split_ref, diag_ref, face_ref, inv_ref, fnorm_ref, fine_ref, rows, work, sems):
+def inverse_kernel(
+    split_ref, diag_ref, face_ref, solved_ref, fnorm_ref, fine_ref, inv_ref, rows, work, sems
+):
     cols = range(4)
     copies = []
     for c in cols:
@@ -133,6 +160,18 @@
             rows[pl.ds(8 * d + 2 * c, 1), :] = sums
             rows[pl.ds(8 * d + 2 * c + 1, 1), :] = sums
     fnorm_ref[...] = norms_of(rows[...])
+
+    def solve():
+        for c in cols:
+            inv = jnp.concatenate([inv_ref[0, c], inv_ref[1, c]], axis=1)
+            last = inv_ref[2, c]
+            for d in (0, 2, 4):
+                face = jnp.concatenate([fine_ref[d, c], fine_ref[d + 1, c]], axis=1)
+                both = mm(inv, wide(face)) + mm(last, face)
+                solved_ref[d, c] = both[:, :B]
+                solved_ref[d + 1, c] = both[:, B:]
+
+    solve()
     reached = jnp.max(worst) <= 1e-3
 
     @pl.when(jnp.logical_not(reached))
@@ -148,6 +187,7 @@
                 work[1] = x + mm32(x, one - mm32(work[0], x))
 
             inv_ref[0, c], inv_ref[1, c], inv_ref[2, c] = thirds(work[1] * down * along)
+        solve()
 
 
 def shifted(own, beyond, step, edge):
@@ -161,6 +201,8 @@
     depth = row % 2
     even_x, even_y = gx % 2 == 0, gy % 2 == 0
 
+    xa, xb = facts_in(ha), facts_in(hb)
+
     def pick(test, first, second, part):
         rows = pl.ds(8 * part, 8)
         return jnp.where(test, first[rows, :], second[rows, :])
@@ -169,8 +211,8 @@
         own = facts_ref[pl.ds(8 * part, 8), :]
         z = hz[pl.ds(8 * part, 8), :]
         return (
-            pick(even_x, hb, ha, part),
-            pick(even_x, ha, hb, part),
+            jnp.where(even_x, xb[part], xa[part]),
+            jnp.where(even_x, xa[part], xb[part]),
             shifted(own, pick(even_y, hd, hc, part), 2, row < 2),
             shifted(own, pick(even_y, hc, hd, part), 6, row >= 6),
             jnp.where(depth == 0, pltpu.roll(z, 7, 0), pltpu.roll(own, 1, 0)),
@@ -204,74 +246,47 @@
 
 
 def interp_kernel(
-    split_ref, diag_ref, fine_ref, inv_ref, fnorm_ref, facts_ref, ha, hb, hc, hd, hz,
-    interp_ref, code_ref, xa_ref, xb_ref, ya_ref, yb_ref, z_ref, near_ref, inside_ref,
-    weight_ref, edge_ref, zero_ref, sems,
+    split_ref, diag_ref, fine_ref, solved_ref, fnorm_ref, facts_ref, ha, hb, hc, hd, hz,
+    code_ref, xa_ref, xb_ref, ya_ref, yb_ref, z_ref, near_ref, inside_ref, weight_ref,
 ):
-    zero_ref[...] = jnp.zeros((B, B), BF16)
     gx, gy = lax.axis_index("gx"), lax.axis_index("gy")
     fines = [fine_of(split_ref, c) for c in range(4)]
     weights_of(facts_ref, (ha, hb, hc, hd, hz), fnorm_ref, weight_ref)
-    copies = []
-
-    def send(block, d, e):
-        copies.append(pltpu.make_async_copy(block, interp_ref.at[d, e], sems.at[len(copies)]))
-        copies[-1].start()
-
-    def slots(c):
-        return (
-            (1 - gx % 2, xa_ref.at[0, c], xa_ref.at[1, c]),
-            (gx % 2, xb_ref.at[0, c], xb_ref.at[1, c]),
-            (4 + fines[c], z_ref.at[0, c], z_ref.at[1, c]),
-            (2, near_ref.at[0, c], edge_ref.at[0] if c == 0 else None),
-            (3, near_ref.at[1, c], edge_ref.at[1] if c == 3 else None),
-            (5 - fines[c], inside_ref.at[c], None),
-        )
-
-    def send_column(c):
-        for d, interp, _ in slots(c):
-            send(interp, d, 2 * c + fines[c])
-
-    for c in range(4):
-        e = 2 * c + fines[c]
-        inv = jnp.concatenate([inv_ref[0, c], inv_ref[1, c]], axis=1)
-        last = inv_ref[2, c]
-        here = slots(c)
-        for s in (0, 2, 4):
-            two = [here[s], here[s + 1]]
-            face = jnp.concatenate([fine_ref[d, c] for d, _, _ in two], axis=1)
-            weight = jnp.concatenate([weight_ref[d, pl.ds(e, 1), :] for d, _, _ in two], axis=1)
-            interp = (weight * (mm(inv, wide(face)) + mm(last, face))).astype(BF16)
-            two[0][1][...] = interp[:, :B]
-            two[1][1][...] = interp[:, B:]
-        for d in range(6):
-            send(zero_ref, d, 2 * c + 1 - fines[c])
-        if c > 0:
-            send_column(c - 1)
+
+    def weighted(d, c):
+        return (weight_ref[d, pl.ds(2 * c + fines[c], 1), :] * solved_ref[d, c]).astype(BF16)
+
+    for c in range(4):
+        xa_ref[c] = weighted(1 - gx % 2, c)
+        xb_ref[c] = weighted(gx % 2, c)
+        near_ref[0, c] = weighted(2, c)
+        near_ref[1, c] = weighted(3, c)
+        inside_ref[c] = weighted(5 - fines[c], c)
+        z_ref[0, c] = weighted(4 + fines[c], c)
     row = lax.broadcasted_iota(jnp.int32, (8, B), 0)
     lane = lax.broadcasted_iota(jnp.int32, (8, B), 1)
     bit = jnp.where((row % 2 == 0) & (lane == 0), 1, 0) * lax.shift_left(1, row // 2)
     code = jnp.zeros((8, B), F32)
-    for place, ref in enumerate((ha, hb, hc, hd)):
-        code = code + ref[pl.ds(8, 8), :] * (bit * (1 << (4 * place))).astype(F32)
+    splits = (facts_in(ha)[1], facts_in(hb)[1], hc[pl.ds(8, 8), :], hd[pl.ds(8, 8), :])
+    for place, flags in enumerate(splits):
+        code = code + flags * (bit * (1 << (4 * place))).astype(F32)
     code = jnp.sum(jnp.sum(code, axis=0, keepdims=True), axis=1, keepdims=True)
     code_ref[...] = jnp.broadcast_to(code, (8, B)).astype(jnp.int32)
-    for c in range(4):
-        here = [slot for slot in slots(c) if slot[2] is not None]
-        a = diag_ref[2 * c + fines[c]]
-        faces = [fine_ref[d, c] for d, _, _ in here]
-        found = contribs(a, faces, [block[...] for _, block, _ in here])
-        for (_, _, into), contrib in zip(here, found):
-            into[...] = contrib
-        if c == 0:
-            send_column(3)
+    edges = []
+    for c in range(4):
+        here = [(4 + fines[c], z_ref[0, c])]
+        if c in (0, 3):
+            here.append((c // 3 + 2, near_ref[c // 3, c]))
+        found = contribs(
+            diag_ref[2 * c + fines[c]], [fine_ref[d, c] for d, _ in here], [p for _, p in here]
+        )
+        z_ref[1, c] = found[0]
+        edges += found[1:]
     up = gy % 2 == 0
     low, high = near_ref[0, 0], near_ref[1, 3]
     ya_ref[0, 0], yb_ref[0, 0] = jnp.where(up, high, low), jnp.where(up, low, high)
-    low, high = edge_ref[0], edge_ref[1]
+    low, high = edges
     ya_ref[1, 0], yb_ref[1, 0] = jnp.where(up, high, low), jnp.where(up, low, high)
-    for copy in copies:
-        copy.wait()
 
 
 def contribs(a, faces, interps):
@@ -289,8 +304,30 @@
     return found
 
 
-def near_kernel(split_ref, diag_ref, face_ref, fine_ref, near_ref, inside_ref, sum_ref):
+def near_kernel(
+    split_ref, diag_ref, face_ref, fine_ref, near_ref, inside_ref, xa_ref, xb_ref, z_ref,
+    sum_ref, interp_ref, zero_ref, sems,
+):
+    gx = lax.axis_index("gx")
     fines = [fine_of(split_ref, c) for c in range(4)]
+    copies = []
+
+    def send(block, d, e):
+        copies.append(pltpu.make_async_copy(block, interp_ref.at[d, e], sems.at[len(copies)]))
+        copies[-1].start()
+
+    zero_ref[...] = jnp.zeros((B, B), BF16)
+    for c in range(4):
+        e = 2 * c + fines[c]
+        send(xa_ref.at[c], 1 - gx % 2, e)
+        send(xb_ref.at[c], gx % 2, e)
+        send(near_ref.at[0, c], 2, e)
+        send(near_ref.at[1, c], 3, e)
+        send(inside_ref.at[c], 5 - fines[c], e)
+        send(z_ref.at[0, c], 4 + fines[c], e)
+    for c in range(4):
+        for d in range(6):
+            send(zero_ref, d, 2 * c + 1 - fines[c])
     parts = [[] for _ in range(4)]
     for c in range(4):
         z = fines[c]
@@ -311,10 +348,12 @@
             for z, part in parts[c]:
                 total = total + jnp.where(z == k, part, 0.0)
             sum_ref[2 * c + k] = total
+    for copy in copies:
+        copy.wait()
 
 
 def coarse_kernel(
-    split_ref, code_ref, sum_ref, face_ref, xa_ref, xb_ref, ya_ref, yb_ref, z_ref,
+    split_ref, code_ref, sum_ref, face_ref, ha, hb, xa_ref, xb_ref, ya_ref, yb_ref, z_ref,
     coarse_ref, total_ref, sems,
 ):
     gx, gy, gz = lax.axis_index("gx"), lax.axis_index("gy"), lax.axis_index("gz")
@@ -326,26 +365,23 @@
 
     copies = []
     for c in (1, 2, 0, 3):
-        arrived = [
-            (bit_at(c), 1 - gx % 2, xa_ref.at[0, c], xa_ref.at[1, c]),
-            (bit_at(4 + c), gx % 2, xb_ref.at[0, c], xb_ref.at[1, c]),
-            (1 - gz, 5 - gz, z_ref.at[0, c], z_ref.at[1, c]),
-        ]
-        extra = None
+        arrived = [(1 - gz, 5 - gz, z_ref[0, c], z_ref[1, c])]
+        for z, d, sent, ref in (
+            (bit_at(c), 1 - gx % 2, ha, xa_ref), (bit_at(4 + c), gx % 2, hb, xb_ref)
+        ):
+            theirs, face = sent[pl.ds(B * c, B), :], sent[pl.ds(B * (4 + c), B), :]
+            arrived.append((z, d, ref[c], contribs(theirs, [face], [ref[c]])[0]))
         if c in (0, 3):
             first = up if c == 3 else jnp.logical_not(up)
             edge = 0 if c == 3 else 3
             z = jnp.where(first, bit_at(8 + edge), bit_at(12 + edge))
             pair = [jnp.where(first, ya_ref[k, 0], yb_ref[k, 0]) for k in range(2)]
-            extra = (z, 3 if c == 3 else 2, pair)
+            arrived.append((z, 3 if c == 3 else 2, *pair))
         totals = [sum_ref[2 * c], sum_ref[2 * c + 1]]
         parts = [
-            (z, contrib[...].astype(F32) + mm(face_ref[d, 2 * c + z], interp[...]))
+            (z, contrib.astype(F32) + mm(face_ref[d, 2 * c + z], interp))
             for z, d, interp, contrib in arrived
         ]
-        if extra:
-            z, d, (interp, contrib) = extra
-            parts.append((z, contrib.astype(F32) + mm(face_ref[d, 2 * c + z], interp)))
         for k in range(2):
             e = 2 * c + k
             keep = split_at(split_ref, c, k) == 1
@@ -387,45 +423,44 @@
     dma = pltpu.SemaphoreType.DMA
     in_hbm = lambda x: pltpu.with_memory_space_constraint(x, pltpu.HBM)
     blocks = lambda *lead: sds(lead + (B, B), BF16)
-    facts, flags, diag = call(
-        facts_kernel, (sds((16, B), F32), sds((8, B), jnp.int32), blocks(8)),
-        [HBM, HBM], (VMEM, VMEM, VMEM),
-        [pltpu.VMEM((8, B), F32), pltpu.SMEM((1, 2, 4), jnp.int32), dma((9,))], 1 << 20,
-    )(in_hbm(split), in_hbm(diag))
-    halo = (
-        swap(facts, "gx", 0), swap(facts, "gx", 1),
-        swap(facts, "gy", 0), swap(facts, "gy", 1),
-        swap(facts, "gz", 0),
-    )
-    inv, fnorm, fine = call(
-        inverse_kernel, (blocks(3, 4), sds((48, B), F32), blocks(6, 4)),
+    packed = sds((8 * B + 32, B), BF16)
+    facts, flags, diag, pa, pb = call(
+        facts_kernel,
+        (sds((16, B), F32), sds((8, B), jnp.int32), blocks(8), packed, packed),
+        [HBM] * 3, (VMEM,) * 5,
+        [pltpu.VMEM((8, B), F32), pltpu.SMEM((1, 2, 4), jnp.int32), dma((25,))], 1 << 20,
+    )(in_hbm(split), in_hbm(diag), in_hbm(face))
+    ha, hb = swap(pa, "gx", 0), swap(pb, "gx", 1)
+    hc, hd = swap(facts, "gy", 0), swap(facts, "gy", 1)
+    hz = swap(facts, "gz", 0)
+    solved, fnorm, fine = call(
+        inverse_kernel, (sds((6, 4, B, B), F32), sds((48, B), F32), blocks(6, 4)),
         [SMEM, VMEM, HBM], (VMEM, VMEM, VMEM),
-        [pltpu.VMEM((48, B), F32), pltpu.VMEM((2, B, B), F32), dma((24,))], 1 << 30,
+        [
+            pltpu.VMEM((3, 4, B, B), BF16), pltpu.VMEM((48, B), F32), pltpu.VMEM((2, B, B), F32),
+            dma((24,)),
+        ],
+        1 << 30,
     )(flags, diag, in_hbm(face))
-    interp, code, xa, xb, ya, yb, z, near, inside = call(
+    code, xa, xb, ya, yb, z, near, inside = call(
         interp_kernel,
         (
-            blocks(6, 8), sds((8, B), jnp.int32), blocks(2, 4), blocks(2, 4), blocks(2, 1),
+            sds((8, B), jnp.int32), blocks(4), blocks(4), blocks(2, 1),
             blocks(2, 1), blocks(2, 4), blocks(2, 4), blocks(4),
         ),
-        [SMEM] + [VMEM] * 10,
-        (HBM,) + (VMEM,) * 8,
-        [
-            pltpu.VMEM((6, 8, B), F32), pltpu.VMEM((2, B, B), BF16),
-            pltpu.VMEM((B, B), BF16), dma((48,)),
-        ],
-        1 << 30,
-    )(flags, diag, fine, inv, fnorm, facts, *halo)
-    xa, xb = swap(xa, "gx", 0), swap(xb, "gx", 1)
+        [SMEM] + [VMEM] * 10, (VMEM,) * 8, [pltpu.VMEM((6, 8, B), F32)], 1 << 30,
+    )(flags, diag, fine, solved, fnorm, facts, ha, hb, hc, hd, hz)
+    sa, sb = swap(xa, "gx", 0), swap(xb, "gx", 1)
     ya, yb = swap(ya, "gy", 0), swap(yb, "gy", 1)
-    z = swap(z, "gz", 0)
-    total = call(
-        near_kernel, sds((8, B, B), F32), [SMEM] + [VMEM] * 5, VMEM, [], 1 << 30,
-    )(flags, diag, face, fine, near, inside)
+    sz = swap(z, "gz", 0)
+    total, interp = call(
+        near_kernel, (sds((8, B, B), F32), blocks(6, 8)), [SMEM] + [VMEM] * 8, (VMEM, HBM),
+        [pltpu.VMEM((B, B), BF16), dma((48,))], 1 << 30,
+    )(flags, diag, face, fine, near, inside, xa, xb, z)
     coarse = call(
-        coarse_kernel, sds((8, B, B), F32), [SMEM, SMEM] + [VMEM] * 7, HBM,
+        coarse_kernel, sds((8, B, B), F32), [SMEM, SMEM] + [VMEM] * 9, HBM,
         [pltpu.VMEM((8, B, B), F32), dma((8,))], 1 << 30,
-    )(flags, code, total, face, xa, xb, ya, yb, z)
+    )(flags, code, total, face, ha, hb, sa, sb, ya, yb, sz)
     return interp.reshape(face_blocks.shape), coarse.reshape(diag_blocks.shape)
 
 

time: 36.7 us -> 36.2 us (0.986)
  the two profiles are of different devices: /device:TPU:24 before, /device:TPU:10 now
where the time goes in v5:
time: 36.2 us; the launch traced here: 35.8 us
  starting transfers between devices  19.8 us (55%)
  Pallas kernels  12.5 us (35%)
  waiting for transfers between devices  2.76 us (8%)
  between operations  0.76 us (2%)
    ppermute x10, starting transfers between devices, swap(): return lax.ppermute(x, axis, matching(lax.axis_size(axis), start))  19.8 us
    pallas_call x1, Pallas kernels, on_device(): call(inverse_kernel, (sds((6, 4, B, B), F32), sds((48, B), F32), blocks(6...  3.67 us
    pallas_call x1, Pallas kernels, on_device(): call(near_kernel, (sds((8, B, B), F32), blocks(6, 8)), [SMEM] + [VMEM] *...  3.03 us
    ppermute x10, waiting for transfers between devices, swap(): return lax.ppermute(x, axis, matching(lax.axis_size(axis), start))  2.76 us
    pallas_call x1, Pallas kernels, on_device(): call(coarse_kernel, sds((8, B, B), F32), [SMEM, SMEM] + [VMEM] * 9, HBM,...  2.47 us
    pallas_call x1, Pallas kernels, on_device(): call(facts_kernel, (sds((16, B), F32), sds((8, B), jnp.int32), blocks(8),...  1.9 us
    pallas_call x1, Pallas kernels, on_device(): call(interp_kernel, (sds((8, B), jnp.int32), blocks(4), blocks(4), blocks...  1.4 us
  transfers between devices with their start and end apart: 10, of which 2 were waited for; matrix products, arithmetic and copies ran while one was open for 0% of the time, Pallas kernels for 19%

profile of v5, /device:TPU:10, one launch (start us, length us, event | category | flops | bytes accessed | tf_op | source)
XLA Modules:
  0.0 35.8 jit_solution(5988109402923470509)
XLA Ops:
  0.6 1.9 %shard_map.50 = (f32[16,128]{1,0:T(8,128)S(1)}, s32[8,128]{1,0:T(8,128)S(1)}, bf16[8,128,128]{2,1,0:T(8,128)(2,1)S(1)}, bf16[1056,128]{1,0:T(8,128)(2,1)S(1)}, bf16[1056,128]{1,0:T(8,128)(2,1)S(1)}) custom-call(s32[1,2,4]{2,1,0:T(2,128)} %bitcast.12, bf16[8,128,128]{2,1,0:T(8,128)(2,1)} %bitcast.11, bf16[6,8,128,128]{3,2,1,0:T(8,128)(2,1)} %bitcast.7), custom_call_target="tpu_custom_call" | custom-call | flops 1048576 | bytes 2097152 | tf_op jit(solution)/shard_map/pallas_call | solution.py:427
  2.5 0.5 %collective-permute-start = (bf16[1056,128]{1,0:T(8,128)(2,1)S(1)}, bf16[1056,128]{1,0:T(8,128)(2,1)S(1)}, u32[]{:S(2)}, u32[]{:S(2)}) collective-permute-start(bf16[1056,128]{1,0:T(8,128)(2,1)S(1)} %get-tuple-element.26), channel_id=1, source_target_pairs={{0,16},{32,48},{64,80},{96,112},{16,0},{48,32},{80,64},{112,96},{1... | collective-permute-start | bytes 811016 | tf_op jit(solution)/shard_map/ppermute | solution.py:403
  3.1 4.3 %collective-permute-start.1 = (bf16[1056,128]{1,0:T(8,128)(2,1)S(1)}, bf16[1056,128]{1,0:T(8,128)(2,1)S(1)}, u32[]{:S(2)}, u32[]{:S(2)}) collective-permute-start(bf16[1056,128]{1,0:T(8,128)(2,1)S(1)} %get-tuple-element.27), channel_id=1, source_target_pairs={{16,32},{48,64},{80,96},{32,16},{64,48},{96,80},{17,33},{49,65},{8... | collective-permute-start | bytes 811016 | tf_op jit(solution)/shard_map/ppermute | solution.py:403
  7.4 2.0 %collective-permute-start.2 = (f32[16,128]{1,0:T(8,128)S(1)}, f32[16,128]{1,0:T(8,128)S(1)}, u32[]{:S(2)}, u32[]{:S(2)}) collective-permute-start(f32[16,128]{1,0:T(8,128)S(1)} %get-tuple-element.25.facts_ref), channel_id=1, source_target_pairs={{0,2},{4,6},{8,10},{12,14},{2,0},{6,4},{10,8},{14,12},{1,3},{5,7},... | collective-permute-start | bytes 24584 | tf_op jit(solution)/shard_map/ppermute | solution.py:403
  9.4 2.0 %collective-permute-start.3 = (f32[16,128]{1,0:T(8,128)S(1)}, f32[16,128]{1,0:T(8,128)S(1)}, u32[]{:S(2)}, u32[]{:S(2)}) collective-permute-start(f32[16,128]{1,0:T(8,128)S(1)} %get-tuple-element.25.facts_ref), channel_id=1, source_target_pairs={{2,4},{6,8},{10,12},{4,2},{8,6},{12,10},{3,5},{7,9},{11,13},{5,3},... | collective-permute-start | bytes 24584 | tf_op jit(solution)/shard_map/ppermute | solution.py:403
  11.4 0.1 collective-permute-start.4
  11.5 3.7 %shard_map.51 = (f32[6,4,128,128]{3,2,1,0:T(8,128)S(1)}, f32[48,128]{1,0:T(8,128)S(1)}, bf16[6,4,128,128]{3,2,1,0:T(8,128)(2,1)S(1)}) custom-call(s32[8,128]{1,0:T(8,128)S(1)} %get-tuple-element.20.split_ref, bf16[8,128,128]{2,1,0:T(8,128)(2,1)S(1)} %get-tuple-element.21.diag_ref, bf16[6,8,128,128]{3,2,1,0:T(8,128)(2,1)} %bitcast.8), custom_call_target="tpu_custom_call" | custom-call | flops 1073741824 | bytes 2097152 | tf_op jit(solution)/shard_map/pallas_call | solution.py:436
  15.1 0.0 collective-permute-done.2.hc
  15.1 0.7 %collective-permute-done.3.hd = f32[16,128]{1,0:T(8,128)S(1)} collective-permute-done((f32[16,128]{1,0:T(8,128)S(1)}, f32[16,128]{1,0:T(8,128)S(1)}, u32[]{:S(2)}, u32[]{:S(2)}) %collective-permute-start.3) | collective-permute-done | bytes 8224 | tf_op jit(solution)/shard_map/ppermute | solution.py:403
  15.8 0.0 collective-permute-done.4.hz
  15.8 0.0 collective-permute-done.ha
  15.8 0.0 collective-permute-done.1.hb
  15.8 0.0 copy-start
  15.8 1.4 %shard_map.52 = (s32[8,128]{1,0:T(8,128)S(1)}, bf16[4,128,128]{2,1,0:T(8,128)(2,1)S(1)}, bf16[4,128,128]{2,1,0:T(8,128)(2,1)S(1)}, bf16[2,1,128,128]{3,2,1,0:T(8...) custom-call(s32[8,128]{1,0:T(8,128)S(1)} %get-tuple-element.20.split, ...), custom_call_target="tpu_custom_call" | custom-call | flops 1073741824 | bytes 2097152 | tf_op jit(solution)/shard_map/pallas_call | solution.py:445
  17.2 0.1 collective-permute-start.9
  17.3 0.1 collective-permute-start.5
  17.4 6.8 %collective-permute-start.6 = (bf16[4,128,128]{2,1,0:T(8,128)(2,1)S(1)}, bf16[4,128,128]{2,1,0:T(8,128)(2,1)S(1)}, u32[]{:S(2)}, u32[]{:S(2)}) collective-permute-start(bf16[4,128,128]{2,1,0:T(8,128)(2,1)S(1)} %get-tuple-element.31.xb_ref), channel_id=1, source_target_pairs={{16,32},{48,64},{80,96},{32,16},{64,48},{96,80},{17,33},{49,65},{8... | collective-permute-start | bytes 393224 | tf_op jit(solution)/shard_map/ppermute | solution.py:403
  24.2 2.1 %collective-permute-start.7 = (bf16[2,1,128,128]{3,2,1,0:T(8,128)(2,1)S(1)}, bf16[2,1,128,128]{3,2,1,0:T(8,128)(2,1)S(1)}, u32[]{:S(2)}, u32[]{:S(2)}) collective-permute-start(bf16[2,1,128,128]{3,2,1,0:T(8,128)(2,1)S(1)} %get-tuple-element.36), channel_id=1, source_target_pairs={{0,2},{4,6},{8,10},{12,14},{2,0},{6,4},{10,8},{14,12},{1,3},{5,7},... | collective-permute-start | bytes 196616 | tf_op jit(solution)/shard_map/ppermute | solution.py:403
  26.3 1.9 %collective-permute-start.8 = (bf16[2,1,128,128]{3,2,1,0:T(8,128)(2,1)S(1)}, bf16[2,1,128,128]{3,2,1,0:T(8,128)(2,1)S(1)}, u32[]{:S(2)}, u32[]{:S(2)}) collective-permute-start(bf16[2,1,128,128]{3,2,1,0:T(8,128)(2,1)S(1)} %get-tuple-element.37), channel_id=1, source_target_pairs={{2,4},{6,8},{10,12},{4,2},{8,6},{12,10},{3,5},{7,9},{11,13},{5,3},... | collective-permute-start | bytes 196616 | tf_op jit(solution)/shard_map/ppermute | solution.py:403
  28.2 0.0 copy-done
  28.2 3.0 %shard_map.53 = (f32[8,128,128]{2,1,0:T(8,128)S(1)}, bf16[6,8,128,128]{3,2,1,0:T(8,128)(2,1)}) custom-call(s32[8,128]{1,0:T(8,128)S(1)} %get-tuple-element.20.split_ref, bf16[8,128,128]{2,1,0:T(8,128)(2,1)S(1)} %get-tuple-element.21.diag_ref, bf16[6,8,128,128]{3,2,1,0:T(8,128)(2,1)S(1)} %bitcast.9, bf16[6,4,128,128]{3,2,1,0:T(8,128)(2,1)S(1)} %get-tuple-element.22.fine_ref, ...), custom_call_target="tpu_custom_call" | custom-call | flops 1073741824 | bytes 2097152 | tf_op jit(solution)/shard_map/pallas_call | solution.py:456
  31.2 0.0 collective-permute-done.7.ya_ref
  31.3 2.1 %collective-permute-done.8.yb_ref = bf16[2,1,128,128]{3,2,1,0:T(8,128)(2,1)S(1)} collective-permute-done((bf16[2,1,128,128]{3,2,1,0:T(8,128)(2,1)S(1)}, bf16[2,1,128,128]{3,2,1,0:T(8,128)(2,1)S(1)}, u32[]{:S(2)}, u32[]{:S(2)}) %collective-permute-start.8) | collective-permute-done | bytes 65568 | tf_op jit(solution)/shard_map/ppermute | solution.py:403
  33.3 0.0 collective-permute-done.5.xa_ref
  33.3 0.0 collective-permute-done.6.xb_ref
  33.3 0.0 collective-permute-done.9.z_ref
  33.3 2.5 %shard_map.54 = f32[8,128,128]{2,1,0:T(8,128)} custom-call(s32[8,128]{1,0:T(8,128)S(1)} %get-tuple-element.20.split_ref, s32[8,128]{1,0:T(8,128)S(1)} %get-tuple-element.34.code_ref, f32[8,128,128]{2,1,0:T(8,128)S(1)} %get-tuple-element.35.sum_ref, bf16[6,8,128,128]{3,2,1,0:T(8,128)(2,1)S(1)} %bitcast.10, bf16[1056,128]{1,0:T(8,128)(2,1)S(1)} %collective-permute-done.ha, ...), custom_call_target="tpu_custom_call" | custom-call | flops 1073741824 | bytes 2097152 | tf_op jit(solution)/shard_map/pallas_call | solution.py:460
Async XLA Ops:
  2.5 13.3 %collective-permute-start = (bf16[1056,128]{1,0:T(8,128)(2,1)S(1)}, bf16[1056,128]{1,0:T(8,128)(2,1)S(1)}, u32[]{:S(2)}, u32[]{:S(2)}) collective-permute-start(bf16[1056,128]{1,0:T(8,128)(2,1)S(1)} %get-tuple-element.26), channel_id=1, source_target_pairs={{0,16},{32,48},{64,80},{96,112},{16,0},{48,32},{80,64},{112,96},{1... | collective-permute-start | bytes 811016 | tf_op jit(solution)/shard_map/ppermute | solution.py:403
  3.1 12.8 %collective-permute-start.1 = (bf16[1056,128]{1,0:T(8,128)(2,1)S(1)}, bf16[1056,128]{1,0:T(8,128)(2,1)S(1)}, u32[]{:S(2)}, u32[]{:S(2)}) collective-permute-start(bf16[1056,128]{1,0:T(8,128)(2,1)S(1)} %get-tuple-element.27), channel_id=1, source_target_pairs={{16,32},{48,64},{80,96},{32,16},{64,48},{96,80},{17,33},{49,65},{8... | collective-permute-start | bytes 811016 | tf_op jit(solution)/shard_map/ppermute | solution.py:403
  7.4 7.8 %collective-permute-start.2 = (f32[16,128]{1,0:T(8,128)S(1)}, f32[16,128]{1,0:T(8,128)S(1)}, u32[]{:S(2)}, u32[]{:S(2)}) collective-permute-start(f32[16,128]{1,0:T(8,128)S(1)} %get-tuple-element.25.facts_ref), channel_id=1, source_target_pairs={{0,2},{4,6},{8,10},{12,14},{2,0},{6,4},{10,8},{14,12},{1,3},{5,7},... | collective-permute-start | bytes 24584 | tf_op jit(solution)/shard_map/ppermute | solution.py:403
  9.4 6.4 %collective-permute-start.3 = (f32[16,128]{1,0:T(8,128)S(1)}, f32[16,128]{1,0:T(8,128)S(1)}, u32[]{:S(2)}, u32[]{:S(2)}) collective-permute-start(f32[16,128]{1,0:T(8,128)S(1)} %get-tuple-element.25.facts_ref), channel_id=1, source_target_pairs={{2,4},{6,8},{10,12},{4,2},{8,6},{12,10},{3,5},{7,9},{11,13},{5,3},... | collective-permute-start | bytes 24584 | tf_op jit(solution)/shard_map/ppermute | solution.py:403
  11.4 4.5 %collective-permute-start.4 = (f32[16,128]{1,0:T(8,128)S(1)}, f32[16,128]{1,0:T(8,128)S(1)}, u32[]{:S(2)}, u32[]{:S(2)}) collective-permute-start(f32[16,128]{1,0:T(8,128)S(1)} %get-tuple-element.25.facts_ref), channel_id=1, source_target_pairs={{0,1},{1,0},{2,3},{3,2},{4,5},{5,4},{6,7},{7,6},{8,9},{9,8},{10,11... | collective-permute-start | bytes 24584 | tf_op jit(solution)/shard_map/ppermute | solution.py:403
  15.8 12.4 %copy-start = (bf16[6,1,4,2,128,128]{5,4,3,2,1,0:T(8,128)(2,1)S(1)}, bf16[6,1,4,2,128,128]{5,4,3,2,1,0:T(8,128)(2,1)}, u32[]{:S(2)}) copy-start(bf16[6,1,4,2,128,128]{5,4,3,2,1,0:T(8,128)(2,1)} %param.4) | copy-start | bytes 4718596
  17.2 16.1 %collective-permute-start.9 = (bf16[2,4,128,128]{3,2,1,0:T(8,128)(2,1)S(1)}, bf16[2,4,128,128]{3,2,1,0:T(8,128)(2,1)S(1)}, u32[]{:S(2)}, u32[]{:S(2)}) collective-permute-start(bf16[2,4,128,128]{3,2,1,0:T(8,128)(2,1)S(1)} %get-tuple-element.32.z_ref), channel_id=1, source_target_pairs={{0,1},{1,0},{2,3},{3,2},{4,5},{5,4},{6,7},{7,6},{8,9},{9,8},{10,11... | collective-permute-start | bytes 786440 | tf_op jit(solution)/shard_map/ppermute | solution.py:403
  17.3 16.0 %collective-permute-start.5 = (bf16[4,128,128]{2,1,0:T(8,128)(2,1)S(1)}, bf16[4,128,128]{2,1,0:T(8,128)(2,1)S(1)}, u32[]{:S(2)}, u32[]{:S(2)}) collective-permute-start(bf16[4,128,128]{2,1,0:T(8,128)(2,1)S(1)} %get-tuple-element.30.xa_ref), channel_id=1, source_target_pairs={{0,16},{32,48},{64,80},{96,112},{16,0},{48,32},{80,64},{112,96},{1... | collective-permute-start | bytes 393224 | tf_op jit(solution)/shard_map/ppermute | solution.py:403
  17.4 15.9 %collective-permute-start.6 = (bf16[4,128,128]{2,1,0:T(8,128)(2,1)S(1)}, bf16[4,128,128]{2,1,0:T(8,128)(2,1)S(1)}, u32[]{:S(2)}, u32[]{:S(2)}) collective-permute-start(bf16[4,128,128]{2,1,0:T(8,128)(2,1)S(1)} %get-tuple-element.31.xb_ref), channel_id=1, source_target_pairs={{16,32},{48,64},{80,96},{32,16},{64,48},{96,80},{17,33},{49,65},{8... | collective-permute-start | bytes 393224 | tf_op jit(solution)/shard_map/ppermute | solution.py:403
  24.2 7.0 %collective-permute-start.7 = (bf16[2,1,128,128]{3,2,1,0:T(8,128)(2,1)S(1)}, bf16[2,1,128,128]{3,2,1,0:T(8,128)(2,1)S(1)}, u32[]{:S(2)}, u32[]{:S(2)}) collective-permute-start(bf16[2,1,128,128]{3,2,1,0:T(8,128)(2,1)S(1)} %get-tuple-element.36), channel_id=1, source_target_pairs={{0,2},{4,6},{8,10},{12,14},{2,0},{6,4},{10,8},{14,12},{1,3},{5,7},... | collective-permute-start | bytes 196616 | tf_op jit(solution)/shard_map/ppermute | solution.py:403
  26.3 7.0 %collective-permute-start.8 = (bf16[2,1,128,128]{3,2,1,0:T(8,128)(2,1)S(1)}, bf16[2,1,128,128]{3,2,1,0:T(8,128)(2,1)S(1)}, u32[]{:S(2)}, u32[]{:S(2)}) collective-permute-start(bf16[2,1,128,128]{3,2,1,0:T(8,128)(2,1)S(1)} %get-tuple-element.37), channel_id=1, source_target_pairs={{2,4},{6,8},{10,12},{4,2},{8,6},{12,10},{3,5},{7,9},{11,13},{5,3},... | collective-permute-start | bytes 196616 | tf_op jit(solution)/shard_map/ppermute | solution.py:403

commit v6 on v5

--- a/solution.py
+++ b/solution.py
@@ -10,7 +10,6 @@
 F32 = jnp.float32
 BF16 = jnp.bfloat16
 VMEM = pl.BlockSpec(memory_space=pltpu.VMEM)
-SMEM = pl.BlockSpec(memory_space=pltpu.SMEM)
 HBM = pl.BlockSpec(memory_space=pltpu.HBM)
 LIMIT = 24 * 1024 * 1024
 
@@ -39,12 +38,12 @@
     return jnp.concatenate([x, x], axis=0)
 
 
-def split_at(split_ref, c, z):
-    return split_ref[2 * c + z, 0]
-
-
-def fine_of(split_ref, c):
-    return jnp.where(split_at(split_ref, c, 0) == 0, 0, 1)
+def split_at(flags, c, z):
+    return lax.shift_right_logical(flags, 2 * c + z) & 1
+
+
+def fine_of(flags, c):
+    return split_at(flags, c, 0)
 
 
 def square_sums(x):
@@ -57,41 +56,43 @@
 
 
 def facts_kernel(
-    split_ref, diag_ref, face_ref, facts_ref, flags_ref, kept_ref, xa_ref, xb_ref, rows, held, sems
+    split_ref, diag_ref, face_ref, facts_ref, flags_ref, kept_ref, xa_ref, xb_ref, rows, held, faces, sems
 ):
     gx = lax.axis_index("gx")
-    first = pltpu.make_async_copy(split_ref, held, sems.at[0])
-    first.start()
     copies = [
-        pltpu.make_async_copy(diag_ref.at[e], kept_ref.at[e], sems.at[1 + e]) for e in range(8)
+        pltpu.make_async_copy(split_ref, held, sems.at[0]),
+        pltpu.make_async_copy(diag_ref, kept_ref, sems.at[1]),
+        pltpu.make_async_copy(face_ref.at[pl.ds(0, 2)], faces, sems.at[2]),
     ]
     for copy in copies:
         copy.start()
-    first.wait()
-    for c in range(4):
-        e = 2 * c + jnp.where(held[0, 0, c] == 0, 0, 1)
-        for ref, d in ((xa_ref, 1 - gx % 2), (xb_ref, gx % 2)):
-            for block, place in ((diag_ref.at[e], c), (face_ref.at[d, e], 4 + c)):
-                into = ref.at[pl.ds(B * place, B), :]
-                copies.append(pltpu.make_async_copy(block, into, sems.at[1 + len(copies)]))
-                copies[-1].start()
+    copies[0].wait()
+    row = lax.broadcasted_iota(jnp.int32, (8, B), 0)
+    splits = [held[0, e % 2, e // 2] for e in range(8)]
+    flags = jnp.zeros((8, B), F32)
+    code = 0
+    for e, split in enumerate(splits):
+        flags = jnp.where(row == e, split.astype(F32), flags)
+        code = code + split * (1 << e)
+    flags_ref[...] = jnp.full((8, B), code, jnp.int32)
+    facts_ref[pl.ds(8, 8), :] = flags
+    copies[1].wait()
     for e in range(8):
-        part = held[0, e % 2, e // 2]
-        flags_ref[pl.ds(e, 1), :] = jnp.full((1, B), part, jnp.int32)
-    flags = flags_ref[...].astype(F32)
-    facts_ref[pl.ds(8, 8), :] = flags
-    for e in range(8):
-        copies[e].wait()
         rows[pl.ds(e, 1), :] = square_sums(kept_ref[e])
     norms = norms_of(rows[...])
     facts_ref[pl.ds(0, 8), :] = norms
+    copies[2].wait()
+    for c in range(4):
+        e = 2 * c + splits[2 * c]
+        block = kept_ref[e]
+        for ref, d in ((xa_ref, 1 - gx % 2), (xb_ref, gx % 2)):
+            ref[pl.ds(B * c, B), :] = block
+            ref[pl.ds(B * (4 + c), B), :] = faces[d, e]
     parts = [part.astype(F32) for part in thirds(norms)] + [flags]
     for ref in (xa_ref, xb_ref):
         for k in range(2):
             both = jnp.concatenate(parts[2 * k:2 * k + 2], axis=0)
             ref[pl.ds(8 * B + 16 * k, 16), :] = both.astype(BF16)
-    for copy in copies[8:]:
-        copy.wait()
 
 
 def facts_in(ref):
@@ -112,19 +113,17 @@
     split_ref, diag_ref, face_ref, solved_ref, fnorm_ref, fine_ref, inv_ref, rows, work, sems
 ):
     cols = range(4)
+    flags = split_ref[...][0, 0]
     copies = []
     for c in cols:
-        e = 2 * c + fine_of(split_ref, c)
-        for d in range(6):
-            copies.append(
-                pltpu.make_async_copy(face_ref.at[d, e], fine_ref.at[d, c], sems.at[6 * c + d])
-            )
-            copies[-1].start()
+        e = 2 * c + fine_of(flags, c)
+        copies.append(pltpu.make_async_copy(face_ref.at[:, e], fine_ref.at[:, c], sems.at[c]))
+        copies[-1].start()
     eye = (
         lax.broadcasted_iota(jnp.int32, (B, B), 0) == lax.broadcasted_iota(jnp.int32, (B, B), 1)
     )
     one = jnp.where(eye, 1.0, 0.0).astype(F32)
-    mats = [diag_ref[2 * c + fine_of(split_ref, c)] for c in cols]
+    mats = [diag_ref[2 * c + fine_of(flags, c)] for c in cols]
     parts = [scaling(m.astype(F32), eye) for m in mats]
     powers = [one - start * a for a, _, _, start in parts]
     sums = [one + p for p in powers]
@@ -151,9 +150,8 @@
         fixed = (hi.astype(F32) + lo.astype(F32)) + (mm(hi, rhi) + (mm(hi, rlo) + mm(lo, rhi)))
         inv_ref[0, c], inv_ref[1, c], inv_ref[2, c] = thirds(fixed)
         worst = worst + jnp.sum(jnp.abs(left[c]), axis=0, keepdims=True)
-    for c in cols:
-        for d in range(6):
-            copies[6 * c + d].wait()
+    for copy in copies:
+        copy.wait()
     for d in range(6):
         for c in cols:
             sums = square_sums(fine_ref[d, c])
@@ -247,43 +245,43 @@
 
 def interp_kernel(
     split_ref, diag_ref, fine_ref, solved_ref, fnorm_ref, facts_ref, ha, hb, hc, hd, hz,
-    code_ref, xa_ref, xb_ref, ya_ref, yb_ref, z_ref, near_ref, inside_ref, weight_ref,
+    code_ref, xa_ref, xb_ref, ya_ref, yb_ref, z_ref, all_ref, weight_ref,
 ):
     gx, gy = lax.axis_index("gx"), lax.axis_index("gy")
-    fines = [fine_of(split_ref, c) for c in range(4)]
+    flags = split_ref[...][0, 0]
+    fines = [fine_of(flags, c) for c in range(4)]
     weights_of(facts_ref, (ha, hb, hc, hd, hz), fnorm_ref, weight_ref)
 
-    def weighted(d, c):
-        return (weight_ref[d, pl.ds(2 * c + fines[c], 1), :] * solved_ref[d, c]).astype(BF16)
-
-    for c in range(4):
-        xa_ref[c] = weighted(1 - gx % 2, c)
-        xb_ref[c] = weighted(gx % 2, c)
-        near_ref[0, c] = weighted(2, c)
-        near_ref[1, c] = weighted(3, c)
-        inside_ref[c] = weighted(5 - fines[c], c)
-        z_ref[0, c] = weighted(4 + fines[c], c)
+    even_x = gx % 2 == 0
+    for c in range(4):
+        for d in range(6):
+            weight = weight_ref[d, pl.ds(2 * c + fines[c], 1), :]
+            all_ref[d, c] = (weight * solved_ref[d, c]).astype(BF16)
+        low, high = all_ref[0, c], all_ref[1, c]
+        xa_ref[c] = jnp.where(even_x, high, low)
+        xb_ref[c] = jnp.where(even_x, low, high)
+        z_ref[0, c] = all_ref[4 + fines[c], c]
     row = lax.broadcasted_iota(jnp.int32, (8, B), 0)
     lane = lax.broadcasted_iota(jnp.int32, (8, B), 1)
     bit = jnp.where((row % 2 == 0) & (lane == 0), 1, 0) * lax.shift_left(1, row // 2)
     code = jnp.zeros((8, B), F32)
     splits = (facts_in(ha)[1], facts_in(hb)[1], hc[pl.ds(8, 8), :], hd[pl.ds(8, 8), :])
-    for place, flags in enumerate(splits):
-        code = code + flags * (bit * (1 << (4 * place))).astype(F32)
+    for place, theirs in enumerate(splits):
+        code = code + theirs * (bit * (1 << (4 * place))).astype(F32)
     code = jnp.sum(jnp.sum(code, axis=0, keepdims=True), axis=1, keepdims=True)
     code_ref[...] = jnp.broadcast_to(code, (8, B)).astype(jnp.int32)
     edges = []
     for c in range(4):
         here = [(4 + fines[c], z_ref[0, c])]
         if c in (0, 3):
-            here.append((c // 3 + 2, near_ref[c // 3, c]))
+            here.append((c // 3 + 2, all_ref[c // 3 + 2, c]))
         found = contribs(
             diag_ref[2 * c + fines[c]], [fine_ref[d, c] for d, _ in here], [p for _, p in here]
         )
         z_ref[1, c] = found[0]
         edges += found[1:]
     up = gy % 2 == 0
-    low, high = near_ref[0, 0], near_ref[1, 3]
+    low, high = all_ref[2, 0], all_ref[3, 3]
     ya_ref[0, 0], yb_ref[0, 0] = jnp.where(up, high, low), jnp.where(up, low, high)
     low, high = edges
     ya_ref[1, 0], yb_ref[1, 0] = jnp.where(up, high, low), jnp.where(up, low, high)
@@ -305,37 +303,26 @@
 
 
 def near_kernel(
-    split_ref, diag_ref, face_ref, fine_ref, near_ref, inside_ref, xa_ref, xb_ref, z_ref,
-    sum_ref, interp_ref, zero_ref, sems,
+    split_ref, diag_ref, face_ref, fine_ref, all_ref, sum_ref, interp_ref, zero_ref, sems
 ):
-    gx = lax.axis_index("gx")
-    fines = [fine_of(split_ref, c) for c in range(4)]
+    flags = split_ref[...][0, 0]
+    fines = [fine_of(flags, c) for c in range(4)]
+    zero_ref[...] = jnp.zeros((6, B, B), BF16)
     copies = []
-
-    def send(block, d, e):
-        copies.append(pltpu.make_async_copy(block, interp_ref.at[d, e], sems.at[len(copies)]))
-        copies[-1].start()
-
-    zero_ref[...] = jnp.zeros((B, B), BF16)
     for c in range(4):
         e = 2 * c + fines[c]
-        send(xa_ref.at[c], 1 - gx % 2, e)
-        send(xb_ref.at[c], gx % 2, e)
-        send(near_ref.at[0, c], 2, e)
-        send(near_ref.at[1, c], 3, e)
-        send(inside_ref.at[c], 5 - fines[c], e)
-        send(z_ref.at[0, c], 4 + fines[c], e)
-    for c in range(4):
-        for d in range(6):
-            send(zero_ref, d, 2 * c + 1 - fines[c])
+        for block, to in ((all_ref.at[:, c], e), (zero_ref, 4 * c + 1 - e)):
+            copies.append(pltpu.make_async_copy(block, interp_ref.at[:, to], sems.at[len(copies)]))
+    for copy in copies[::2] + copies[1::2]:
+        copy.start()
     parts = [[] for _ in range(4)]
     for c in range(4):
         z = fines[c]
-        here = [(c, 1 - z, 4 + z, 5 - z, inside_ref[c])]
+        here = [(c, 1 - z, 4 + z, 5 - z, all_ref[5 - z, c])]
         if c > 0:
-            here.append((c - 1, z, 3, 2, near_ref[0, c]))
+            here.append((c - 1, z, 3, 2, all_ref[2, c]))
         if c < 3:
-            here.append((c + 1, z, 2, 3, near_ref[1, c]))
+            here.append((c + 1, z, 2, 3, all_ref[3, c]))
         found = contribs(
             diag_ref[2 * c + z], [fine_ref[d, c] for _, _, _, d, _ in here], [p for *_, p in here]
         )
@@ -352,41 +339,56 @@
         copy.wait()
 
 
+def bit_at(code, place):
+    return lax.shift_right_logical(code, place) & 1
+
+
+def from_x(z, d, sent, interp, c):
+    theirs, face = sent[pl.ds(B * c, B), :], sent[pl.ds(B * (4 + c), B), :]
+    return z, d, interp[c], contribs(theirs, [face], [interp[c]])[0]
+
+
+def added(c, arrived, sum_ref, face_ref):
+    totals = [sum_ref[2 * c], sum_ref[2 * c + 1]]
+    for z, d, interp, contrib in arrived:
+        part = contrib.astype(F32) + mm(face_ref[d, 2 * c + z], interp)
+        totals = [total + jnp.where(z == k, part, 0.0) for k, total in enumerate(totals)]
+    return totals
+
+
+def middle_kernel(code_ref, sum_ref, face_ref, ha, xa_ref, z_ref, total_ref):
+    gx, gz = lax.axis_index("gx"), lax.axis_index("gz")
+    code = code_ref[...][0, 0]
+    for c in range(4):
+        arrived = [
+            (1 - gz, 5 - gz, z_ref[0, c], z_ref[1, c]),
+            from_x(bit_at(code, c), 1 - gx % 2, ha, xa_ref, c),
+        ]
+        totals = added(c, arrived, sum_ref, face_ref)
+        total_ref[2 * c], total_ref[2 * c + 1] = totals
+
+
 def coarse_kernel(
-    split_ref, code_ref, sum_ref, face_ref, ha, hb, xa_ref, xb_ref, ya_ref, yb_ref, z_ref,
+    split_ref, code_ref, sum_ref, face_ref, hb, xb_ref, ya_ref, yb_ref,
     coarse_ref, total_ref, sems,
 ):
-    gx, gy, gz = lax.axis_index("gx"), lax.axis_index("gy"), lax.axis_index("gz")
-    code = code_ref[0, 0]
+    gx, gy = lax.axis_index("gx"), lax.axis_index("gy")
+    code = code_ref[...][0, 0]
     up = gy % 2 == 0
-
-    def bit_at(place):
-        return lax.shift_right_logical(code, place) & 1
-
+    flags = split_ref[...][0, 0]
     copies = []
     for c in (1, 2, 0, 3):
-        arrived = [(1 - gz, 5 - gz, z_ref[0, c], z_ref[1, c])]
-        for z, d, sent, ref in (
-            (bit_at(c), 1 - gx % 2, ha, xa_ref), (bit_at(4 + c), gx % 2, hb, xb_ref)
-        ):
-            theirs, face = sent[pl.ds(B * c, B), :], sent[pl.ds(B * (4 + c), B), :]
-            arrived.append((z, d, ref[c], contribs(theirs, [face], [ref[c]])[0]))
+        arrived = [from_x(bit_at(code, 4 + c), gx % 2, hb, xb_ref, c)]
         if c in (0, 3):
             first = up if c == 3 else jnp.logical_not(up)
             edge = 0 if c == 3 else 3
-            z = jnp.where(first, bit_at(8 + edge), bit_at(12 + edge))
+            z = jnp.where(first, bit_at(code, 8 + edge), bit_at(code, 12 + edge))
             pair = [jnp.where(first, ya_ref[k, 0], yb_ref[k, 0]) for k in range(2)]
             arrived.append((z, 3 if c == 3 else 2, *pair))
-        totals = [sum_ref[2 * c], sum_ref[2 * c + 1]]
-        parts = [
-            (z, contrib.astype(F32) + mm(face_ref[d, 2 * c + z], interp))
-            for z, d, interp, contrib in arrived
-        ]
+        totals = added(c, arrived, sum_ref, face_ref)
         for k in range(2):
             e = 2 * c + k
-            keep = split_at(split_ref, c, k) == 1
-            for z, part in parts:
-                totals[k] = totals[k] + jnp.where(z == k, part, 0.0)
+            keep = split_at(flags, c, k) == 1
             total_ref[e] = jnp.where(keep, totals[k], 0.0)
             copies.append(pltpu.make_async_copy(total_ref.at[e], coarse_ref.at[e], sems.at[e]))
             copies[-1].start()
@@ -428,39 +430,46 @@
         facts_kernel,
         (sds((16, B), F32), sds((8, B), jnp.int32), blocks(8), packed, packed),
         [HBM] * 3, (VMEM,) * 5,
-        [pltpu.VMEM((8, B), F32), pltpu.SMEM((1, 2, 4), jnp.int32), dma((25,))], 1 << 20,
+        [
+            pltpu.VMEM((8, B), F32), pltpu.SMEM((1, 2, 4), jnp.int32),
+            pltpu.VMEM((2, 8, B, B), BF16), dma((3,)),
+        ],
+        1 << 20,
     )(in_hbm(split), in_hbm(diag), in_hbm(face))
     ha, hb = swap(pa, "gx", 0), swap(pb, "gx", 1)
     hc, hd = swap(facts, "gy", 0), swap(facts, "gy", 1)
     hz = swap(facts, "gz", 0)
     solved, fnorm, fine = call(
         inverse_kernel, (sds((6, 4, B, B), F32), sds((48, B), F32), blocks(6, 4)),
-        [SMEM, VMEM, HBM], (VMEM, VMEM, VMEM),
+        [VMEM, VMEM, HBM], (VMEM, VMEM, VMEM),
         [
             pltpu.VMEM((3, 4, B, B), BF16), pltpu.VMEM((48, B), F32), pltpu.VMEM((2, B, B), F32),
-            dma((24,)),
+            dma((4,)),
         ],
         1 << 30,
     )(flags, diag, in_hbm(face))
-    code, xa, xb, ya, yb, z, near, inside = call(
+    code, xa, xb, ya, yb, z, both = call(
         interp_kernel,
         (
             sds((8, B), jnp.int32), blocks(4), blocks(4), blocks(2, 1),
-            blocks(2, 1), blocks(2, 4), blocks(2, 4), blocks(4),
+            blocks(2, 1), blocks(2, 4), blocks(6, 4),
         ),
-        [SMEM] + [VMEM] * 10, (VMEM,) * 8, [pltpu.VMEM((6, 8, B), F32)], 1 << 30,
+        [VMEM] + [VMEM] * 10, (VMEM,) * 7, [pltpu.VMEM((6, 8, B), F32)], 1 << 30,
     )(flags, diag, fine, solved, fnorm, facts, ha, hb, hc, hd, hz)
-    sa, sb = swap(xa, "gx", 0), swap(xb, "gx", 1)
+    xa, xb = swap(xa, "gx", 0), swap(xb, "gx", 1)
     ya, yb = swap(ya, "gy", 0), swap(yb, "gy", 1)
-    sz = swap(z, "gz", 0)
+    z = swap(z, "gz", 0)
     total, interp = call(
-        near_kernel, (sds((8, B, B), F32), blocks(6, 8)), [SMEM] + [VMEM] * 8, (VMEM, HBM),
-        [pltpu.VMEM((B, B), BF16), dma((48,))], 1 << 30,
-    )(flags, diag, face, fine, near, inside, xa, xb, z)
+        near_kernel, (sds((8, B, B), F32), blocks(6, 8)), [VMEM] + [VMEM] * 4, (VMEM, HBM),
+        [pltpu.VMEM((6, B, B), BF16), dma((8,))], 1 << 30,
+    )(flags, diag, face, fine, both)
+    total = call(
+        middle_kernel, sds((8, B, B), F32), [VMEM] + [VMEM] * 5, VMEM, [], 1 << 30,
+    )(code, total, face, ha, xa, z)
     coarse = call(
-        coarse_kernel, sds((8, B, B), F32), [SMEM, SMEM] + [VMEM] * 9, HBM,
+        coarse_kernel, sds((8, B, B), F32), [VMEM] * 8, HBM,
         [pltpu.VMEM((8, B, B), F32), dma((8,))], 1 << 30,
-    )(flags, code, total, face, ha, hb, sa, sb, ya, yb, sz)
+    )(flags, code, total, face, hb, xb, ya, yb)
     return interp.reshape(face_blocks.shape), coarse.reshape(diag_blocks.shape)
 
 

time: 36.2 us -> 35.2 us (0.972)
  the two profiles are of different devices: /device:TPU:10 before, /device:TPU:98 now
where the time goes in v6:
time: 35.2 us; the launch traced here: 35 us
  starting transfers between devices  19.2 us (55%)
  Pallas kernels  8.32 us (24%)
  waiting for transfers between devices  6.63 us (19%)
  between operations  0.8 us (2%)
    ppermute x10, starting transfers between devices, swap(): return lax.ppermute(x, axis, matching(lax.axis_size(axis), start))  19.2 us
    ppermute x10, waiting for transfers between devices, swap(): return lax.ppermute(x, axis, matching(lax.axis_size(axis), start))  6.63 us
    pallas_call x1, Pallas kernels, on_device(): call(inverse_kernel, (sds((6, 4, B, B), F32), sds((48, B), F32), blocks(6...  2.75 us
    pallas_call x1, Pallas kernels, on_device(): call(coarse_kernel, sds((8, B, B), F32), [VMEM] * 8, HBM, [pltpu.VMEM((8,...  1.29 us
    pallas_call x1, Pallas kernels, on_device(): call(near_kernel, (sds((8, B, B), F32), blocks(6, 8)), [VMEM] + [VMEM] *...  1.28 us
    pallas_call x1, Pallas kernels, on_device(): call(facts_kernel, (sds((16, B), F32), sds((8, B), jnp.int32), blocks(8),...  1.21 us
    pallas_call x1, Pallas kernels, on_device(): call(interp_kernel, (sds((8, B), jnp.int32), blocks(4), blocks(4), blocks...  0.96 us
    pallas_call x1, Pallas kernels, on_device(): call(middle_kernel, sds((8, B, B), F32), [VMEM] + [VMEM] * 5, VMEM, [], 1...  0.84 us
  transfers between devices with their start and end apart: 10, of which 2 were waited for; matrix products, arithmetic and copies ran while one was open for 0% of the time, Pallas kernels for 14%

profile of v6, /device:TPU:98, one launch (start us, length us, event | category | flops | bytes accessed | tf_op | source)
XLA Modules:
  0.0 35.0 jit_solution(15683376349871481684)
XLA Ops:
  0.6 1.2 %shard_map.50 = (f32[16,128]{1,0:T(8,128)S(1)}, s32[8,128]{1,0:T(8,128)S(1)}, bf16[8,128,128]{2,1,0:T(8,128)(2,1)S(1)}, bf16[1056,128]{1,0:T(8,128)(2,1)S(1)}, bf16[1056,128]{1,0:T(8,128)(2,1)S(1)}) custom-call(s32[1,2,4]{2,1,0:T(2,128)} %bitcast.13, bf16[8,128,128]{2,1,0:T(8,128)(2,1)} %bitcast.12, bf16[6,8,128,128]{3,2,1,0:T(8,128)(2,1)} %bitcast.7), custom_call_target="tpu_custom_call" | custom-call | flops 1048576 | bytes 2097152 | tf_op jit(solution)/shard_map/pallas_call | solution.py:429
  1.8 1.7 %collective-permute-start = (bf16[1056,128]{1,0:T(8,128)(2,1)S(1)}, bf16[1056,128]{1,0:T(8,128)(2,1)S(1)}, u32[]{:S(2)}, u32[]{:S(2)}) collective-permute-start(bf16[1056,128]{1,0:T(8,128)(2,1)S(1)} %get-tuple-element.25), channel_id=1, source_target_pairs={{0,16},{32,48},{64,80},{96,112},{16,0},{48,32},{80,64},{112,96},{1... | collective-permute-start | bytes 811016 | tf_op jit(solution)/shard_map/ppermute | solution.py:405
  3.5 4.1 %collective-permute-start.1 = (bf16[1056,128]{1,0:T(8,128)(2,1)S(1)}, bf16[1056,128]{1,0:T(8,128)(2,1)S(1)}, u32[]{:S(2)}, u32[]{:S(2)}) collective-permute-start(bf16[1056,128]{1,0:T(8,128)(2,1)S(1)} %get-tuple-element.26), channel_id=1, source_target_pairs={{16,32},{48,64},{80,96},{32,16},{64,48},{96,80},{17,33},{49,65},{8... | collective-permute-start | bytes 811016 | tf_op jit(solution)/shard_map/ppermute | solution.py:405
  7.6 0.1 collective-permute-start.4
  7.7 2.3 %collective-permute-start.3 = (f32[16,128]{1,0:T(8,128)S(1)}, f32[16,128]{1,0:T(8,128)S(1)}, u32[]{:S(2)}, u32[]{:S(2)}) collective-permute-start(f32[16,128]{1,0:T(8,128)S(1)} %get-tuple-element.24.facts_ref), channel_id=1, source_target_pairs={{2,4},{6,8},{10,12},{4,2},{8,6},{12,10},{3,5},{7,9},{11,13},{5,3},... | collective-permute-start | bytes 24584 | tf_op jit(solution)/shard_map/ppermute | solution.py:405
  10.0 1.6 %collective-permute-start.2 = (f32[16,128]{1,0:T(8,128)S(1)}, f32[16,128]{1,0:T(8,128)S(1)}, u32[]{:S(2)}, u32[]{:S(2)}) collective-permute-start(f32[16,128]{1,0:T(8,128)S(1)} %get-tuple-element.24.facts_ref), channel_id=1, source_target_pairs={{0,2},{4,6},{8,10},{12,14},{2,0},{6,4},{10,8},{14,12},{1,3},{5,7},... | collective-permute-start | bytes 24584 | tf_op jit(solution)/shard_map/ppermute | solution.py:405
  11.7 2.7 %shard_map.51 = (f32[6,4,128,128]{3,2,1,0:T(8,128)S(1)}, f32[48,128]{1,0:T(8,128)S(1)}, bf16[6,4,128,128]{3,2,1,0:T(8,128)(2,1)S(1)}) custom-call(s32[8,128]{1,0:T(8,128)S(1)} %get-tuple-element.19.split_ref, bf16[8,128,128]{2,1,0:T(8,128)(2,1)S(1)} %get-tuple-element.20.diag_ref, bf16[6,8,128,128]{3,2,1,0:T(8,128)(2,1)} %bitcast.8), custom_call_target="tpu_custom_call" | custom-call | flops 1073741824 | bytes 2097152 | tf_op jit(solution)/shard_map/pallas_call | solution.py:442
  14.4 0.0 collective-permute-done.4.hz
  14.4 0.0 collective-permute-done.3.hd
  14.4 0.0 collective-permute-done.2.hc
  14.4 0.0 collective-permute-done.ha
  14.5 2.5 %collective-permute-done.1.hb = bf16[1056,128]{1,0:T(8,128)(2,1)S(1)} collective-permute-done((bf16[1056,128]{1,0:T(8,128)(2,1)S(1)}, bf16[1056,128]{1,0:T(8,128)(2,1)S(1)}, u32[]{:S(2)}, u32[]{:S(2)}) %collective-permute-start.1) | collective-permute-done | bytes 270368 | tf_op jit(solution)/shard_map/ppermute | solution.py:405
  16.9 0.0 copy-start
  16.9 1.0 %shard_map.52 = (s32[8,128]{1,0:T(8,128)S(1)}, bf16[4,128,128]{2,1,0:T(8,128)(2,1)S(1)}, bf16[4,128,128]{2,1,0:T(8,128)(2,1)S(1)}, bf16[2,1,128,128]{3,2,1,0:T(8...) custom-call(s32[8,128]{1,0:T(8,128)S(1)} %get-tuple-element.19.split, ...), custom_call_target="tpu_custom_call" | custom-call | flops 1073741824 | bytes 2097152 | tf_op jit(solution)/shard_map/pallas_call | solution.py:451
  17.9 0.1 collective-permute-start.6
  18.0 0.1 collective-permute-start.5
  18.1 0.5 %collective-permute-start.8 = (bf16[2,1,128,128]{3,2,1,0:T(8,128)(2,1)S(1)}, bf16[2,1,128,128]{3,2,1,0:T(8,128)(2,1)S(1)}, u32[]{:S(2)}, u32[]{:S(2)}) collective-permute-start(bf16[2,1,128,128]{3,2,1,0:T(8,128)(2,1)S(1)} %get-tuple-element.34), channel_id=1, source_target_pairs={{0,2},{4,6},{8,10},{12,14},{2,0},{6,4},{10,8},{14,12},{1,3},{5,7},... | collective-permute-start | bytes 196616 | tf_op jit(solution)/shard_map/ppermute | solution.py:405
  18.6 4.4 %collective-permute-start.9 = (bf16[2,1,128,128]{3,2,1,0:T(8,128)(2,1)S(1)}, bf16[2,1,128,128]{3,2,1,0:T(8,128)(2,1)S(1)}, u32[]{:S(2)}, u32[]{:S(2)}) collective-permute-start(bf16[2,1,128,128]{3,2,1,0:T(8,128)(2,1)S(1)} %get-tuple-element.35), channel_id=1, source_target_pairs={{2,4},{6,8},{10,12},{4,2},{8,6},{12,10},{3,5},{7,9},{11,13},{5,3},... | collective-permute-start | bytes 196616 | tf_op jit(solution)/shard_map/ppermute | solution.py:405
  23.0 4.4 %collective-permute-start.7 = (bf16[4,128,128]{2,1,0:T(8,128)(2,1)S(1)}, bf16[4,128,128]{2,1,0:T(8,128)(2,1)S(1)}, u32[]{:S(2)}, u32[]{:S(2)}) collective-permute-start(bf16[4,128,128]{2,1,0:T(8,128)(2,1)S(1)} %get-tuple-element.33), channel_id=1, source_target_pairs={{16,32},{48,64},{80,96},{32,16},{64,48},{96,80},{17,33},{49,65},{8... | collective-permute-start | bytes 393224 | tf_op jit(solution)/shard_map/ppermute | solution.py:405
  27.4 0.0 copy-done
  27.4 1.3 %shard_map.53 = (f32[8,128,128]{2,1,0:T(8,128)S(1)}, bf16[6,8,128,128]{3,2,1,0:T(8,128)(2,1)}) custom-call(s32[8,128]{1,0:T(8,128)S(1)} %get-tuple-element.19.split_ref, bf16[8,128,128]{2,1,0:T(8,128)(2,1)S(1)} %get-tuple-element.20.diag_ref, bf16[6,8,128,128]{3,2,1,0:T(8,128)(2,1)S(1)} %bitcast.9, bf16[6,4,128,128]{3,2,1,0:T(8,128)(2,1)S(1)} %get-tuple-element.21.fine_ref, ...), custom_call_target="tpu_custom_call" | custom-call | flops 1073741824 | bytes 2097152 | tf_op jit(solution)/shard_map/pallas_call | solution.py:462
  28.7 0.0 collective-permute-done.5.xa_ref
  28.7 0.0 collective-permute-done.6.z_ref
  28.7 0.8 %shard_map.54.sum_ref = f32[8,128,128]{2,1,0:T(8,128)S(1)} custom-call(s32[8,128]{1,0:T(8,128)S(1)} %get-tuple-element.29.code_ref, f32[8,128,128]{2,1,0:T(8,128)S(1)} %get-tuple-element.30.sum_ref, bf16[6,8,128,128]{3,2,1,0:T(8,128)(2,1)S(1)} %bitcast.10, bf16[1056,128]{1,0:T(8,128)(2,1)S(1)} %collective-permute-done.ha, ...), custom_call_target="tpu_custom_call" | custom-call | flops 1073741824 | bytes 2097152 | tf_op jit(solution)/shard_map/pallas_call | solution.py:466
  29.6 0.0 collective-permute-done.8.ya_ref
  29.6 0.0 collective-permute-done.9.yb_ref
  29.6 4.1 %collective-permute-done.7.xb_ref = bf16[4,128,128]{2,1,0:T(8,128)(2,1)S(1)} collective-permute-done((bf16[4,128,128]{2,1,0:T(8,128)(2,1)S(1)}, bf16[4,128,128]{2,1,0:T(8,128)(2,1)S(1)}, u32[]{:S(2)}, u32[]{:S(2)}) %collective-permute-start.7) | collective-permute-done | bytes 131104 | tf_op jit(solution)/shard_map/ppermute | solution.py:405
  33.7 1.3 %shard_map.55 = f32[8,128,128]{2,1,0:T(8,128)} custom-call(s32[8,128]{1,0:T(8,128)S(1)} %get-tuple-element.19.split_ref, s32[8,128]{1,0:T(8,128)S(1)} %get-tuple-element.29.code_ref, f32[8,128,128]{2,1,0:T(8,128)S(1)} %shard_map.54.sum_ref, bf16[6,8,128,128]{3,2,1,0:T(8,128)(2,1)S(1)} %bitcast.11, bf16[1056,128]{1,0:T(8,128)(2,1)S(1)} %collective-permute-done.1.hb, ...), custom_call_target="tpu_custom_call" | custom-call | flops 1073741824 | bytes 2097152 | tf_op jit(solution)/shard_map/pallas_call | solution.py:469
Async XLA Ops:
  1.8 12.6 %collective-permute-start = (bf16[1056,128]{1,0:T(8,128)(2,1)S(1)}, bf16[1056,128]{1,0:T(8,128)(2,1)S(1)}, u32[]{:S(2)}, u32[]{:S(2)}) collective-permute-start(bf16[1056,128]{1,0:T(8,128)(2,1)S(1)} %get-tuple-element.25), channel_id=1, source_target_pairs={{0,16},{32,48},{64,80},{96,112},{16,0},{48,32},{80,64},{112,96},{1... | collective-permute-start | bytes 811016 | tf_op jit(solution)/shard_map/ppermute | solution.py:405
  3.5 13.4 %collective-permute-start.1 = (bf16[1056,128]{1,0:T(8,128)(2,1)S(1)}, bf16[1056,128]{1,0:T(8,128)(2,1)S(1)}, u32[]{:S(2)}, u32[]{:S(2)}) collective-permute-start(bf16[1056,128]{1,0:T(8,128)(2,1)S(1)} %get-tuple-element.26), channel_id=1, source_target_pairs={{16,32},{48,64},{80,96},{32,16},{64,48},{96,80},{17,33},{49,65},{8... | collective-permute-start | bytes 811016 | tf_op jit(solution)/shard_map/ppermute | solution.py:405
  7.6 6.8 %collective-permute-start.4 = (f32[16,128]{1,0:T(8,128)S(1)}, f32[16,128]{1,0:T(8,128)S(1)}, u32[]{:S(2)}, u32[]{:S(2)}) collective-permute-start(f32[16,128]{1,0:T(8,128)S(1)} %get-tuple-element.24.facts_ref), channel_id=1, source_target_pairs={{0,1},{1,0},{2,3},{3,2},{4,5},{5,4},{6,7},{7,6},{8,9},{9,8},{10,11... | collective-permute-start | bytes 24584 | tf_op jit(solution)/shard_map/ppermute | solution.py:405
  7.7 6.8 %collective-permute-start.3 = (f32[16,128]{1,0:T(8,128)S(1)}, f32[16,128]{1,0:T(8,128)S(1)}, u32[]{:S(2)}, u32[]{:S(2)}) collective-permute-start(f32[16,128]{1,0:T(8,128)S(1)} %get-tuple-element.24.facts_ref), channel_id=1, source_target_pairs={{2,4},{6,8},{10,12},{4,2},{8,6},{12,10},{3,5},{7,9},{11,13},{5,3},... | collective-permute-start | bytes 24584 | tf_op jit(solution)/shard_map/ppermute | solution.py:405
  10.0 4.4 %collective-permute-start.2 = (f32[16,128]{1,0:T(8,128)S(1)}, f32[16,128]{1,0:T(8,128)S(1)}, u32[]{:S(2)}, u32[]{:S(2)}) collective-permute-start(f32[16,128]{1,0:T(8,128)S(1)} %get-tuple-element.24.facts_ref), channel_id=1, source_target_pairs={{0,2},{4,6},{8,10},{12,14},{2,0},{6,4},{10,8},{14,12},{1,3},{5,7},... | collective-permute-start | bytes 24584 | tf_op jit(solution)/shard_map/ppermute | solution.py:405
  16.9 10.5 %copy-start = (bf16[6,1,4,2,128,128]{5,4,3,2,1,0:T(8,128)(2,1)S(1)}, bf16[6,1,4,2,128,128]{5,4,3,2,1,0:T(8,128)(2,1)}, u32[]{:S(2)}) copy-start(bf16[6,1,4,2,128,128]{5,4,3,2,1,0:T(8,128)(2,1)} %param.4) | copy-start | bytes 4718596
  17.9 10.8 %collective-permute-start.6 = (bf16[2,4,128,128]{3,2,1,0:T(8,128)(2,1)S(1)}, bf16[2,4,128,128]{3,2,1,0:T(8,128)(2,1)S(1)}, u32[]{:S(2)}, u32[]{:S(2)}) collective-permute-start(bf16[2,4,128,128]{3,2,1,0:T(8,128)(2,1)S(1)} %get-tuple-element.32), channel_id=1, source_target_pairs={{0,1},{1,0},{2,3},{3,2},{4,5},{5,4},{6,7},{7,6},{8,9},{9,8},{10,11... | collective-permute-start | bytes 786440 | tf_op jit(solution)/shard_map/ppermute | solution.py:405
  18.0 10.7 %collective-permute-start.5 = (bf16[4,128,128]{2,1,0:T(8,128)(2,1)S(1)}, bf16[4,128,128]{2,1,0:T(8,128)(2,1)S(1)}, u32[]{:S(2)}, u32[]{:S(2)}) collective-permute-start(bf16[4,128,128]{2,1,0:T(8,128)(2,1)S(1)} %get-tuple-element.31), channel_id=1, source_target_pairs={{0,16},{32,48},{64,80},{96,112},{16,0},{48,32},{80,64},{112,96},{1... | collective-permute-start | bytes 393224 | tf_op jit(solution)/shard_map/ppermute | solution.py:405
  18.1 11.5 %collective-permute-start.8 = (bf16[2,1,128,128]{3,2,1,0:T(8,128)(2,1)S(1)}, bf16[2,1,128,128]{3,2,1,0:T(8,128)(2,1)S(1)}, u32[]{:S(2)}, u32[]{:S(2)}) collective-permute-start(bf16[2,1,128,128]{3,2,1,0:T(8,128)(2,1)S(1)} %get-tuple-element.34), channel_id=1, source_target_pairs={{0,2},{4,6},{8,10},{12,14},{2,0},{6,4},{10,8},{14,12},{1,3},{5,7},... | collective-permute-start | bytes 196616 | tf_op jit(solution)/shard_map/ppermute | solution.py:405
  18.6 11.0 %collective-permute-start.9 = (bf16[2,1,128,128]{3,2,1,0:T(8,128)(2,1)S(1)}, bf16[2,1,128,128]{3,2,1,0:T(8,128)(2,1)S(1)}, u32[]{:S(2)}, u32[]{:S(2)}) collective-permute-start(bf16[2,1,128,128]{3,2,1,0:T(8,128)(2,1)S(1)} %get-tuple-element.35), channel_id=1, source_target_pairs={{2,4},{6,8},{10,12},{4,2},{8,6},{12,10},{3,5},{7,9},{11,13},{5,3},... | collective-permute-start | bytes 196616 | tf_op jit(solution)/shard_map/ppermute | solution.py:405
  23.0 10.7 %collective-permute-start.7 = (bf16[4,128,128]{2,1,0:T(8,128)(2,1)S(1)}, bf16[4,128,128]{2,1,0:T(8,128)(2,1)S(1)}, u32[]{:S(2)}, u32[]{:S(2)}) collective-permute-start(bf16[4,128,128]{2,1,0:T(8,128)(2,1)S(1)} %get-tuple-element.33), channel_id=1, source_target_pairs={{16,32},{48,64},{80,96},{32,16},{64,48},{96,80},{17,33},{49,65},{8... | collective-permute-start | bytes 393224 | tf_op jit(solution)/shard_map/ppermute | solution.py:405

commit v7 on v6

--- a/solution.py
+++ b/solution.py
@@ -56,14 +56,18 @@
 
 
 def facts_kernel(
-    split_ref, diag_ref, face_ref, facts_ref, flags_ref, kept_ref, xa_ref, xb_ref, rows, held, faces, sems
+    split_ref, diag_ref, face_ref,
+    facts_ref, flags_ref, kept_ref, xa_ref, xb_ref, z_ref, rows, held, faces, sems,
 ):
-    gx = lax.axis_index("gx")
+    gx, gz = lax.axis_index("gx"), lax.axis_index("gz")
     copies = [
         pltpu.make_async_copy(split_ref, held, sems.at[0]),
         pltpu.make_async_copy(diag_ref, kept_ref, sems.at[1]),
         pltpu.make_async_copy(face_ref.at[pl.ds(0, 2)], faces, sems.at[2]),
     ]
+    for c in range(4):
+        block, into = face_ref.at[5 - gz, 2 * c + 1 - gz], z_ref.at[pl.ds(B * (4 + c), B), :]
+        copies.append(pltpu.make_async_copy(block, into, sems.at[3 + c]))
     for copy in copies:
         copy.start()
     copies[0].wait()
@@ -81,18 +85,20 @@
         rows[pl.ds(e, 1), :] = square_sums(kept_ref[e])
     norms = norms_of(rows[...])
     facts_ref[pl.ds(0, 8), :] = norms
-    copies[2].wait()
+    parts = [part.astype(F32) for part in thirds(norms)] + [flags]
+    for ref in (xa_ref, xb_ref, z_ref):
+        for k in range(2):
+            both = jnp.concatenate(parts[2 * k:2 * k + 2], axis=0)
+            ref[pl.ds(8 * B + 16 * k, 16), :] = both.astype(BF16)
+    for copy in copies[2:]:
+        copy.wait()
     for c in range(4):
         e = 2 * c + splits[2 * c]
         block = kept_ref[e]
+        z_ref[pl.ds(B * c, B), :] = kept_ref[2 * c + 1 - gz]
         for ref, d in ((xa_ref, 1 - gx % 2), (xb_ref, gx % 2)):
             ref[pl.ds(B * c, B), :] = block
             ref[pl.ds(B * (4 + c), B), :] = faces[d, e]
-    parts = [part.astype(F32) for part in thirds(norms)] + [flags]
-    for ref in (xa_ref, xb_ref):
-        for k in range(2):
-            both = jnp.concatenate(parts[2 * k:2 * k + 2], axis=0)
-            ref[pl.ds(8 * B + 16 * k, 16), :] = both.astype(BF16)
 
 
 def facts_in(ref):
@@ -199,20 +205,17 @@
     depth = row % 2
     even_x, even_y = gx % 2 == 0, gy % 2 == 0
 
-    xa, xb = facts_in(ha), facts_in(hb)
-
-    def pick(test, first, second, part):
-        rows = pl.ds(8 * part, 8)
-        return jnp.where(test, first[rows, :], second[rows, :])
+    xa, xb, beyond = facts_in(ha), facts_in(hb), facts_in(hz)
+    ya, yb = (hc[pl.ds(0, 8), :], hc[pl.ds(8, 8), :]), (hd[pl.ds(0, 8), :], hd[pl.ds(8, 8), :])
 
     def neighbours(part):
         own = facts_ref[pl.ds(8 * part, 8), :]
-        z = hz[pl.ds(8 * part, 8), :]
+        z = beyond[part]
         return (
             jnp.where(even_x, xb[part], xa[part]),
             jnp.where(even_x, xa[part], xb[part]),
-            shifted(own, pick(even_y, hd, hc, part), 2, row < 2),
-            shifted(own, pick(even_y, hc, hd, part), 6, row >= 6),
+            shifted(own, jnp.where(even_y, yb[part], ya[part]), 2, row < 2),
+            shifted(own, jnp.where(even_y, ya[part], yb[part]), 6, row >= 6),
             jnp.where(depth == 0, pltpu.roll(z, 7, 0), pltpu.roll(own, 1, 0)),
             jnp.where(depth == 1, pltpu.roll(z, 1, 0), pltpu.roll(own, 7, 0)),
         )
@@ -260,30 +263,21 @@
         low, high = all_ref[0, c], all_ref[1, c]
         xa_ref[c] = jnp.where(even_x, high, low)
         xb_ref[c] = jnp.where(even_x, low, high)
-        z_ref[0, c] = all_ref[4 + fines[c], c]
+        z_ref[c] = all_ref[4 + fines[c], c]
     row = lax.broadcasted_iota(jnp.int32, (8, B), 0)
     lane = lax.broadcasted_iota(jnp.int32, (8, B), 1)
     bit = jnp.where((row % 2 == 0) & (lane == 0), 1, 0) * lax.shift_left(1, row // 2)
     code = jnp.zeros((8, B), F32)
-    splits = (facts_in(ha)[1], facts_in(hb)[1], hc[pl.ds(8, 8), :], hd[pl.ds(8, 8), :])
+    splits = [facts_in(ha)[1], facts_in(hb)[1], hc[pl.ds(8, 8), :], hd[pl.ds(8, 8), :]]
     for place, theirs in enumerate(splits):
         code = code + theirs * (bit * (1 << (4 * place))).astype(F32)
     code = jnp.sum(jnp.sum(code, axis=0, keepdims=True), axis=1, keepdims=True)
     code_ref[...] = jnp.broadcast_to(code, (8, B)).astype(jnp.int32)
-    edges = []
-    for c in range(4):
-        here = [(4 + fines[c], z_ref[0, c])]
-        if c in (0, 3):
-            here.append((c // 3 + 2, all_ref[c // 3 + 2, c]))
-        found = contribs(
-            diag_ref[2 * c + fines[c]], [fine_ref[d, c] for d, _ in here], [p for _, p in here]
-        )
-        z_ref[1, c] = found[0]
-        edges += found[1:]
     up = gy % 2 == 0
     low, high = all_ref[2, 0], all_ref[3, 3]
     ya_ref[0, 0], yb_ref[0, 0] = jnp.where(up, high, low), jnp.where(up, low, high)
-    low, high = edges
+    low = contribs(diag_ref[fines[0]], [fine_ref[2, 0]], [low])[0]
+    high = contribs(diag_ref[6 + fines[3]], [fine_ref[3, 3]], [high])[0]
     ya_ref[1, 0], yb_ref[1, 0] = jnp.where(up, high, low), jnp.where(up, low, high)
 
 
@@ -343,9 +337,13 @@
     return lax.shift_right_logical(code, place) & 1
 
 
-def from_x(z, d, sent, interp, c):
+def computed(z, d, theirs, face, interp):
+    return z, d, interp, contribs(theirs, [face], [interp])[0]
+
+
+def from_four(z, d, sent, interp, c):
     theirs, face = sent[pl.ds(B * c, B), :], sent[pl.ds(B * (4 + c), B), :]
-    return z, d, interp[c], contribs(theirs, [face], [interp[c]])[0]
+    return computed(z, d, theirs, face, interp[c])
 
 
 def added(c, arrived, sum_ref, face_ref):
@@ -356,13 +354,13 @@
     return totals
 
 
-def middle_kernel(code_ref, sum_ref, face_ref, ha, xa_ref, z_ref, total_ref):
+def middle_kernel(code_ref, sum_ref, face_ref, ha, hz, xa_ref, z_ref, total_ref):
     gx, gz = lax.axis_index("gx"), lax.axis_index("gz")
     code = code_ref[...][0, 0]
     for c in range(4):
         arrived = [
-            (1 - gz, 5 - gz, z_ref[0, c], z_ref[1, c]),
-            from_x(bit_at(code, c), 1 - gx % 2, ha, xa_ref, c),
+            from_four(1 - gz, 5 - gz, hz, z_ref, c),
+            from_four(bit_at(code, c), 1 - gx % 2, ha, xa_ref, c),
         ]
         totals = added(c, arrived, sum_ref, face_ref)
         total_ref[2 * c], total_ref[2 * c + 1] = totals
@@ -378,7 +376,7 @@
     flags = split_ref[...][0, 0]
     copies = []
     for c in (1, 2, 0, 3):
-        arrived = [from_x(bit_at(code, 4 + c), gx % 2, hb, xb_ref, c)]
+        arrived = [from_four(bit_at(code, 4 + c), gx % 2, hb, xb_ref, c)]
         if c in (0, 3):
             first = up if c == 3 else jnp.logical_not(up)
             edge = 0 if c == 3 else 3
@@ -426,19 +424,22 @@
     in_hbm = lambda x: pltpu.with_memory_space_constraint(x, pltpu.HBM)
     blocks = lambda *lead: sds(lead + (B, B), BF16)
     packed = sds((8 * B + 32, B), BF16)
-    facts, flags, diag, pa, pb = call(
+    facts, flags, diag, pa, pb, pz = call(
         facts_kernel,
-        (sds((16, B), F32), sds((8, B), jnp.int32), blocks(8), packed, packed),
-        [HBM] * 3, (VMEM,) * 5,
+        (
+            sds((16, B), F32), sds((8, B), jnp.int32), blocks(8),
+            packed, packed, packed,
+        ),
+        [HBM] * 3, (VMEM,) * 6,
         [
             pltpu.VMEM((8, B), F32), pltpu.SMEM((1, 2, 4), jnp.int32),
-            pltpu.VMEM((2, 8, B, B), BF16), dma((3,)),
+            pltpu.VMEM((2, 8, B, B), BF16), dma((7,)),
         ],
         1 << 20,
     )(in_hbm(split), in_hbm(diag), in_hbm(face))
     ha, hb = swap(pa, "gx", 0), swap(pb, "gx", 1)
     hc, hd = swap(facts, "gy", 0), swap(facts, "gy", 1)
-    hz = swap(facts, "gz", 0)
+    hz = swap(pz, "gz", 0)
     solved, fnorm, fine = call(
         inverse_kernel, (sds((6, 4, B, B), F32), sds((48, B), F32), blocks(6, 4)),
         [VMEM, VMEM, HBM], (VMEM, VMEM, VMEM),
@@ -451,10 +452,10 @@
     code, xa, xb, ya, yb, z, both = call(
         interp_kernel,
         (
-            sds((8, B), jnp.int32), blocks(4), blocks(4), blocks(2, 1),
-            blocks(2, 1), blocks(2, 4), blocks(6, 4),
+            sds((8, B), jnp.int32), blocks(4), blocks(4), blocks(2, 1), blocks(2, 1), blocks(4),
+            blocks(6, 4),
         ),
-        [VMEM] + [VMEM] * 10, (VMEM,) * 7, [pltpu.VMEM((6, 8, B), F32)], 1 << 30,
+        [VMEM] * 11, (VMEM,) * 7, [pltpu.VMEM((6, 8, B), F32)], 1 << 30,
     )(flags, diag, fine, solved, fnorm, facts, ha, hb, hc, hd, hz)
     xa, xb = swap(xa, "gx", 0), swap(xb, "gx", 1)
     ya, yb = swap(ya, "gy", 0), swap(yb, "gy", 1)
@@ -464,8 +465,8 @@
         [pltpu.VMEM((6, B, B), BF16), dma((8,))], 1 << 30,
     )(flags, diag, face, fine, both)
     total = call(
-        middle_kernel, sds((8, B, B), F32), [VMEM] + [VMEM] * 5, VMEM, [], 1 << 30,
-    )(code, total, face, ha, xa, z)
+        middle_kernel, sds((8, B, B), F32), [VMEM] * 7, VMEM, [], 1 << 30,
+    )(code, total, face, ha, hz, xa, z)
     coarse = call(
         coarse_kernel, sds((8, B, B), F32), [VMEM] * 8, HBM,
         [pltpu.VMEM((8, B, B), F32), dma((8,))], 1 << 30,

time: 35.2 us -> 35 us (level)
    pallas_call x1, Pallas kernels: 0.96 us -> 0.53 us  [on_device(): call(interp_kernel, (sds((8, B), jnp.int32), blocks(4), blocks(4), blocks...]
where the time goes in v7:
time: 35 us; the launch traced here: 34.7 us
  starting transfers between devices  19.2 us (55%)
  Pallas kernels  8.08 us (23%)
  waiting for transfers between devices  6.6 us (19%)
  between operations  0.79 us (2%)
    ppermute x10, starting transfers between devices, swap(): return lax.ppermute(x, axis, matching(lax.axis_size(axis), start))  19.2 us
    ppermute x10, waiting for transfers between devices, swap(): return lax.ppermute(x, axis, matching(lax.axis_size(axis), start))  6.6 us
    pallas_call x1, Pallas kernels, on_device(): call(inverse_kernel, (sds((6, 4, B, B), F32), sds((48, B), F32), blocks(6...  2.75 us
    pallas_call x1, Pallas kernels, on_device(): call(coarse_kernel, sds((8, B, B), F32), [VMEM] * 8, HBM, [pltpu.VMEM((8,...  1.29 us
    pallas_call x1, Pallas kernels, on_device(): call(near_kernel, (sds((8, B, B), F32), blocks(6, 8)), [VMEM] + [VMEM] *...  1.28 us
    pallas_call x1, Pallas kernels, on_device(): call(facts_kernel, (sds((16, B), F32), sds((8, B), jnp.int32), blocks(8),...  1.26 us
    pallas_call x1, Pallas kernels, on_device(): call(middle_kernel, sds((8, B, B), F32), [VMEM] * 7, VMEM, [], 1 << 30)  0.97 us
  transfers between devices with their start and end apart: 10, of which 2 were waited for; matrix products, arithmetic and copies ran while one was open for 0% of the time, Pallas kernels for 14%

profile of v7, /device:TPU:98, one launch (start us, length us, event | category | flops | bytes accessed | tf_op | source)
XLA Modules:
  0.0 34.7 jit_solution(4935521447587061813)
XLA Ops:
  0.6 1.3 %shard_map.50 = (f32[16,128]{1,0:T(8,128)S(1)}, s32[8,128]{1,0:T(8,128)S(1)}, bf16[8,128,128]{2,1,0:T(8,128)(2,1)S(1)}, bf16[1056,128]{1,0:T(8,128)(2,1)S(1)}, b...) custom-call(s32[1,2,4]{2,1,0:T(2,128)} %bitcast.13, bf16[8,128,128]{2,1,0:T(8,128)(2,1)} %bitcast.12, ...), custom_call_target="tpu_custom_call" | custom-call | flops 1048576 | bytes 2097152 | tf_op jit(solution)/shard_map/pallas_call | solution.py:427
  1.9 1.7 %collective-permute-start = (bf16[1056,128]{1,0:T(8,128)(2,1)S(1)}, bf16[1056,128]{1,0:T(8,128)(2,1)S(1)}, u32[]{:S(2)}, u32[]{:S(2)}) collective-permute-start(bf16[1056,128]{1,0:T(8,128)(2,1)S(1)} %get-tuple-element.26), channel_id=1, source_target_pairs={{0,16},{32,48},{64,80},{96,112},{16,0},{48,32},{80,64},{112,96},{1... | collective-permute-start | bytes 811016 | tf_op jit(solution)/shard_map/ppermute | solution.py:403
  3.5 4.1 %collective-permute-start.1 = (bf16[1056,128]{1,0:T(8,128)(2,1)S(1)}, bf16[1056,128]{1,0:T(8,128)(2,1)S(1)}, u32[]{:S(2)}, u32[]{:S(2)}) collective-permute-start(bf16[1056,128]{1,0:T(8,128)(2,1)S(1)} %get-tuple-element.27), channel_id=1, source_target_pairs={{16,32},{48,64},{80,96},{32,16},{64,48},{96,80},{17,33},{49,65},{8... | collective-permute-start | bytes 811016 | tf_op jit(solution)/shard_map/ppermute | solution.py:403
  7.6 0.1 collective-permute-start.4
  7.7 2.3 %collective-permute-start.3 = (f32[16,128]{1,0:T(8,128)S(1)}, f32[16,128]{1,0:T(8,128)S(1)}, u32[]{:S(2)}, u32[]{:S(2)}) collective-permute-start(f32[16,128]{1,0:T(8,128)S(1)} %get-tuple-element.25.facts_ref), channel_id=1, source_target_pairs={{2,4},{6,8},{10,12},{4,2},{8,6},{12,10},{3,5},{7,9},{11,13},{5,3},... | collective-permute-start | bytes 24584 | tf_op jit(solution)/shard_map/ppermute | solution.py:403
  10.1 1.6 %collective-permute-start.2 = (f32[16,128]{1,0:T(8,128)S(1)}, f32[16,128]{1,0:T(8,128)S(1)}, u32[]{:S(2)}, u32[]{:S(2)}) collective-permute-start(f32[16,128]{1,0:T(8,128)S(1)} %get-tuple-element.25.facts_ref), channel_id=1, source_target_pairs={{0,2},{4,6},{8,10},{12,14},{2,0},{6,4},{10,8},{14,12},{1,3},{5,7},... | collective-permute-start | bytes 24584 | tf_op jit(solution)/shard_map/ppermute | solution.py:403
  11.7 2.8 %shard_map.51 = (f32[6,4,128,128]{3,2,1,0:T(8,128)S(1)}, f32[48,128]{1,0:T(8,128)S(1)}, bf16[6,4,128,128]{3,2,1,0:T(8,128)(2,1)S(1)}) custom-call(s32[8,128]{1,0:T(8,128)S(1)} %get-tuple-element.20.split_ref, bf16[8,128,128]{2,1,0:T(8,128)(2,1)S(1)} %get-tuple-element.21.diag_ref, bf16[6,8,128,128]{3,2,1,0:T(8,128)(2,1)} %bitcast.8), custom_call_target="tpu_custom_call" | custom-call | flops 1073741824 | bytes 2097152 | tf_op jit(solution)/shard_map/pallas_call | solution.py:443
  14.5 0.0 collective-permute-done.3.hd
  14.5 0.0 collective-permute-done.2.hc
  14.5 0.0 collective-permute-done.ha
  14.5 2.5 %collective-permute-done.1.hb = bf16[1056,128]{1,0:T(8,128)(2,1)S(1)} collective-permute-done((bf16[1056,128]{1,0:T(8,128)(2,1)S(1)}, bf16[1056,128]{1,0:T(8,128)(2,1)S(1)}, u32[]{:S(2)}, u32[]{:S(2)}) %collective-permute-start.1) | collective-permute-done | bytes 270368 | tf_op jit(solution)/shard_map/ppermute | solution.py:403
  17.0 0.0 collective-permute-done.4.hz
  17.0 0.0 copy-start
  17.0 0.5 %shard_map.52 = (s32[8,128]{1,0:T(8,128)S(1)}, bf16[4,128,128]{2,1,0:T(8,128)(2,1)S(1)}, bf16[4,128,128]{2,1,0:T(8,128)(2,1)S(1)}, bf16[2,1,128,128]{3,2,1,0:T(8...) custom-call(s32[8,128]{1,0:T(8,128)S(1)} %get-tuple-element.20.split, ...), custom_call_target="tpu_custom_call" | custom-call | flops 1073741824 | bytes 2097152 | tf_op jit(solution)/shard_map/pallas_call | solution.py:452
  17.5 0.1 collective-permute-start.5
  17.6 0.1 collective-permute-start.6
  17.7 0.5 %collective-permute-start.8 = (bf16[2,1,128,128]{3,2,1,0:T(8,128)(2,1)S(1)}, bf16[2,1,128,128]{3,2,1,0:T(8,128)(2,1)S(1)}, u32[]{:S(2)}, u32[]{:S(2)}) collective-permute-start(bf16[2,1,128,128]{3,2,1,0:T(8,128)(2,1)S(1)} %get-tuple-element.36), channel_id=1, source_target_pairs={{0,2},{4,6},{8,10},{12,14},{2,0},{6,4},{10,8},{14,12},{1,3},{5,7},... | collective-permute-start | bytes 196616 | tf_op jit(solution)/shard_map/ppermute | solution.py:403
  18.2 4.4 %collective-permute-start.9 = (bf16[2,1,128,128]{3,2,1,0:T(8,128)(2,1)S(1)}, bf16[2,1,128,128]{3,2,1,0:T(8,128)(2,1)S(1)}, u32[]{:S(2)}, u32[]{:S(2)}) collective-permute-start(bf16[2,1,128,128]{3,2,1,0:T(8,128)(2,1)S(1)} %get-tuple-element.37), channel_id=1, source_target_pairs={{2,4},{6,8},{10,12},{4,2},{8,6},{12,10},{3,5},{7,9},{11,13},{5,3},... | collective-permute-start | bytes 196616 | tf_op jit(solution)/shard_map/ppermute | solution.py:403
  22.7 4.4 %collective-permute-start.7 = (bf16[4,128,128]{2,1,0:T(8,128)(2,1)S(1)}, bf16[4,128,128]{2,1,0:T(8,128)(2,1)S(1)}, u32[]{:S(2)}, u32[]{:S(2)}) collective-permute-start(bf16[4,128,128]{2,1,0:T(8,128)(2,1)S(1)} %get-tuple-element.35), channel_id=1, source_target_pairs={{16,32},{48,64},{80,96},{32,16},{64,48},{96,80},{17,33},{49,65},{8... | collective-permute-start | bytes 393224 | tf_op jit(solution)/shard_map/ppermute | solution.py:403
  27.0 0.0 copy-done
  27.0 1.3 %shard_map.53 = (f32[8,128,128]{2,1,0:T(8,128)S(1)}, bf16[6,8,128,128]{3,2,1,0:T(8,128)(2,1)}) custom-call(s32[8,128]{1,0:T(8,128)S(1)} %get-tuple-element.20.split_ref, bf16[8,128,128]{2,1,0:T(8,128)(2,1)S(1)} %get-tuple-element.21.diag_ref, bf16[6,8,128,128]{3,2,1,0:T(8,128)(2,1)S(1)} %bitcast.9, bf16[6,4,128,128]{3,2,1,0:T(8,128)(2,1)S(1)} %get-tuple-element.22.fine_ref, ...), custom_call_target="tpu_custom_call" | custom-call | flops 1073741824 | bytes 2097152 | tf_op jit(solution)/shard_map/pallas_call | solution.py:463
  28.3 0.0 collective-permute-done.5.xa_ref
  28.3 0.0 collective-permute-done.6.z_ref
  28.3 1.0 %shard_map.54.sum_ref = f32[8,128,128]{2,1,0:T(8,128)S(1)} custom-call(s32[8,128]{1,0:T(8,128)S(1)} %get-tuple-element.31.code_ref, f32[8,128,128]{2,1,0:T(8,128)S(1)} %get-tuple-element.32.sum_ref, bf16[6,8,128,128]{3,2,1,0:T(8,128)(2,1)S(1)} %bitcast.10, bf16[1056,128]{1,0:T(8,128)(2,1)S(1)} %collective-permute-done.ha, ...), custom_call_target="tpu_custom_call" | custom-call | flops 1073741824 | bytes 2097152 | tf_op jit(solution)/shard_map/pallas_call | solution.py:467
  29.3 0.0 collective-permute-done.8.ya_ref
  29.3 0.0 collective-permute-done.9.yb_ref
  29.3 4.1 %collective-permute-done.7.xb_ref = bf16[4,128,128]{2,1,0:T(8,128)(2,1)S(1)} collective-permute-done((bf16[4,128,128]{2,1,0:T(8,128)(2,1)S(1)}, bf16[4,128,128]{2,1,0:T(8,128)(2,1)S(1)}, u32[]{:S(2)}, u32[]{:S(2)}) %collective-permute-start.7) | collective-permute-done | bytes 131104 | tf_op jit(solution)/shard_map/ppermute | solution.py:403
  33.4 1.3 %shard_map.55 = f32[8,128,128]{2,1,0:T(8,128)} custom-call(s32[8,128]{1,0:T(8,128)S(1)} %get-tuple-element.20.split_ref, s32[8,128]{1,0:T(8,128)S(1)} %get-tuple-element.31.code_ref, f32[8,128,128]{2,1,0:T(8,128)S(1)} %shard_map.54.sum_ref, bf16[6,8,128,128]{3,2,1,0:T(8,128)(2,1)S(1)} %bitcast.11, bf16[1056,128]{1,0:T(8,128)(2,1)S(1)} %collective-permute-done.1.hb, ...), custom_call_target="tpu_custom_call" | custom-call | flops 1073741824 | bytes 2097152 | tf_op jit(solution)/shard_map/pallas_call | solution.py:470
Async XLA Ops:
  1.9 12.6 %collective-permute-start = (bf16[1056,128]{1,0:T(8,128)(2,1)S(1)}, bf16[1056,128]{1,0:T(8,128)(2,1)S(1)}, u32[]{:S(2)}, u32[]{:S(2)}) collective-permute-start(bf16[1056,128]{1,0:T(8,128)(2,1)S(1)} %get-tuple-element.26), channel_id=1, source_target_pairs={{0,16},{32,48},{64,80},{96,112},{16,0},{48,32},{80,64},{112,96},{1... | collective-permute-start | bytes 811016 | tf_op jit(solution)/shard_map/ppermute | solution.py:403
  3.5 13.4 %collective-permute-start.1 = (bf16[1056,128]{1,0:T(8,128)(2,1)S(1)}, bf16[1056,128]{1,0:T(8,128)(2,1)S(1)}, u32[]{:S(2)}, u32[]{:S(2)}) collective-permute-start(bf16[1056,128]{1,0:T(8,128)(2,1)S(1)} %get-tuple-element.27), channel_id=1, source_target_pairs={{16,32},{48,64},{80,96},{32,16},{64,48},{96,80},{17,33},{49,65},{8... | collective-permute-start | bytes 811016 | tf_op jit(solution)/shard_map/ppermute | solution.py:403
  7.6 9.4 %collective-permute-start.4 = (bf16[1056,128]{1,0:T(8,128)(2,1)S(1)}, bf16[1056,128]{1,0:T(8,128)(2,1)S(1)}, u32[]{:S(2)}, u32[]{:S(2)}) collective-permute-start(bf16[1056,128]{1,0:T(8,128)(2,1)S(1)} %get-tuple-element.28), channel_id=1, source_target_pairs={{0,1},{1,0},{2,3},{3,2},{4,5},{5,4},{6,7},{7,6},{8,9},{9,8},{10,11... | collective-permute-start | bytes 811016 | tf_op jit(solution)/shard_map/ppermute | solution.py:403
  7.7 6.8 %collective-permute-start.3 = (f32[16,128]{1,0:T(8,128)S(1)}, f32[16,128]{1,0:T(8,128)S(1)}, u32[]{:S(2)}, u32[]{:S(2)}) collective-permute-start(f32[16,128]{1,0:T(8,128)S(1)} %get-tuple-element.25.facts_ref), channel_id=1, source_target_pairs={{2,4},{6,8},{10,12},{4,2},{8,6},{12,10},{3,5},{7,9},{11,13},{5,3},... | collective-permute-start | bytes 24584 | tf_op jit(solution)/shard_map/ppermute | solution.py:403
  10.1 4.4 %collective-permute-start.2 = (f32[16,128]{1,0:T(8,128)S(1)}, f32[16,128]{1,0:T(8,128)S(1)}, u32[]{:S(2)}, u32[]{:S(2)}) collective-permute-start(f32[16,128]{1,0:T(8,128)S(1)} %get-tuple-element.25.facts_ref), channel_id=1, source_target_pairs={{0,2},{4,6},{8,10},{12,14},{2,0},{6,4},{10,8},{14,12},{1,3},{5,7},... | collective-permute-start | bytes 24584 | tf_op jit(solution)/shard_map/ppermute | solution.py:403
  17.0 10.0 %copy-start = (bf16[6,1,4,2,128,128]{5,4,3,2,1,0:T(8,128)(2,1)S(1)}, bf16[6,1,4,2,128,128]{5,4,3,2,1,0:T(8,128)(2,1)}, u32[]{:S(2)}) copy-start(bf16[6,1,4,2,128,128]{5,4,3,2,1,0:T(8,128)(2,1)} %param.4) | copy-start | bytes 4718596
  17.5 10.8 %collective-permute-start.5 = (bf16[4,128,128]{2,1,0:T(8,128)(2,1)S(1)}, bf16[4,128,128]{2,1,0:T(8,128)(2,1)S(1)}, u32[]{:S(2)}, u32[]{:S(2)}) collective-permute-start(bf16[4,128,128]{2,1,0:T(8,128)(2,1)S(1)} %get-tuple-element.33), channel_id=1, source_target_pairs={{0,16},{32,48},{64,80},{96,112},{16,0},{48,32},{80,64},{112,96},{1... | collective-permute-start | bytes 393224 | tf_op jit(solution)/shard_map/ppermute | solution.py:403
  17.6 10.7 %collective-permute-start.6 = (bf16[4,128,128]{2,1,0:T(8,128)(2,1)S(1)}, bf16[4,128,128]{2,1,0:T(8,128)(2,1)S(1)}, u32[]{:S(2)}, u32[]{:S(2)}) collective-permute-start(bf16[4,128,128]{2,1,0:T(8,128)(2,1)S(1)} %get-tuple-element.34), channel_id=1, source_target_pairs={{0,1},{1,0},{2,3},{3,2},{4,5},{5,4},{6,7},{7,6},{8,9},{9,8},{10,11... | collective-permute-start | bytes 393224 | tf_op jit(solution)/shard_map/ppermute | solution.py:403
  17.7 11.6 %collective-permute-start.8 = (bf16[2,1,128,128]{3,2,1,0:T(8,128)(2,1)S(1)}, bf16[2,1,128,128]{3,2,1,0:T(8,128)(2,1)S(1)}, u32[]{:S(2)}, u32[]{:S(2)}) collective-permute-start(bf16[2,1,128,128]{3,2,1,0:T(8,128)(2,1)S(1)} %get-tuple-element.36), channel_id=1, source_target_pairs={{0,2},{4,6},{8,10},{12,14},{2,0},{6,4},{10,8},{14,12},{1,3},{5,7},... | collective-permute-start | bytes 196616 | tf_op jit(solution)/shard_map/ppermute | solution.py:403
  18.2 11.1 %collective-permute-start.9 = (bf16[2,1,128,128]{3,2,1,0:T(8,128)(2,1)S(1)}, bf16[2,1,128,128]{3,2,1,0:T(8,128)(2,1)S(1)}, u32[]{:S(2)}, u32[]{:S(2)}) collective-permute-start(bf16[2,1,128,128]{3,2,1,0:T(8,128)(2,1)S(1)} %get-tuple-element.37), channel_id=1, source_target_pairs={{2,4},{6,8},{10,12},{4,2},{8,6},{12,10},{3,5},{7,9},{11,13},{5,3},... | collective-permute-start | bytes 196616 | tf_op jit(solution)/shard_map/ppermute | solution.py:403
  22.7 10.8 %collective-permute-start.7 = (bf16[4,128,128]{2,1,0:T(8,128)(2,1)S(1)}, bf16[4,128,128]{2,1,0:T(8,128)(2,1)S(1)}, u32[]{:S(2)}, u32[]{:S(2)}) collective-permute-start(bf16[4,128,128]{2,1,0:T(8,128)(2,1)S(1)} %get-tuple-element.35), channel_id=1, source_target_pairs={{16,32},{48,64},{80,96},{32,16},{64,48},{96,80},{17,33},{49,65},{8... | collective-permute-start | bytes 393224 | tf_op jit(solution)/shard_map/ppermute | solution.py:403

commit v8 on v7

--- a/solution.py
+++ b/solution.py
@@ -366,17 +366,25 @@
         total_ref[2 * c], total_ref[2 * c + 1] = totals
 
 
+def late_kernel(code_ref, sum_ref, face_ref, hb, xb_ref, total_ref):
+    gx = lax.axis_index("gx")
+    code = code_ref[...][0, 0]
+    for c in range(4):
+        arrived = [from_four(bit_at(code, 4 + c), gx % 2, hb, xb_ref, c)]
+        totals = added(c, arrived, sum_ref, face_ref)
+        total_ref[2 * c], total_ref[2 * c + 1] = totals
+
+
 def coarse_kernel(
-    split_ref, code_ref, sum_ref, face_ref, hb, xb_ref, ya_ref, yb_ref,
-    coarse_ref, total_ref, sems,
+    split_ref, code_ref, sum_ref, face_ref, ya_ref, yb_ref, coarse_ref, total_ref, sems
 ):
-    gx, gy = lax.axis_index("gx"), lax.axis_index("gy")
+    gy = lax.axis_index("gy")
     code = code_ref[...][0, 0]
     up = gy % 2 == 0
     flags = split_ref[...][0, 0]
     copies = []
     for c in (1, 2, 0, 3):
-        arrived = [from_four(bit_at(code, 4 + c), gx % 2, hb, xb_ref, c)]
+        arrived = []
         if c in (0, 3):
             first = up if c == 3 else jnp.logical_not(up)
             edge = 0 if c == 3 else 3
@@ -385,11 +393,13 @@
             arrived.append((z, 3 if c == 3 else 2, *pair))
         totals = added(c, arrived, sum_ref, face_ref)
         for k in range(2):
-            e = 2 * c + k
             keep = split_at(flags, c, k) == 1
-            total_ref[e] = jnp.where(keep, totals[k], 0.0)
-            copies.append(pltpu.make_async_copy(total_ref.at[e], coarse_ref.at[e], sems.at[e]))
-            copies[-1].start()
+            total_ref[2 * c + k] = jnp.where(keep, totals[k], 0.0)
+        pair = pl.ds(2 * c, 2)
+        copies.append(
+            pltpu.make_async_copy(total_ref.at[pair], coarse_ref.at[pair], sems.at[c])
+        )
+        copies[-1].start()
     for copy in copies:
         copy.wait()
 
@@ -467,10 +477,13 @@
     total = call(
         middle_kernel, sds((8, B, B), F32), [VMEM] * 7, VMEM, [], 1 << 30,
     )(code, total, face, ha, hz, xa, z)
+    total = call(
+        late_kernel, sds((8, B, B), F32), [VMEM] * 5, VMEM, [], 1 << 30,
+    )(code, total, face, hb, xb)
     coarse = call(
-        coarse_kernel, sds((8, B, B), F32), [VMEM] * 8, HBM,
-        [pltpu.VMEM((8, B, B), F32), dma((8,))], 1 << 30,
-    )(flags, code, total, face, hb, xb, ya, yb)
+        coarse_kernel, sds((8, B, B), F32), [VMEM] * 6, HBM,
+        [pltpu.VMEM((8, B, B), F32), dma((4,))], 1 << 30,
+    )(flags, code, total, face, ya, yb)
     return interp.reshape(face_blocks.shape), coarse.reshape(diag_blocks.shape)
 
 

time: 35 us -> 35 us (level)
    pallas_call x1 -> x2, Pallas kernels: 1.29 us -> 1.34 us  [the longest x1 0.93 us: on_device(): call(coarse_kernel, sds((8, B, B), F32), [VMEM] * 6, HBM, [pltpu.VMEM((8,...]
  transfers between devices with their start and end apart: 10 -> 10, of which waited for: 2 -> 2; matrix products, arithmetic and copies ran while one was open for 0% -> 0% of each run, Pallas kernels for 14% -> 16%
where the time goes in v8:
time: 35 us; the launch traced here: 34.8 us
  starting transfers between devices  19.2 us (55%)
  Pallas kernels  8.13 us (23%)
  waiting for transfers between devices  6.62 us (19%)
  between operations  0.79 us (2%)
    ppermute x10, starting transfers between devices, swap(): return lax.ppermute(x, axis, matching(lax.axis_size(axis), start))  19.2 us
    ppermute x10, waiting for transfers between devices, swap(): return lax.ppermute(x, axis, matching(lax.axis_size(axis), start))  6.62 us
    pallas_call x1, Pallas kernels, on_device(): call(inverse_kernel, (sds((6, 4, B, B), F32), sds((48, B), F32), blocks(6...  2.75 us
    pallas_call x1, Pallas kernels, on_device(): call(near_kernel, (sds((8, B, B), F32), blocks(6, 8)), [VMEM] + [VMEM] *...  1.28 us
    pallas_call x1, Pallas kernels, on_device(): call(facts_kernel, (sds((16, B), F32), sds((8, B), jnp.int32), blocks(8),...  1.26 us
    pallas_call x1, Pallas kernels, on_device(): call(middle_kernel, sds((8, B, B), F32), [VMEM] * 7, VMEM, [], 1 << 30)  0.97 us
    pallas_call x1, Pallas kernels, on_device(): call(coarse_kernel, sds((8, B, B), F32), [VMEM] * 6, HBM, [pltpu.VMEM((8,...  0.93 us
  transfers between devices with their start and end apart: 10, of which 2 were waited for; matrix products, arithmetic and copies ran while one was open for 0% of the time, Pallas kernels for 16%

profile of v8, /device:TPU:98, one launch (start us, length us, event | category | flops | bytes accessed | tf_op | source)
XLA Modules:
  0.0 34.8 jit_solution(14188906368291210696)
XLA Ops:
  0.6 1.3 %shard_map.50 = (f32[16,128]{1,0:T(8,128)S(1)}, s32[8,128]{1,0:T(8,128)S(1)}, bf16[8,128,128]{2,1,0:T(8,128)(2,1)S(1)}, bf16[1056,128]{1,0:T(8,128)(2,1)S(1)}, b...) custom-call(s32[1,2,4]{2,1,0:T(2,128)} %bitcast.14, bf16[8,128,128]{2,1,0:T(8,128)(2,1)} %bitcast.13, ...), custom_call_target="tpu_custom_call" | custom-call | flops 1048576 | bytes 2097152 | tf_op jit(solution)/shard_map/pallas_call | solution.py:437
  1.9 1.7 %collective-permute-start = (bf16[1056,128]{1,0:T(8,128)(2,1)S(1)}, bf16[1056,128]{1,0:T(8,128)(2,1)S(1)}, u32[]{:S(2)}, u32[]{:S(2)}) collective-permute-start(bf16[1056,128]{1,0:T(8,128)(2,1)S(1)} %get-tuple-element.26), channel_id=1, source_target_pairs={{0,16},{32,48},{64,80},{96,112},{16,0},{48,32},{80,64},{112,96},{1... | collective-permute-start | bytes 811016 | tf_op jit(solution)/shard_map/ppermute | solution.py:413
  3.5 4.1 %collective-permute-start.1 = (bf16[1056,128]{1,0:T(8,128)(2,1)S(1)}, bf16[1056,128]{1,0:T(8,128)(2,1)S(1)}, u32[]{:S(2)}, u32[]{:S(2)}) collective-permute-start(bf16[1056,128]{1,0:T(8,128)(2,1)S(1)} %get-tuple-element.27), channel_id=1, source_target_pairs={{16,32},{48,64},{80,96},{32,16},{64,48},{96,80},{17,33},{49,65},{8... | collective-permute-start | bytes 811016 | tf_op jit(solution)/shard_map/ppermute | solution.py:413
  7.6 0.1 collective-permute-start.4
  7.7 2.3 %collective-permute-start.3 = (f32[16,128]{1,0:T(8,128)S(1)}, f32[16,128]{1,0:T(8,128)S(1)}, u32[]{:S(2)}, u32[]{:S(2)}) collective-permute-start(f32[16,128]{1,0:T(8,128)S(1)} %get-tuple-element.25.facts_ref), channel_id=1, source_target_pairs={{2,4},{6,8},{10,12},{4,2},{8,6},{12,10},{3,5},{7,9},{11,13},{5,3},... | collective-permute-start | bytes 24584 | tf_op jit(solution)/shard_map/ppermute | solution.py:413
  10.1 1.6 %collective-permute-start.2 = (f32[16,128]{1,0:T(8,128)S(1)}, f32[16,128]{1,0:T(8,128)S(1)}, u32[]{:S(2)}, u32[]{:S(2)}) collective-permute-start(f32[16,128]{1,0:T(8,128)S(1)} %get-tuple-element.25.facts_ref), channel_id=1, source_target_pairs={{0,2},{4,6},{8,10},{12,14},{2,0},{6,4},{10,8},{14,12},{1,3},{5,7},... | collective-permute-start | bytes 24584 | tf_op jit(solution)/shard_map/ppermute | solution.py:413
  11.7 2.8 %shard_map.51 = (f32[6,4,128,128]{3,2,1,0:T(8,128)S(1)}, f32[48,128]{1,0:T(8,128)S(1)}, bf16[6,4,128,128]{3,2,1,0:T(8,128)(2,1)S(1)}) custom-call(s32[8,128]{1,0:T(8,128)S(1)} %get-tuple-element.20.split_ref, bf16[8,128,128]{2,1,0:T(8,128)(2,1)S(1)} %get-tuple-element.21.diag_ref, bf16[6,8,128,128]{3,2,1,0:T(8,128)(2,1)} %bitcast.8), custom_call_target="tpu_custom_call" | custom-call | flops 1073741824 | bytes 2097152 | tf_op jit(solution)/shard_map/pallas_call | solution.py:453
  14.5 0.0 collective-permute-done.3.hd
  14.5 0.0 collective-permute-done.2.hc
  14.5 0.0 collective-permute-done.ha
  14.5 2.5 %collective-permute-done.1.hb = bf16[1056,128]{1,0:T(8,128)(2,1)S(1)} collective-permute-done((bf16[1056,128]{1,0:T(8,128)(2,1)S(1)}, bf16[1056,128]{1,0:T(8,128)(2,1)S(1)}, u32[]{:S(2)}, u32[]{:S(2)}) %collective-permute-start.1) | collective-permute-done | bytes 270368 | tf_op jit(solution)/shard_map/ppermute | solution.py:413
  17.0 0.0 collective-permute-done.4.hz
  17.0 0.0 copy-start
  17.0 0.5 %shard_map.52 = (s32[8,128]{1,0:T(8,128)S(1)}, bf16[4,128,128]{2,1,0:T(8,128)(2,1)S(1)}, bf16[4,128,128]{2,1,0:T(8,128)(2,1)S(1)}, bf16[2,1,128,128]{3,2,1,0:T(8...) custom-call(s32[8,128]{1,0:T(8,128)S(1)} %get-tuple-element.20.split, ...), custom_call_target="tpu_custom_call" | custom-call | flops 1073741824 | bytes 2097152 | tf_op jit(solution)/shard_map/pallas_call | solution.py:462
  17.5 0.1 collective-permute-start.5
  17.6 0.1 collective-permute-start.6
  17.7 0.5 %collective-permute-start.8 = (bf16[2,1,128,128]{3,2,1,0:T(8,128)(2,1)S(1)}, bf16[2,1,128,128]{3,2,1,0:T(8,128)(2,1)S(1)}, u32[]{:S(2)}, u32[]{:S(2)}) collective-permute-start(bf16[2,1,128,128]{3,2,1,0:T(8,128)(2,1)S(1)} %get-tuple-element.36), channel_id=1, source_target_pairs={{0,2},{4,6},{8,10},{12,14},{2,0},{6,4},{10,8},{14,12},{1,3},{5,7},... | collective-permute-start | bytes 196616 | tf_op jit(solution)/shard_map/ppermute | solution.py:413
  18.2 4.4 %collective-permute-start.9 = (bf16[2,1,128,128]{3,2,1,0:T(8,128)(2,1)S(1)}, bf16[2,1,128,128]{3,2,1,0:T(8,128)(2,1)S(1)}, u32[]{:S(2)}, u32[]{:S(2)}) collective-permute-start(bf16[2,1,128,128]{3,2,1,0:T(8,128)(2,1)S(1)} %get-tuple-element.37), channel_id=1, source_target_pairs={{2,4},{6,8},{10,12},{4,2},{8,6},{12,10},{3,5},{7,9},{11,13},{5,3},... | collective-permute-start | bytes 196616 | tf_op jit(solution)/shard_map/ppermute | solution.py:413
  22.7 4.4 %collective-permute-start.7 = (bf16[4,128,128]{2,1,0:T(8,128)(2,1)S(1)}, bf16[4,128,128]{2,1,0:T(8,128)(2,1)S(1)}, u32[]{:S(2)}, u32[]{:S(2)}) collective-permute-start(bf16[4,128,128]{2,1,0:T(8,128)(2,1)S(1)} %get-tuple-element.35), channel_id=1, source_target_pairs={{16,32},{48,64},{80,96},{32,16},{64,48},{96,80},{17,33},{49,65},{8... | collective-permute-start | bytes 393224 | tf_op jit(solution)/shard_map/ppermute | solution.py:413
  27.0 0.0 copy-done
  27.0 1.3 %shard_map.53 = (f32[8,128,128]{2,1,0:T(8,128)S(1)}, bf16[6,8,128,128]{3,2,1,0:T(8,128)(2,1)}) custom-call(s32[8,128]{1,0:T(8,128)S(1)} %get-tuple-element.20.split_ref, bf16[8,128,128]{2,1,0:T(8,128)(2,1)S(1)} %get-tuple-element.21.diag_ref, bf16[6,8,128,128]{3,2,1,0:T(8,128)(2,1)S(1)} %bitcast.9, bf16[6,4,128,128]{3,2,1,0:T(8,128)(2,1)S(1)} %get-tuple-element.22.fine_ref, ...), custom_call_target="tpu_custom_call" | custom-call | flops 1073741824 | bytes 2097152 | tf_op jit(solution)/shard_map/pallas_call | solution.py:473
  28.3 0.0 collective-permute-done.5.xa_ref
  28.3 0.0 collective-permute-done.6.z_ref
  28.3 1.0 %shard_map.54.sum_ref = f32[8,128,128]{2,1,0:T(8,128)S(1)} custom-call(s32[8,128]{1,0:T(8,128)S(1)} %get-tuple-element.31.code_ref, f32[8,128,128]{2,1,0:T(8,128)S(1)} %get-tuple-element.32.sum_ref, bf16[6,8,128,128]{3,2,1,0:T(8,128)(2,1)S(1)} %bitcast.10, bf16[1056,128]{1,0:T(8,128)(2,1)S(1)} %collective-permute-done.ha, ...), custom_call_target="tpu_custom_call" | custom-call | flops 1073741824 | bytes 2097152 | tf_op jit(solution)/shard_map/pallas_call | solution.py:477
  29.3 4.1 %collective-permute-done.7.xb_ref = bf16[4,128,128]{2,1,0:T(8,128)(2,1)S(1)} collective-permute-done((bf16[4,128,128]{2,1,0:T(8,128)(2,1)S(1)}, bf16[4,128,128]{2,1,0:T(8,128)(2,1)S(1)}, u32[]{:S(2)}, u32[]{:S(2)}) %collective-permute-start.7) | collective-permute-done | bytes 131104 | tf_op jit(solution)/shard_map/ppermute | solution.py:413
  33.4 0.4 %shard_map.55.sum_ref = f32[8,128,128]{2,1,0:T(8,128)S(1)} custom-call(s32[8,128]{1,0:T(8,128)S(1)} %get-tuple-element.31.code_ref, f32[8,128,128]{2,1,0:T(8,128)S(1)} %shard_map.54.sum_ref, bf16[6,8,128,128]{3,2,1,0:T(8,128)(2,1)S(1)} %bitcast.11, bf16[1056,128]{1,0:T(8,128)(2,1)S(1)} %collective-permute-done.1.hb, ...), custom_call_target="tpu_custom_call" | custom-call | flops 1073741824 | bytes 2097152 | tf_op jit(solution)/shard_map/pallas_call | solution.py:480
  33.8 0.0 collective-permute-done.8.ya_ref
  33.9 0.0 collective-permute-done.9.yb_ref
  33.9 0.9 %shard_map.56 = f32[8,128,128]{2,1,0:T(8,128)} custom-call(s32[8,128]{1,0:T(8,128)S(1)} %get-tuple-element.20.split_ref, s32[8,128]{1,0:T(8,128)S(1)} %get-tuple-element.31.code_ref, f32[8,128,128]{2,1,0:T(8,128)S(1)} %shard_map.55.sum_ref, bf16[6,8,128,128]{3,2,1,0:T(8,128)(2,1)S(1)} %bitcast.12, ...), custom_call_target="tpu_custom_call" | custom-call | flops 1073741824 | bytes 2097152 | tf_op jit(solution)/shard_map/pallas_call | solution.py:483
Async XLA Ops:
  1.9 12.6 %collective-permute-start = (bf16[1056,128]{1,0:T(8,128)(2,1)S(1)}, bf16[1056,128]{1,0:T(8,128)(2,1)S(1)}, u32[]{:S(2)}, u32[]{:S(2)}) collective-permute-start(bf16[1056,128]{1,0:T(8,128)(2,1)S(1)} %get-tuple-element.26), channel_id=1, source_target_pairs={{0,16},{32,48},{64,80},{96,112},{16,0},{48,32},{80,64},{112,96},{1... | collective-permute-start | bytes 811016 | tf_op jit(solution)/shard_map/ppermute | solution.py:413
  3.5 13.4 %collective-permute-start.1 = (bf16[1056,128]{1,0:T(8,128)(2,1)S(1)}, bf16[1056,128]{1,0:T(8,128)(2,1)S(1)}, u32[]{:S(2)}, u32[]{:S(2)}) collective-permute-start(bf16[1056,128]{1,0:T(8,128)(2,1)S(1)} %get-tuple-element.27), channel_id=1, source_target_pairs={{16,32},{48,64},{80,96},{32,16},{64,48},{96,80},{17,33},{49,65},{8... | collective-permute-start | bytes 811016 | tf_op jit(solution)/shard_map/ppermute | solution.py:413
  7.6 9.4 %collective-permute-start.4 = (bf16[1056,128]{1,0:T(8,128)(2,1)S(1)}, bf16[1056,128]{1,0:T(8,128)(2,1)S(1)}, u32[]{:S(2)}, u32[]{:S(2)}) collective-permute-start(bf16[1056,128]{1,0:T(8,128)(2,1)S(1)} %get-tuple-element.28), channel_id=1, source_target_pairs={{0,1},{1,0},{2,3},{3,2},{4,5},{5,4},{6,7},{7,6},{8,9},{9,8},{10,11... | collective-permute-start | bytes 811016 | tf_op jit(solution)/shard_map/ppermute | solution.py:413
  7.7 6.8 %collective-permute-start.3 = (f32[16,128]{1,0:T(8,128)S(1)}, f32[16,128]{1,0:T(8,128)S(1)}, u32[]{:S(2)}, u32[]{:S(2)}) collective-permute-start(f32[16,128]{1,0:T(8,128)S(1)} %get-tuple-element.25.facts_ref), channel_id=1, source_target_pairs={{2,4},{6,8},{10,12},{4,2},{8,6},{12,10},{3,5},{7,9},{11,13},{5,3},... | collective-permute-start | bytes 24584 | tf_op jit(solution)/shard_map/ppermute | solution.py:413
  10.1 4.4 %collective-permute-start.2 = (f32[16,128]{1,0:T(8,128)S(1)}, f32[16,128]{1,0:T(8,128)S(1)}, u32[]{:S(2)}, u32[]{:S(2)}) collective-permute-start(f32[16,128]{1,0:T(8,128)S(1)} %get-tuple-element.25.facts_ref), channel_id=1, source_target_pairs={{0,2},{4,6},{8,10},{12,14},{2,0},{6,4},{10,8},{14,12},{1,3},{5,7},... | collective-permute-start | bytes 24584 | tf_op jit(solution)/shard_map/ppermute | solution.py:413
  17.0 10.0 %copy-start = (bf16[6,1,4,2,128,128]{5,4,3,2,1,0:T(8,128)(2,1)S(1)}, bf16[6,1,4,2,128,128]{5,4,3,2,1,0:T(8,128)(2,1)}, u32[]{:S(2)}) copy-start(bf16[6,1,4,2,128,128]{5,4,3,2,1,0:T(8,128)(2,1)} %param.4) | copy-start | bytes 4718596
  17.5 10.8 %collective-permute-start.5 = (bf16[4,128,128]{2,1,0:T(8,128)(2,1)S(1)}, bf16[4,128,128]{2,1,0:T(8,128)(2,1)S(1)}, u32[]{:S(2)}, u32[]{:S(2)}) collective-permute-start(bf16[4,128,128]{2,1,0:T(8,128)(2,1)S(1)} %get-tuple-element.33), channel_id=1, source_target_pairs={{0,16},{32,48},{64,80},{96,112},{16,0},{48,32},{80,64},{112,96},{1... | collective-permute-start | bytes 393224 | tf_op jit(solution)/shard_map/ppermute | solution.py:413
  17.6 10.7 %collective-permute-start.6 = (bf16[4,128,128]{2,1,0:T(8,128)(2,1)S(1)}, bf16[4,128,128]{2,1,0:T(8,128)(2,1)S(1)}, u32[]{:S(2)}, u32[]{:S(2)}) collective-permute-start(bf16[4,128,128]{2,1,0:T(8,128)(2,1)S(1)} %get-tuple-element.34), channel_id=1, source_target_pairs={{0,1},{1,0},{2,3},{3,2},{4,5},{5,4},{6,7},{7,6},{8,9},{9,8},{10,11... | collective-permute-start | bytes 393224 | tf_op jit(solution)/shard_map/ppermute | solution.py:413
  17.7 16.1 %collective-permute-start.8 = (bf16[2,1,128,128]{3,2,1,0:T(8,128)(2,1)S(1)}, bf16[2,1,128,128]{3,2,1,0:T(8,128)(2,1)S(1)}, u32[]{:S(2)}, u32[]{:S(2)}) collective-permute-start(bf16[2,1,128,128]{3,2,1,0:T(8,128)(2,1)S(1)} %get-tuple-element.36), channel_id=1, source_target_pairs={{0,2},{4,6},{8,10},{12,14},{2,0},{6,4},{10,8},{14,12},{1,3},{5,7},... | collective-permute-start | bytes 196616 | tf_op jit(solution)/shard_map/ppermute | solution.py:413
  18.2 15.7 %collective-permute-start.9 = (bf16[2,1,128,128]{3,2,1,0:T(8,128)(2,1)S(1)}, bf16[2,1,128,128]{3,2,1,0:T(8,128)(2,1)S(1)}, u32[]{:S(2)}, u32[]{:S(2)}) collective-permute-start(bf16[2,1,128,128]{3,2,1,0:T(8,128)(2,1)S(1)} %get-tuple-element.37), channel_id=1, source_target_pairs={{2,4},{6,8},{10,12},{4,2},{8,6},{12,10},{3,5},{7,9},{11,13},{5,3},... | collective-permute-start | bytes 196616 | tf_op jit(solution)/shard_map/ppermute | solution.py:413
  22.7 10.8 %collective-permute-start.7 = (bf16[4,128,128]{2,1,0:T(8,128)(2,1)S(1)}, bf16[4,128,128]{2,1,0:T(8,128)(2,1)S(1)}, u32[]{:S(2)}, u32[]{:S(2)}) collective-permute-start(bf16[4,128,128]{2,1,0:T(8,128)(2,1)S(1)} %get-tuple-element.35), channel_id=1, source_target_pairs={{16,32},{48,64},{80,96},{32,16},{64,48},{96,80},{17,33},{49,65},{8... | collective-permute-start | bytes 393224 | tf_op jit(solution)/shard_map/ppermute | solution.py:413

commit v9 on v8

--- a/solution.py
+++ b/solution.py
@@ -12,6 +12,9 @@
 VMEM = pl.BlockSpec(memory_space=pltpu.VMEM)
 HBM = pl.BlockSpec(memory_space=pltpu.HBM)
 LIMIT = 24 * 1024 * 1024
+HALF = 64
+FACES = 272
+FACTS = 784
 
 
 def mm(a, b):
@@ -83,26 +86,53 @@
     copies[1].wait()
     for e in range(8):
         rows[pl.ds(e, 1), :] = square_sums(kept_ref[e])
-    norms = norms_of(rows[...])
+    norms = norms_of(rows[pl.ds(0, 8), :])
     facts_ref[pl.ds(0, 8), :] = norms
     parts = [part.astype(F32) for part in thirds(norms)] + [flags]
-    for ref in (xa_ref, xb_ref, z_ref):
+    for ref, start in ((xa_ref, FACTS), (xb_ref, FACTS), (z_ref, 8 * B)):
         for k in range(2):
             both = jnp.concatenate(parts[2 * k:2 * k + 2], axis=0)
-            ref[pl.ds(8 * B + 16 * k, 16), :] = both.astype(BF16)
+            ref[pl.ds(start + 16 * k, 16), :] = both.astype(BF16)
+    row = lax.broadcasted_iota(jnp.int32, (HALF, B), 0)
+    lane = lax.broadcasted_iota(jnp.int32, (HALF, B), 1)
+    rows[pl.ds(8, 8), :] = jnp.zeros((8, B), F32)
+    for c in range(4):
+        block = kept_ref[2 * c + splits[2 * c]].astype(F32)
+        top, bottom = block[:HALF], block[HALF:]
+        folded = jnp.where((lane >= HALF) | (row >= lane), top, pltpu.roll(bottom, HALF, 1))
+        folded = folded.astype(BF16)
+        rows[pl.ds(8 + c, 1), :] = jnp.sum(
+            jnp.where(row == lane - HALF, bottom, 0.0), axis=0, keepdims=True
+        )
+        for ref in (xa_ref, xb_ref):
+            ref[pl.ds(HALF * c, HALF), :] = folded
+    tail = jnp.concatenate([rows[pl.ds(8, 8), :], jnp.zeros((8, B), F32)], axis=0).astype(BF16)
+    for ref in (xa_ref, xb_ref):
+        ref[pl.ds(4 * HALF, 16), :] = tail
     for copy in copies[2:]:
         copy.wait()
     for c in range(4):
         e = 2 * c + splits[2 * c]
-        block = kept_ref[e]
         z_ref[pl.ds(B * c, B), :] = kept_ref[2 * c + 1 - gz]
         for ref, d in ((xa_ref, 1 - gx % 2), (xb_ref, gx % 2)):
-            ref[pl.ds(B * c, B), :] = block
-            ref[pl.ds(B * (4 + c), B), :] = faces[d, e]
-
-
-def facts_in(ref):
-    high, low = ref[pl.ds(8 * B, 16), :].astype(F32), ref[pl.ds(8 * B + 16, 16), :].astype(F32)
+            ref[pl.ds(FACES + B * c, B), :] = faces[d, e]
+
+
+def unfolded(ref, c):
+    row = lax.broadcasted_iota(jnp.int32, (HALF, B), 0)
+    lane = lax.broadcasted_iota(jnp.int32, (HALF, B), 1)
+    folded = ref[pl.ds(HALF * c, HALF), :].astype(F32)
+    turned = jnp.transpose(jnp.concatenate([folded, folded], axis=0))
+    corner = ref[pl.ds(4 * HALF, 16), :].astype(F32)[c:c + 1]
+    top = jnp.where((lane >= HALF) | (row >= lane), folded, turned[:HALF])
+    low = jnp.where(row < lane - HALF, pltpu.roll(folded, HALF, 1), turned[:HALF])
+    low = jnp.where(row == lane - HALF, corner, low)
+    bottom = jnp.where(lane < HALF, turned[HALF:], low)
+    return jnp.concatenate([top, bottom], axis=0).astype(BF16)
+
+
+def facts_in(ref, start):
+    high, low = ref[pl.ds(start, 16), :].astype(F32), ref[pl.ds(start + 16, 16), :].astype(F32)
     return high[:8] + high[8:] + low[:8], low[8:]
 
 
@@ -134,7 +164,7 @@
     powers = [one - start * a for a, _, _, start in parts]
     sums = [one + p for p in powers]
     powers = [p.astype(BF16) for p in powers]
-    for _ in range(4):
+    for _ in range(3):
         powers = [mm(p, p).astype(BF16) for p in powers]
         sums = [s + mm(s.astype(BF16), p) for s, p in zip(sums, powers)]
     guess = [
@@ -205,7 +235,7 @@
     depth = row % 2
     even_x, even_y = gx % 2 == 0, gy % 2 == 0
 
-    xa, xb, beyond = facts_in(ha), facts_in(hb), facts_in(hz)
+    xa, xb, beyond = facts_in(ha, FACTS), facts_in(hb, FACTS), facts_in(hz, 8 * B)
     ya, yb = (hc[pl.ds(0, 8), :], hc[pl.ds(8, 8), :]), (hd[pl.ds(0, 8), :], hd[pl.ds(8, 8), :])
 
     def neighbours(part):
@@ -268,7 +298,7 @@
     lane = lax.broadcasted_iota(jnp.int32, (8, B), 1)
     bit = jnp.where((row % 2 == 0) & (lane == 0), 1, 0) * lax.shift_left(1, row // 2)
     code = jnp.zeros((8, B), F32)
-    splits = [facts_in(ha)[1], facts_in(hb)[1], hc[pl.ds(8, 8), :], hd[pl.ds(8, 8), :]]
+    splits = [facts_in(ha, FACTS)[1], facts_in(hb, FACTS)[1], hc[pl.ds(8, 8), :], hd[pl.ds(8, 8), :]]
     for place, theirs in enumerate(splits):
         code = code + theirs * (bit * (1 << (4 * place))).astype(F32)
     code = jnp.sum(jnp.sum(code, axis=0, keepdims=True), axis=1, keepdims=True)
@@ -297,7 +327,8 @@
 
 
 def near_kernel(
-    split_ref, diag_ref, face_ref, fine_ref, all_ref, sum_ref, interp_ref, zero_ref, sems
+    split_ref, diag_ref, face_ref, fine_ref, all_ref, ha, hb, sum_ref, interp_ref, far_ref,
+    zero_ref, sems,
 ):
     flags = split_ref[...][0, 0]
     fines = [fine_of(flags, c) for c in range(4)]
@@ -329,6 +360,8 @@
             for z, part in parts[c]:
                 total = total + jnp.where(z == k, part, 0.0)
             sum_ref[2 * c + k] = total
+    for c in range(4):
+        far_ref[0, c], far_ref[1, c] = unfolded(ha, c), unfolded(hb, c)
     for copy in copies:
         copy.wait()
 
@@ -344,6 +377,10 @@
 def from_four(z, d, sent, interp, c):
     theirs, face = sent[pl.ds(B * c, B), :], sent[pl.ds(B * (4 + c), B), :]
     return computed(z, d, theirs, face, interp[c])
+
+
+def from_x(z, d, theirs, sent, interp, c):
+    return computed(z, d, theirs, sent[pl.ds(FACES + B * c, B), :], interp[c])
 
 
 def added(c, arrived, sum_ref, face_ref):
@@ -354,23 +391,23 @@
     return totals
 
 
-def middle_kernel(code_ref, sum_ref, face_ref, ha, hz, xa_ref, z_ref, total_ref):
+def middle_kernel(code_ref, sum_ref, face_ref, far_ref, ha, hz, xa_ref, z_ref, total_ref):
     gx, gz = lax.axis_index("gx"), lax.axis_index("gz")
     code = code_ref[...][0, 0]
     for c in range(4):
         arrived = [
             from_four(1 - gz, 5 - gz, hz, z_ref, c),
-            from_four(bit_at(code, c), 1 - gx % 2, ha, xa_ref, c),
+            from_x(bit_at(code, c), 1 - gx % 2, far_ref[0, c], ha, xa_ref, c),
         ]
         totals = added(c, arrived, sum_ref, face_ref)
         total_ref[2 * c], total_ref[2 * c + 1] = totals
 
 
-def late_kernel(code_ref, sum_ref, face_ref, hb, xb_ref, total_ref):
+def late_kernel(code_ref, sum_ref, face_ref, far_ref, hb, xb_ref, total_ref):
     gx = lax.axis_index("gx")
     code = code_ref[...][0, 0]
     for c in range(4):
-        arrived = [from_four(bit_at(code, 4 + c), gx % 2, hb, xb_ref, c)]
+        arrived = [from_x(bit_at(code, 4 + c), gx % 2, far_ref[1, c], hb, xb_ref, c)]
         totals = added(c, arrived, sum_ref, face_ref)
         total_ref[2 * c], total_ref[2 * c + 1] = totals
 
@@ -433,16 +470,16 @@
     dma = pltpu.SemaphoreType.DMA
     in_hbm = lambda x: pltpu.with_memory_space_constraint(x, pltpu.HBM)
     blocks = lambda *lead: sds(lead + (B, B), BF16)
-    packed = sds((8 * B + 32, B), BF16)
+    packed = lambda rows: sds((rows, B), BF16)
     facts, flags, diag, pa, pb, pz = call(
         facts_kernel,
         (
             sds((16, B), F32), sds((8, B), jnp.int32), blocks(8),
-            packed, packed, packed,
+            packed(FACTS + 32), packed(FACTS + 32), packed(8 * B + 32),
         ),
         [HBM] * 3, (VMEM,) * 6,
         [
-            pltpu.VMEM((8, B), F32), pltpu.SMEM((1, 2, 4), jnp.int32),
+            pltpu.VMEM((16, B), F32), pltpu.SMEM((1, 2, 4), jnp.int32),
             pltpu.VMEM((2, 8, B, B), BF16), dma((7,)),
         ],
         1 << 20,
@@ -470,16 +507,16 @@
     xa, xb = swap(xa, "gx", 0), swap(xb, "gx", 1)
     ya, yb = swap(ya, "gy", 0), swap(yb, "gy", 1)
     z = swap(z, "gz", 0)
-    total, interp = call(
-        near_kernel, (sds((8, B, B), F32), blocks(6, 8)), [VMEM] + [VMEM] * 4, (VMEM, HBM),
-        [pltpu.VMEM((6, B, B), BF16), dma((8,))], 1 << 30,
-    )(flags, diag, face, fine, both)
+    total, interp, far = call(
+        near_kernel, (sds((8, B, B), F32), blocks(6, 8), blocks(2, 4)), [VMEM] * 7,
+        (VMEM, HBM, VMEM), [pltpu.VMEM((6, B, B), BF16), dma((8,))], 1 << 30,
+    )(flags, diag, face, fine, both, ha, hb)
     total = call(
-        middle_kernel, sds((8, B, B), F32), [VMEM] * 7, VMEM, [], 1 << 30,
-    )(code, total, face, ha, hz, xa, z)
+        middle_kernel, sds((8, B, B), F32), [VMEM] * 8, VMEM, [], 1 << 30,
+    )(code, total, face, far, ha, hz, xa, z)
     total = call(
-        late_kernel, sds((8, B, B), F32), [VMEM] * 5, VMEM, [], 1 << 30,
-    )(code, total, face, hb, xb)
+        late_kernel, sds((8, B, B), F32), [VMEM] * 6, VMEM, [], 1 << 30,
+    )(code, total, face, far, hb, xb)
     coarse = call(
         coarse_kernel, sds((8, B, B), F32), [VMEM] * 6, HBM,
         [pltpu.VMEM((8, B, B), F32), dma((4,))], 1 << 30,

time: 35 us -> 34.3 us (0.980)
  transfers between devices with their start and end apart: 10 -> 10, of which waited for: 2 -> 2; matrix products, arithmetic and copies ran while one was open for 0% -> 0% of each run, Pallas kernels for 16% -> 15%
where the time goes in v9:
time: 34.3 us; the launch traced here: 34.1 us
  starting transfers between devices  19.1 us (56%)
  Pallas kernels  7.9 us (23%)
  waiting for transfers between devices  6.28 us (18%)
  between operations  0.79 us (2%)
    ppermute x10, starting transfers between devices, swap(): return lax.ppermute(x, axis, matching(lax.axis_size(axis), start))  19.1 us
    ppermute x10, waiting for transfers between devices, swap(): return lax.ppermute(x, axis, matching(lax.axis_size(axis), start))  6.28 us
    pallas_call x1, Pallas kernels, on_device(): call(inverse_kernel, (sds((6, 4, B, B), F32), sds((48, B), F32), blocks(6...  2.55 us
    pallas_call x1, Pallas kernels, on_device(): call(near_kernel, (sds((8, B, B), F32), blocks(6, 8), blocks(2, 4)), [VME...  1.28 us
    pallas_call x1, Pallas kernels, on_device(): call(facts_kernel, (sds((16, B), F32), sds((8, B), jnp.int32), blocks(8),...  1.22 us
    pallas_call x1, Pallas kernels, on_device(): call(middle_kernel, sds((8, B, B), F32), [VMEM] * 8, VMEM, [], 1 << 30)  0.97 us
    pallas_call x1, Pallas kernels, on_device(): call(coarse_kernel, sds((8, B, B), F32), [VMEM] * 6, HBM, [pltpu.VMEM((8,...  0.93 us
  transfers between devices with their start and end apart: 10, of which 2 were waited for; matrix products, arithmetic and copies ran while one was open for 0% of the time, Pallas kernels for 15%

profile of v9, /device:TPU:98, one launch (start us, length us, event | category | flops | bytes accessed | tf_op | source)
XLA Modules:
  0.0 34.1 jit_solution(15522743383175216724)
XLA Ops:
  0.6 1.2 %shard_map.50 = (f32[16,128]{1,0:T(8,128)S(1)}, s32[8,128]{1,0:T(8,128)S(1)}, bf16[8,128,128]{2,1,0:T(8,128)(2,1)S(1)}, bf16[816,128]{1,0:T(8,128)(2,1)S(1)}, bf...) custom-call(s32[1,2,4]{2,1,0:T(2,128)} %bitcast.14, bf16[8,128,128]{2,1,0:T(8,128)(2,1)} %bitcast.13, ...), custom_call_target="tpu_custom_call" | custom-call | flops 1048576 | bytes 2097152 | tf_op jit(solution)/shard_map/pallas_call | solution.py:474
  1.9 0.1 collective-permute-start.4
  2.0 1.7 %collective-permute-start = (bf16[816,128]{1,0:T(8,128)(2,1)S(1)}, bf16[816,128]{1,0:T(8,128)(2,1)S(1)}, u32[]{:S(2)}, u32[]{:S(2)}) collective-permute-start(bf16[816,128]{1,0:T(8,128)(2,1)S(1)} %get-tuple-element.27), channel_id=1, source_target_pairs={{0,16},{32,48},{64,80},{96,112},{16,0},{48,32},{80,64},{112,96},{1... | collective-permute-start | bytes 626696 | tf_op jit(solution)/shard_map/ppermute | solution.py:450
  3.6 4.1 %collective-permute-start.1 = (bf16[816,128]{1,0:T(8,128)(2,1)S(1)}, bf16[816,128]{1,0:T(8,128)(2,1)S(1)}, u32[]{:S(2)}, u32[]{:S(2)}) collective-permute-start(bf16[816,128]{1,0:T(8,128)(2,1)S(1)} %get-tuple-element.28), channel_id=1, source_target_pairs={{16,32},{48,64},{80,96},{32,16},{64,48},{96,80},{17,33},{49,65},{8... | collective-permute-start | bytes 626696 | tf_op jit(solution)/shard_map/ppermute | solution.py:450
  7.7 2.3 %collective-permute-start.3 = (f32[16,128]{1,0:T(8,128)S(1)}, f32[16,128]{1,0:T(8,128)S(1)}, u32[]{:S(2)}, u32[]{:S(2)}) collective-permute-start(f32[16,128]{1,0:T(8,128)S(1)} %get-tuple-element.26.facts_ref), channel_id=1, source_target_pairs={{2,4},{6,8},{10,12},{4,2},{8,6},{12,10},{3,5},{7,9},{11,13},{5,3},... | collective-permute-start | bytes 24584 | tf_op jit(solution)/shard_map/ppermute | solution.py:450
  10.0 1.6 %collective-permute-start.2 = (f32[16,128]{1,0:T(8,128)S(1)}, f32[16,128]{1,0:T(8,128)S(1)}, u32[]{:S(2)}, u32[]{:S(2)}) collective-permute-start(f32[16,128]{1,0:T(8,128)S(1)} %get-tuple-element.26.facts_ref), channel_id=1, source_target_pairs={{0,2},{4,6},{8,10},{12,14},{2,0},{6,4},{10,8},{14,12},{1,3},{5,7},... | collective-permute-start | bytes 24584 | tf_op jit(solution)/shard_map/ppermute | solution.py:450
  11.7 2.5 %shard_map.51 = (f32[6,4,128,128]{3,2,1,0:T(8,128)S(1)}, f32[48,128]{1,0:T(8,128)S(1)}, bf16[6,4,128,128]{3,2,1,0:T(8,128)(2,1)S(1)}) custom-call(s32[8,128]{1,0:T(8,128)S(1)} %get-tuple-element.21.split_ref, bf16[8,128,128]{2,1,0:T(8,128)(2,1)S(1)} %get-tuple-element.22.diag_ref, bf16[6,8,128,128]{3,2,1,0:T(8,128)(2,1)} %bitcast.8), custom_call_target="tpu_custom_call" | custom-call | flops 1073741824 | bytes 2097152 | tf_op jit(solution)/shard_map/pallas_call | solution.py:490
  14.2 0.0 collective-permute-done.3.hd
  14.2 0.0 collective-permute-done.2.hc
  14.3 0.0 collective-permute-done.ha
  14.3 2.0 %collective-permute-done.1.hb = bf16[816,128]{1,0:T(8,128)(2,1)S(1)} collective-permute-done((bf16[816,128]{1,0:T(8,128)(2,1)S(1)}, bf16[816,128]{1,0:T(8,128)(2,1)S(1)}, u32[]{:S(2)}, u32[]{:S(2)}) %collective-permute-start.1) | collective-permute-done | bytes 208928 | tf_op jit(solution)/shard_map/ppermute | solution.py:450
  16.3 0.0 collective-permute-done.4.hz
  16.3 0.0 copy-start
  16.3 0.5 %shard_map.52 = (s32[8,128]{1,0:T(8,128)S(1)}, bf16[4,128,128]{2,1,0:T(8,128)(2,1)S(1)}, bf16[4,128,128]{2,1,0:T(8,128)(2,1)S(1)}, bf16[2,1,128,128]{3,2,1,0:T(8...) custom-call(s32[8,128]{1,0:T(8,128)S(1)} %get-tuple-element.21.split, ...), custom_call_target="tpu_custom_call" | custom-call | flops 1073741824 | bytes 2097152 | tf_op jit(solution)/shard_map/pallas_call | solution.py:499
  16.9 0.1 collective-permute-start.5
  17.0 0.1 collective-permute-start.6
  17.0 0.5 %collective-permute-start.8 = (bf16[2,1,128,128]{3,2,1,0:T(8,128)(2,1)S(1)}, bf16[2,1,128,128]{3,2,1,0:T(8,128)(2,1)S(1)}, u32[]{:S(2)}, u32[]{:S(2)}) collective-permute-start(bf16[2,1,128,128]{3,2,1,0:T(8,128)(2,1)S(1)} %get-tuple-element.38), channel_id=1, source_target_pairs={{0,2},{4,6},{8,10},{12,14},{2,0},{6,4},{10,8},{14,12},{1,3},{5,7},... | collective-permute-start | bytes 196616 | tf_op jit(solution)/shard_map/ppermute | solution.py:450
  17.5 4.4 %collective-permute-start.9 = (bf16[2,1,128,128]{3,2,1,0:T(8,128)(2,1)S(1)}, bf16[2,1,128,128]{3,2,1,0:T(8,128)(2,1)S(1)}, u32[]{:S(2)}, u32[]{:S(2)}) collective-permute-start(bf16[2,1,128,128]{3,2,1,0:T(8,128)(2,1)S(1)} %get-tuple-element.39), channel_id=1, source_target_pairs={{2,4},{6,8},{10,12},{4,2},{8,6},{12,10},{3,5},{7,9},{11,13},{5,3},... | collective-permute-start | bytes 196616 | tf_op jit(solution)/shard_map/ppermute | solution.py:450
  22.0 4.3 %collective-permute-start.7 = (bf16[4,128,128]{2,1,0:T(8,128)(2,1)S(1)}, bf16[4,128,128]{2,1,0:T(8,128)(2,1)S(1)}, u32[]{:S(2)}, u32[]{:S(2)}) collective-permute-start(bf16[4,128,128]{2,1,0:T(8,128)(2,1)S(1)} %get-tuple-element.37), channel_id=1, source_target_pairs={{16,32},{48,64},{80,96},{32,16},{64,48},{96,80},{17,33},{49,65},{8... | collective-permute-start | bytes 393224 | tf_op jit(solution)/shard_map/ppermute | solution.py:450
  26.2 0.0 copy-done
  26.3 1.3 %shard_map.53 = (f32[8,128,128]{2,1,0:T(8,128)S(1)}, bf16[6,8,128,128]{3,2,1,0:T(8,128)(2,1)}, bf16[2,4,128,128]{3,2,1,0:T(8,128)(2,1)S(1)}) custom-call(s32[8,128]{1,0:T(8,128)S(1)} %get-tuple-element.21.split_ref, bf16[8,128,128]{2,1,0:T(8,128)(2,1)S(1)} %get-tuple-element.22.diag_ref, bf16[6,8,128,128]{3,2,1,0:T(8,128)(2,1)S(1)} %bitcast.9, ...), custom_call_target="tpu_custom_call" | custom-call | flops 1073741824 | bytes 2097152 | tf_op jit(solution)/shard_map/pallas_call | solution.py:510
  27.5 0.0 collective-permute-done.5.xa_ref
  27.6 0.0 collective-permute-done.6.z_ref
  27.6 1.0 %shard_map.54.sum_ref = f32[8,128,128]{2,1,0:T(8,128)S(1)} custom-call(s32[8,128]{1,0:T(8,128)S(1)} %get-tuple-element.32.code_ref, f32[8,128,128]{2,1,0:T(8,128)S(1)} %get-tuple-element.33.sum_ref, bf16[6,8,128,128]{3,2,1,0:T(8,128)(2,1)S(1)} %bitcast.10, bf16[2,4,128,128]{3,2,1,0:T(8,128)(2,1)S(1)} %get-tuple-element.34.far_ref, ...), custom_call_target="tpu_custom_call" | custom-call | flops 1073741824 | bytes 2097152 | tf_op jit(solution)/shard_map/pallas_call | solution.py:514
  28.5 4.2 %collective-permute-done.7.xb_ref = bf16[4,128,128]{2,1,0:T(8,128)(2,1)S(1)} collective-permute-done((bf16[4,128,128]{2,1,0:T(8,128)(2,1)S(1)}, bf16[4,128,128]{2,1,0:T(8,128)(2,1)S(1)}, u32[]{:S(2)}, u32[]{:S(2)}) %collective-permute-start.7) | collective-permute-done | bytes 131104 | tf_op jit(solution)/shard_map/ppermute | solution.py:450
  32.8 0.4 %shard_map.55.sum_ref = f32[8,128,128]{2,1,0:T(8,128)S(1)} custom-call(s32[8,128]{1,0:T(8,128)S(1)} %get-tuple-element.32.code_ref, f32[8,128,128]{2,1,0:T(8,128)S(1)} %shard_map.54.sum_ref, bf16[6,8,128,128]{3,2,1,0:T(8,128)(2,1)S(1)} %bitcast.11, bf16[2,4,128,128]{3,2,1,0:T(8,128)(2,1)S(1)} %get-tuple-element.34.far_ref, ...), custom_call_target="tpu_custom_call" | custom-call | flops 1073741824 | bytes 2097152 | tf_op jit(solution)/shard_map/pallas_call | solution.py:517
  33.2 0.0 collective-permute-done.8.ya_ref
  33.2 0.0 collective-permute-done.9.yb_ref
  33.2 0.9 %shard_map.56 = f32[8,128,128]{2,1,0:T(8,128)} custom-call(s32[8,128]{1,0:T(8,128)S(1)} %get-tuple-element.21.split_ref, s32[8,128]{1,0:T(8,128)S(1)} %get-tuple-element.32.code_ref, f32[8,128,128]{2,1,0:T(8,128)S(1)} %shard_map.55.sum_ref, bf16[6,8,128,128]{3,2,1,0:T(8,128)(2,1)S(1)} %bitcast.12, ...), custom_call_target="tpu_custom_call" | custom-call | flops 1073741824 | bytes 2097152 | tf_op jit(solution)/shard_map/pallas_call | solution.py:520
Async XLA Ops:
  1.9 14.5 %collective-permute-start.4 = (bf16[1056,128]{1,0:T(8,128)(2,1)S(1)}, bf16[1056,128]{1,0:T(8,128)(2,1)S(1)}, u32[]{:S(2)}, u32[]{:S(2)}) collective-permute-start(bf16[1056,128]{1,0:T(8,128)(2,1)S(1)} %get-tuple-element.29), channel_id=1, source_target_pairs={{0,1},{1,0},{2,3},{3,2},{4,5},{5,4},{6,7},{7,6},{8,9},{9,8},{10,11... | collective-permute-start | bytes 811016 | tf_op jit(solution)/shard_map/ppermute | solution.py:450
  2.0 12.3 %collective-permute-start = (bf16[816,128]{1,0:T(8,128)(2,1)S(1)}, bf16[816,128]{1,0:T(8,128)(2,1)S(1)}, u32[]{:S(2)}, u32[]{:S(2)}) collective-permute-start(bf16[816,128]{1,0:T(8,128)(2,1)S(1)} %get-tuple-element.27), channel_id=1, source_target_pairs={{0,16},{32,48},{64,80},{96,112},{16,0},{48,32},{80,64},{112,96},{1... | collective-permute-start | bytes 626696 | tf_op jit(solution)/shard_map/ppermute | solution.py:450
  3.6 12.7 %collective-permute-start.1 = (bf16[816,128]{1,0:T(8,128)(2,1)S(1)}, bf16[816,128]{1,0:T(8,128)(2,1)S(1)}, u32[]{:S(2)}, u32[]{:S(2)}) collective-permute-start(bf16[816,128]{1,0:T(8,128)(2,1)S(1)} %get-tuple-element.28), channel_id=1, source_target_pairs={{16,32},{48,64},{80,96},{32,16},{64,48},{96,80},{17,33},{49,65},{8... | collective-permute-start | bytes 626696 | tf_op jit(solution)/shard_map/ppermute | solution.py:450
  7.7 6.6 %collective-permute-start.3 = (f32[16,128]{1,0:T(8,128)S(1)}, f32[16,128]{1,0:T(8,128)S(1)}, u32[]{:S(2)}, u32[]{:S(2)}) collective-permute-start(f32[16,128]{1,0:T(8,128)S(1)} %get-tuple-element.26.facts_ref), channel_id=1, source_target_pairs={{2,4},{6,8},{10,12},{4,2},{8,6},{12,10},{3,5},{7,9},{11,13},{5,3},... | collective-permute-start | bytes 24584 | tf_op jit(solution)/shard_map/ppermute | solution.py:450
  10.0 4.2 %collective-permute-start.2 = (f32[16,128]{1,0:T(8,128)S(1)}, f32[16,128]{1,0:T(8,128)S(1)}, u32[]{:S(2)}, u32[]{:S(2)}) collective-permute-start(f32[16,128]{1,0:T(8,128)S(1)} %get-tuple-element.26.facts_ref), channel_id=1, source_target_pairs={{0,2},{4,6},{8,10},{12,14},{2,0},{6,4},{10,8},{14,12},{1,3},{5,7},... | collective-permute-start | bytes 24584 | tf_op jit(solution)/shard_map/ppermute | solution.py:450
  16.3 9.9 %copy-start = (bf16[6,1,4,2,128,128]{5,4,3,2,1,0:T(8,128)(2,1)S(1)}, bf16[6,1,4,2,128,128]{5,4,3,2,1,0:T(8,128)(2,1)}, u32[]{:S(2)}) copy-start(bf16[6,1,4,2,128,128]{5,4,3,2,1,0:T(8,128)(2,1)} %param.4) | copy-start | bytes 4718596
  16.9 10.7 %collective-permute-start.5 = (bf16[4,128,128]{2,1,0:T(8,128)(2,1)S(1)}, bf16[4,128,128]{2,1,0:T(8,128)(2,1)S(1)}, u32[]{:S(2)}, u32[]{:S(2)}) collective-permute-start(bf16[4,128,128]{2,1,0:T(8,128)(2,1)S(1)} %get-tuple-element.35), channel_id=1, source_target_pairs={{0,16},{32,48},{64,80},{96,112},{16,0},{48,32},{80,64},{112,96},{1... | collective-permute-start | bytes 393224 | tf_op jit(solution)/shard_map/ppermute | solution.py:450
  17.0 10.6 %collective-permute-start.6 = (bf16[4,128,128]{2,1,0:T(8,128)(2,1)S(1)}, bf16[4,128,128]{2,1,0:T(8,128)(2,1)S(1)}, u32[]{:S(2)}, u32[]{:S(2)}) collective-permute-start(bf16[4,128,128]{2,1,0:T(8,128)(2,1)S(1)} %get-tuple-element.36), channel_id=1, source_target_pairs={{0,1},{1,0},{2,3},{3,2},{4,5},{5,4},{6,7},{7,6},{8,9},{9,8},{10,11... | collective-permute-start | bytes 393224 | tf_op jit(solution)/shard_map/ppermute | solution.py:450
  17.0 16.1 %collective-permute-start.8 = (bf16[2,1,128,128]{3,2,1,0:T(8,128)(2,1)S(1)}, bf16[2,1,128,128]{3,2,1,0:T(8,128)(2,1)S(1)}, u32[]{:S(2)}, u32[]{:S(2)}) collective-permute-start(bf16[2,1,128,128]{3,2,1,0:T(8,128)(2,1)S(1)} %get-tuple-element.38), channel_id=1, source_target_pairs={{0,2},{4,6},{8,10},{12,14},{2,0},{6,4},{10,8},{14,12},{1,3},{5,7},... | collective-permute-start | bytes 196616 | tf_op jit(solution)/shard_map/ppermute | solution.py:450
  17.5 15.7 %collective-permute-start.9 = (bf16[2,1,128,128]{3,2,1,0:T(8,128)(2,1)S(1)}, bf16[2,1,128,128]{3,2,1,0:T(8,128)(2,1)S(1)}, u32[]{:S(2)}, u32[]{:S(2)}) collective-permute-start(bf16[2,1,128,128]{3,2,1,0:T(8,128)(2,1)S(1)} %get-tuple-element.39), channel_id=1, source_target_pairs={{2,4},{6,8},{10,12},{4,2},{8,6},{12,10},{3,5},{7,9},{11,13},{5,3},... | collective-permute-start | bytes 196616 | tf_op jit(solution)/shard_map/ppermute | solution.py:450
  22.0 10.8 %collective-permute-start.7 = (bf16[4,128,128]{2,1,0:T(8,128)(2,1)S(1)}, bf16[4,128,128]{2,1,0:T(8,128)(2,1)S(1)}, u32[]{:S(2)}, u32[]{:S(2)}) collective-permute-start(bf16[4,128,128]{2,1,0:T(8,128)(2,1)S(1)} %get-tuple-element.37), channel_id=1, source_target_pairs={{16,32},{48,64},{80,96},{32,16},{64,48},{96,80},{17,33},{49,65},{8... | collective-permute-start | bytes 393224 | tf_op jit(solution)/shard_map/ppermute | solution.py:450

commit v10 on v9

--- a/solution.py
+++ b/solution.py
@@ -403,38 +403,52 @@
         total_ref[2 * c], total_ref[2 * c + 1] = totals
 
 
-def late_kernel(code_ref, sum_ref, face_ref, far_ref, hb, xb_ref, total_ref):
+def late_kernel(
+    split_ref, code_ref, sum_ref, face_ref, far_ref, hb, xb_ref, total_ref, coarse_ref, done_ref, sems
+):
     gx = lax.axis_index("gx")
     code = code_ref[...][0, 0]
-    for c in range(4):
+    flags = split_ref[...][0, 0]
+    for c in (1, 2, 0, 3):
         arrived = [from_x(bit_at(code, 4 + c), gx % 2, far_ref[1, c], hb, xb_ref, c)]
         totals = added(c, arrived, sum_ref, face_ref)
-        total_ref[2 * c], total_ref[2 * c + 1] = totals
+        for k in range(2):
+            if c in (1, 2):
+                keep = split_at(flags, c, k) == 1
+                done_ref[2 * c + k - 2] = jnp.where(keep, totals[k], 0.0)
+            else:
+                total_ref[2 * (c // 3) + k] = totals[k]
+        if c == 2:
+            copy = pltpu.make_async_copy(done_ref, coarse_ref.at[pl.ds(2, 4)], sems.at[0])
+            copy.start()
+    copy.wait()
 
 
 def coarse_kernel(
-    split_ref, code_ref, sum_ref, face_ref, ya_ref, yb_ref, coarse_ref, total_ref, sems
+    split_ref, code_ref, sum_ref, face_ref, ya_ref, yb_ref, part_ref, coarse_ref, total_ref, sems
 ):
     gy = lax.axis_index("gy")
     code = code_ref[...][0, 0]
     up = gy % 2 == 0
     flags = split_ref[...][0, 0]
     copies = []
-    for c in (1, 2, 0, 3):
-        arrived = []
-        if c in (0, 3):
-            first = up if c == 3 else jnp.logical_not(up)
-            edge = 0 if c == 3 else 3
-            z = jnp.where(first, bit_at(code, 8 + edge), bit_at(code, 12 + edge))
-            pair = [jnp.where(first, ya_ref[k, 0], yb_ref[k, 0]) for k in range(2)]
-            arrived.append((z, 3 if c == 3 else 2, *pair))
-        totals = added(c, arrived, sum_ref, face_ref)
+    for c in (0, 3):
+        first = up if c == 3 else jnp.logical_not(up)
+        edge = 0 if c == 3 else 3
+        z = jnp.where(first, bit_at(code, 8 + edge), bit_at(code, 12 + edge))
+        interp, contrib = (jnp.where(first, ya_ref[k, 0], yb_ref[k, 0]) for k in range(2))
+        product = mm(face_ref[3 if c == 3 else 2, 2 * c + z], interp)
+        part = contrib.astype(F32) + product
         for k in range(2):
+            place = 2 * (c // 3) + k
+            total = sum_ref[place] + jnp.where(z == k, part, 0.0)
             keep = split_at(flags, c, k) == 1
-            total_ref[2 * c + k] = jnp.where(keep, totals[k], 0.0)
-        pair = pl.ds(2 * c, 2)
+            total_ref[place] = jnp.where(keep, total, 0.0)
         copies.append(
-            pltpu.make_async_copy(total_ref.at[pair], coarse_ref.at[pair], sems.at[c])
+            pltpu.make_async_copy(
+                total_ref.at[pl.ds(2 * (c // 3), 2)], coarse_ref.at[pl.ds(2 * c, 2)],
+                sems.at[c // 3],
+            )
         )
         copies[-1].start()
     for copy in copies:
@@ -450,7 +464,7 @@
     return lax.ppermute(x, axis, matching(lax.axis_size(axis), start))
 
 
-def call(body, out_shape, in_specs, out_specs, scratch, flops):
+def call(body, out_shape, in_specs, out_specs, scratch, flops, aliases={}):
     return pl.pallas_call(
         body,
         out_shape=out_shape,
@@ -459,6 +473,7 @@
         scratch_shapes=scratch,
         compiler_params=pltpu.CompilerParams(vmem_limit_bytes=LIMIT),
         cost_estimate=pl.CostEstimate(flops=flops, bytes_accessed=2 << 20, transcendentals=0),
+        input_output_aliases=aliases,
     )
 
 
@@ -514,13 +529,14 @@
     total = call(
         middle_kernel, sds((8, B, B), F32), [VMEM] * 8, VMEM, [], 1 << 30,
     )(code, total, face, far, ha, hz, xa, z)
-    total = call(
-        late_kernel, sds((8, B, B), F32), [VMEM] * 6, VMEM, [], 1 << 30,
-    )(code, total, face, far, hb, xb)
+    total, coarse = call(
+        late_kernel, (sds((4, B, B), F32), sds((8, B, B), F32)), [VMEM] * 7, (VMEM, HBM),
+        [pltpu.VMEM((4, B, B), F32), dma((1,))], 1 << 30,
+    )(flags, code, total, face, far, hb, xb)
     coarse = call(
-        coarse_kernel, sds((8, B, B), F32), [VMEM] * 6, HBM,
-        [pltpu.VMEM((8, B, B), F32), dma((4,))], 1 << 30,
-    )(flags, code, total, face, ya, yb)
+        coarse_kernel, sds((8, B, B), F32), [VMEM] * 6 + [HBM], HBM,
+        [pltpu.VMEM((4, B, B), F32), dma((2,))], 1 << 30, {6: 0},
+    )(flags, code, total, face, ya, yb, coarse)
     return interp.reshape(face_blocks.shape), coarse.reshape(diag_blocks.shape)
 
 

time: 34.3 us -> 35 us (1.020)
  the two profiles are of different devices: /device:TPU:98 before, /device:TPU:96 now
where the time goes in v10:
time: 35 us; the launch traced here: 34.8 us
  starting transfers between devices  17.7 us (51%)
  Pallas kernels  8.54 us (24%)
  waiting for transfers between devices  7.74 us (22%)
  between operations  0.78 us (2%)
    ppermute x10, starting transfers between devices, swap(): return lax.ppermute(x, axis, matching(lax.axis_size(axis), start))  17.7 us
    ppermute x10, waiting for transfers between devices, swap(): return lax.ppermute(x, axis, matching(lax.axis_size(axis), start))  7.74 us
    pallas_call x1, Pallas kernels, on_device(): call(inverse_kernel, (sds((6, 4, B, B), F32), sds((48, B), F32), blocks(6...  2.56 us
    pallas_call x1, Pallas kernels, on_device(): call(near_kernel, (sds((8, B, B), F32), blocks(6, 8), blocks(2, 4)), [VME...  1.28 us
    pallas_call x1, Pallas kernels, on_device(): call(facts_kernel, (sds((16, B), F32), sds((8, B), jnp.int32), blocks(8),...  1.22 us
    pallas_call x1, Pallas kernels, on_device(): call(late_kernel, (sds((4, B, B), F32), sds((8, B, B), F32)), [VMEM] * 7,...  1.06 us
    pallas_call x1, Pallas kernels, on_device(): call(middle_kernel, sds((8, B, B), F32), [VMEM] * 8, VMEM, [], 1 << 30)  0.97 us
    pallas_call x1, Pallas kernels, on_device(): call(coarse_kernel, sds((8, B, B), F32), [VMEM] * 6 + [HBM], HBM, [pltpu....  0.91 us
  transfers between devices with their start and end apart: 10, of which 3 were waited for; matrix products, arithmetic and copies ran while one was open for 0% of the time, Pallas kernels for 17%

profile of v10, /device:TPU:96, one launch (start us, length us, event | category | flops | bytes accessed | tf_op | source)
XLA Modules:
  0.0 34.8 jit_solution(17010852753012226397)
XLA Ops:
  0.6 1.2 %shard_map.50 = (f32[16,128]{1,0:T(8,128)S(1)}, s32[8,128]{1,0:T(8,128)S(1)}, bf16[8,128,128]{2,1,0:T(8,128)(2,1)S(1)}, bf16[816,128]{1,0:T(8,128)(2,1)S(1)}, bf...) custom-call(s32[1,2,4]{2,1,0:T(2,128)} %bitcast.14, bf16[8,128,128]{2,1,0:T(8,128)(2,1)} %bitcast.13, ...), custom_call_target="tpu_custom_call" | custom-call | flops 1048576 | bytes 2097152 | tf_op jit(solution)/shard_map/pallas_call | solution.py:489
  1.9 0.1 collective-permute-start.4
  2.0 1.7 %collective-permute-start = (bf16[816,128]{1,0:T(8,128)(2,1)S(1)}, bf16[816,128]{1,0:T(8,128)(2,1)S(1)}, u32[]{:S(2)}, u32[]{:S(2)}) collective-permute-start(bf16[816,128]{1,0:T(8,128)(2,1)S(1)} %get-tuple-element.29), channel_id=1, source_target_pairs={{0,16},{32,48},{64,80},{96,112},{16,0},{48,32},{80,64},{112,96},{1... | collective-permute-start | bytes 626696 | tf_op jit(solution)/shard_map/ppermute | solution.py:464
  3.6 4.1 %collective-permute-start.1 = (bf16[816,128]{1,0:T(8,128)(2,1)S(1)}, bf16[816,128]{1,0:T(8,128)(2,1)S(1)}, u32[]{:S(2)}, u32[]{:S(2)}) collective-permute-start(bf16[816,128]{1,0:T(8,128)(2,1)S(1)} %get-tuple-element.30), channel_id=1, source_target_pairs={{16,32},{48,64},{80,96},{32,16},{64,48},{96,80},{17,33},{49,65},{8... | collective-permute-start | bytes 626696 | tf_op jit(solution)/shard_map/ppermute | solution.py:464
  7.7 2.3 %collective-permute-start.3 = (f32[16,128]{1,0:T(8,128)S(1)}, f32[16,128]{1,0:T(8,128)S(1)}, u32[]{:S(2)}, u32[]{:S(2)}) collective-permute-start(f32[16,128]{1,0:T(8,128)S(1)} %get-tuple-element.28.facts_ref), channel_id=1, source_target_pairs={{2,4},{6,8},{10,12},{4,2},{8,6},{12,10},{3,5},{7,9},{11,13},{5,3},... | collective-permute-start | bytes 24584 | tf_op jit(solution)/shard_map/ppermute | solution.py:464
  10.0 0.1 collective-permute-start.2
  10.1 2.6 %shard_map.51 = (f32[6,4,128,128]{3,2,1,0:T(8,128)S(1)}, f32[48,128]{1,0:T(8,128)S(1)}, bf16[6,4,128,128]{3,2,1,0:T(8,128)(2,1)S(1)}) custom-call(s32[8,128]{1,0:T(8,128)S(1)} %get-tuple-element.23.split_ref, bf16[8,128,128]{2,1,0:T(8,128)(2,1)S(1)} %get-tuple-element.24.diag_ref, bf16[6,8,128,128]{3,2,1,0:T(8,128)(2,1)} %bitcast.8), custom_call_target="tpu_custom_call" | custom-call | flops 1073741824 | bytes 2097152 | tf_op jit(solution)/shard_map/pallas_call | solution.py:505
  12.7 1.4 %collective-permute-done.3.hd = f32[16,128]{1,0:T(8,128)S(1)} collective-permute-done((f32[16,128]{1,0:T(8,128)S(1)}, f32[16,128]{1,0:T(8,128)S(1)}, u32[]{:S(2)}, u32[]{:S(2)}) %collective-permute-start.3) | collective-permute-done | bytes 8224 | tf_op jit(solution)/shard_map/ppermute | solution.py:464
  14.1 0.0 collective-permute-done.2.hc
  14.1 0.0 collective-permute-done.ha
  14.1 2.2 %collective-permute-done.1.hb = bf16[816,128]{1,0:T(8,128)(2,1)S(1)} collective-permute-done((bf16[816,128]{1,0:T(8,128)(2,1)S(1)}, bf16[816,128]{1,0:T(8,128)(2,1)S(1)}, u32[]{:S(2)}, u32[]{:S(2)}) %collective-permute-start.1) | collective-permute-done | bytes 208928 | tf_op jit(solution)/shard_map/ppermute | solution.py:464
  16.3 0.0 collective-permute-done.4.hz
  16.3 0.0 copy-start
  16.3 0.5 %shard_map.52 = (s32[8,128]{1,0:T(8,128)S(1)}, bf16[4,128,128]{2,1,0:T(8,128)(2,1)S(1)}, bf16[4,128,128]{2,1,0:T(8,128)(2,1)S(1)}, bf16[2,1,128,128]{3,2,1,0:T(8...) custom-call(s32[8,128]{1,0:T(8,128)S(1)} %get-tuple-element.23.split, ...), custom_call_target="tpu_custom_call" | custom-call | flops 1073741824 | bytes 2097152 | tf_op jit(solution)/shard_map/pallas_call | solution.py:514
  16.9 0.1 collective-permute-start.5
  17.0 0.1 collective-permute-start.6
  17.0 0.5 %collective-permute-start.8 = (bf16[2,1,128,128]{3,2,1,0:T(8,128)(2,1)S(1)}, bf16[2,1,128,128]{3,2,1,0:T(8,128)(2,1)S(1)}, u32[]{:S(2)}, u32[]{:S(2)}) collective-permute-start(bf16[2,1,128,128]{3,2,1,0:T(8,128)(2,1)S(1)} %get-tuple-element.41), channel_id=1, source_target_pairs={{0,2},{4,6},{8,10},{12,14},{2,0},{6,4},{10,8},{14,12},{1,3},{5,7},... | collective-permute-start | bytes 196616 | tf_op jit(solution)/shard_map/ppermute | solution.py:464
  17.5 4.4 %collective-permute-start.9 = (bf16[2,1,128,128]{3,2,1,0:T(8,128)(2,1)S(1)}, bf16[2,1,128,128]{3,2,1,0:T(8,128)(2,1)S(1)}, u32[]{:S(2)}, u32[]{:S(2)}) collective-permute-start(bf16[2,1,128,128]{3,2,1,0:T(8,128)(2,1)S(1)} %get-tuple-element.42), channel_id=1, source_target_pairs={{2,4},{6,8},{10,12},{4,2},{8,6},{12,10},{3,5},{7,9},{11,13},{5,3},... | collective-permute-start | bytes 196616 | tf_op jit(solution)/shard_map/ppermute | solution.py:464
  22.0 4.4 %collective-permute-start.7 = (bf16[4,128,128]{2,1,0:T(8,128)(2,1)S(1)}, bf16[4,128,128]{2,1,0:T(8,128)(2,1)S(1)}, u32[]{:S(2)}, u32[]{:S(2)}) collective-permute-start(bf16[4,128,128]{2,1,0:T(8,128)(2,1)S(1)} %get-tuple-element.39), channel_id=1, source_target_pairs={{16,32},{48,64},{80,96},{32,16},{64,48},{96,80},{17,33},{49,65},{8... | collective-permute-start | bytes 393224 | tf_op jit(solution)/shard_map/ppermute | solution.py:464
  26.3 0.0 copy-done
  26.4 1.3 %shard_map.53 = (f32[8,128,128]{2,1,0:T(8,128)S(1)}, bf16[6,8,128,128]{3,2,1,0:T(8,128)(2,1)}, bf16[2,4,128,128]{3,2,1,0:T(8,128)(2,1)S(1)}) custom-call(s32[8,128]{1,0:T(8,128)S(1)} %get-tuple-element.23.split_ref, bf16[8,128,128]{2,1,0:T(8,128)(2,1)S(1)} %get-tuple-element.24.diag_ref, bf16[6,8,128,128]{3,2,1,0:T(8,128)(2,1)S(1)} %bitcast.9, ...), custom_call_target="tpu_custom_call" | custom-call | flops 1073741824 | bytes 2097152 | tf_op jit(solution)/shard_map/pallas_call | solution.py:525
  27.6 0.0 collective-permute-done.5.xa_ref
  27.7 0.0 collective-permute-done.6.z_ref
  27.7 1.0 %shard_map.54.sum_ref = f32[8,128,128]{2,1,0:T(8,128)S(1)} custom-call(s32[8,128]{1,0:T(8,128)S(1)} %get-tuple-element.34.code_ref, f32[8,128,128]{2,1,0:T(8,128)S(1)} %get-tuple-element.35.sum_ref, bf16[6,8,128,128]{3,2,1,0:T(8,128)(2,1)S(1)} %bitcast.10, bf16[2,4,128,128]{3,2,1,0:T(8,128)(2,1)S(1)} %get-tuple-element.36.far_ref, ...), custom_call_target="tpu_custom_call" | custom-call | flops 1073741824 | bytes 2097152 | tf_op jit(solution)/shard_map/pallas_call | solution.py:529
  28.6 4.1 %collective-permute-done.7.xb_ref = bf16[4,128,128]{2,1,0:T(8,128)(2,1)S(1)} collective-permute-done((bf16[4,128,128]{2,1,0:T(8,128)(2,1)S(1)}, bf16[4,128,128]{2,1,0:T(8,128)(2,1)S(1)}, u32[]{:S(2)}, u32[]{:S(2)}) %collective-permute-start.7) | collective-permute-done | bytes 131104 | tf_op jit(solution)/shard_map/ppermute | solution.py:464
  32.8 1.1 %shard_map.55 = (f32[4,128,128]{2,1,0:T(8,128)S(1)}, f32[8,128,128]{2,1,0:T(8,128)}) custom-call(s32[8,128]{1,0:T(8,128)S(1)} %get-tuple-element.23.split_ref, s32[8,128]{1,0:T(8,128)S(1)} %get-tuple-element.34.code_ref, f32[8,128,128]{2,1,0:T(8,128)S(1)} %shard_map.54.sum_ref, bf16[6,8,128,128]{3,2,1,0:T(8,128)(2,1)S(1)} %bitcast.11, ...), custom_call_target="tpu_custom_call" | custom-call | flops 1073741824 | bytes 2097152 | tf_op jit(solution)/shard_map/pallas_call | solution.py:532
  33.8 0.0 collective-permute-done.8.ya_ref
  33.8 0.0 collective-permute-done.9.yb_ref
  33.8 0.9 %shard_map.56 = f32[8,128,128]{2,1,0:T(8,128)} custom-call(s32[8,128]{1,0:T(8,128)S(1)} %get-tuple-element.23.split_ref, s32[8,128]{1,0:T(8,128)S(1)} %get-tuple-element.34.code_ref, f32[4,128,128]{2,1,0:T(8,128)S(1)} %get-tuple-element.40.sum_ref, bf16[6,8,128,128]{3,2,1,0:T(8,128)(2,1)S(1)} %bitcast.12, ...), custom_call_target="tpu_custom_call", output_to_operand_aliasing={{}: (6, {})} | custom-call | flops 1073741824 | bytes 2097152 | tf_op jit(solution)/shard_map/pallas_call | solution.py:536
Async XLA Ops:
  1.9 14.5 %collective-permute-start.4 = (bf16[1056,128]{1,0:T(8,128)(2,1)S(1)}, bf16[1056,128]{1,0:T(8,128)(2,1)S(1)}, u32[]{:S(2)}, u32[]{:S(2)}) collective-permute-start(bf16[1056,128]{1,0:T(8,128)(2,1)S(1)} %get-tuple-element.31), channel_id=1, source_target_pairs={{0,1},{1,0},{2,3},{3,2},{4,5},{5,4},{6,7},{7,6},{8,9},{9,8},{10,11... | collective-permute-start | bytes 811016 | tf_op jit(solution)/shard_map/ppermute | solution.py:464
  2.0 12.2 %collective-permute-start = (bf16[816,128]{1,0:T(8,128)(2,1)S(1)}, bf16[816,128]{1,0:T(8,128)(2,1)S(1)}, u32[]{:S(2)}, u32[]{:S(2)}) collective-permute-start(bf16[816,128]{1,0:T(8,128)(2,1)S(1)} %get-tuple-element.29), channel_id=1, source_target_pairs={{0,16},{32,48},{64,80},{96,112},{16,0},{48,32},{80,64},{112,96},{1... | collective-permute-start | bytes 626696 | tf_op jit(solution)/shard_map/ppermute | solution.py:464
  3.6 12.7 %collective-permute-start.1 = (bf16[816,128]{1,0:T(8,128)(2,1)S(1)}, bf16[816,128]{1,0:T(8,128)(2,1)S(1)}, u32[]{:S(2)}, u32[]{:S(2)}) collective-permute-start(bf16[816,128]{1,0:T(8,128)(2,1)S(1)} %get-tuple-element.30), channel_id=1, source_target_pairs={{16,32},{48,64},{80,96},{32,16},{64,48},{96,80},{17,33},{49,65},{8... | collective-permute-start | bytes 626696 | tf_op jit(solution)/shard_map/ppermute | solution.py:464
  7.7 6.4 %collective-permute-start.3 = (f32[16,128]{1,0:T(8,128)S(1)}, f32[16,128]{1,0:T(8,128)S(1)}, u32[]{:S(2)}, u32[]{:S(2)}) collective-permute-start(f32[16,128]{1,0:T(8,128)S(1)} %get-tuple-element.28.facts_ref), channel_id=1, source_target_pairs={{2,4},{6,8},{10,12},{4,2},{8,6},{12,10},{3,5},{7,9},{11,13},{5,3},... | collective-permute-start | bytes 24584 | tf_op jit(solution)/shard_map/ppermute | solution.py:464
  10.0 4.1 %collective-permute-start.2 = (f32[16,128]{1,0:T(8,128)S(1)}, f32[16,128]{1,0:T(8,128)S(1)}, u32[]{:S(2)}, u32[]{:S(2)}) collective-permute-start(f32[16,128]{1,0:T(8,128)S(1)} %get-tuple-element.28.facts_ref), channel_id=1, source_target_pairs={{0,2},{4,6},{8,10},{12,14},{2,0},{6,4},{10,8},{14,12},{1,3},{5,7},... | collective-permute-start | bytes 24584 | tf_op jit(solution)/shard_map/ppermute | solution.py:464
  16.3 10.0 %copy-start = (bf16[6,1,4,2,128,128]{5,4,3,2,1,0:T(8,128)(2,1)S(1)}, bf16[6,1,4,2,128,128]{5,4,3,2,1,0:T(8,128)(2,1)}, u32[]{:S(2)}) copy-start(bf16[6,1,4,2,128,128]{5,4,3,2,1,0:T(8,128)(2,1)} %param.4) | copy-start | bytes 4718596
  16.9 10.8 %collective-permute-start.5 = (bf16[4,128,128]{2,1,0:T(8,128)(2,1)S(1)}, bf16[4,128,128]{2,1,0:T(8,128)(2,1)S(1)}, u32[]{:S(2)}, u32[]{:S(2)}) collective-permute-start(bf16[4,128,128]{2,1,0:T(8,128)(2,1)S(1)} %get-tuple-element.37), channel_id=1, source_target_pairs={{0,16},{32,48},{64,80},{96,112},{16,0},{48,32},{80,64},{112,96},{1... | collective-permute-start | bytes 393224 | tf_op jit(solution)/shard_map/ppermute | solution.py:464
  17.0 10.7 %collective-permute-start.6 = (bf16[4,128,128]{2,1,0:T(8,128)(2,1)S(1)}, bf16[4,128,128]{2,1,0:T(8,128)(2,1)S(1)}, u32[]{:S(2)}, u32[]{:S(2)}) collective-permute-start(bf16[4,128,128]{2,1,0:T(8,128)(2,1)S(1)} %get-tuple-element.38), channel_id=1, source_target_pairs={{0,1},{1,0},{2,3},{3,2},{4,5},{5,4},{6,7},{7,6},{8,9},{9,8},{10,11... | collective-permute-start | bytes 393224 | tf_op jit(solution)/shard_map/ppermute | solution.py:464
  17.0 16.8 %collective-permute-start.8 = (bf16[2,1,128,128]{3,2,1,0:T(8,128)(2,1)S(1)}, bf16[2,1,128,128]{3,2,1,0:T(8,128)(2,1)S(1)}, u32[]{:S(2)}, u32[]{:S(2)}) collective-permute-start(bf16[2,1,128,128]{3,2,1,0:T(8,128)(2,1)S(1)} %get-tuple-element.41), channel_id=1, source_target_pairs={{0,2},{4,6},{8,10},{12,14},{2,0},{6,4},{10,8},{14,12},{1,3},{5,7},... | collective-permute-start | bytes 196616 | tf_op jit(solution)/shard_map/ppermute | solution.py:464
  17.5 16.3 %collective-permute-start.9 = (bf16[2,1,128,128]{3,2,1,0:T(8,128)(2,1)S(1)}, bf16[2,1,128,128]{3,2,1,0:T(8,128)(2,1)S(1)}, u32[]{:S(2)}, u32[]{:S(2)}) collective-permute-start(bf16[2,1,128,128]{3,2,1,0:T(8,128)(2,1)S(1)} %get-tuple-element.42), channel_id=1, source_target_pairs={{2,4},{6,8},{10,12},{4,2},{8,6},{12,10},{3,5},{7,9},{11,13},{5,3},... | collective-permute-start | bytes 196616 | tf_op jit(solution)/shard_map/ppermute | solution.py:464
  22.0 10.8 %collective-permute-start.7 = (bf16[4,128,128]{2,1,0:T(8,128)(2,1)S(1)}, bf16[4,128,128]{2,1,0:T(8,128)(2,1)S(1)}, u32[]{:S(2)}, u32[]{:S(2)}) collective-permute-start(bf16[4,128,128]{2,1,0:T(8,128)(2,1)S(1)} %get-tuple-element.39), channel_id=1, source_target_pairs={{16,32},{48,64},{80,96},{32,16},{64,48},{96,80},{17,33},{49,65},{8... | collective-permute-start | bytes 393224 | tf_op jit(solution)/shard_map/ppermute | solution.py:464

commit v11 on v9

--- a/solution.py
+++ b/solution.py
@@ -65,13 +65,14 @@
     gx, gz = lax.axis_index("gx"), lax.axis_index("gz")
     copies = [
         pltpu.make_async_copy(split_ref, held, sems.at[0]),
-        pltpu.make_async_copy(diag_ref, kept_ref, sems.at[1]),
+        pltpu.make_async_copy(diag_ref.at[pl.ds(0, 4)], kept_ref.at[pl.ds(0, 4)], sems.at[1]),
         pltpu.make_async_copy(face_ref.at[pl.ds(0, 2)], faces, sems.at[2]),
     ]
     for c in range(4):
         block, into = face_ref.at[5 - gz, 2 * c + 1 - gz], z_ref.at[pl.ds(B * (4 + c), B), :]
         copies.append(pltpu.make_async_copy(block, into, sems.at[3 + c]))
-    for copy in copies:
+    half = pltpu.make_async_copy(diag_ref.at[pl.ds(4, 4)], kept_ref.at[pl.ds(4, 4)], sems.at[7])
+    for copy in copies[:2] + [half] + copies[2:]:
         copy.start()
     copies[0].wait()
     row = lax.broadcasted_iota(jnp.int32, (8, B), 0)
@@ -85,6 +86,8 @@
     facts_ref[pl.ds(8, 8), :] = flags
     copies[1].wait()
     for e in range(8):
+        if e == 4:
+            half.wait()
         rows[pl.ds(e, 1), :] = square_sums(kept_ref[e])
     norms = norms_of(rows[pl.ds(0, 8), :])
     facts_ref[pl.ds(0, 8), :] = norms
@@ -480,7 +483,7 @@
         [HBM] * 3, (VMEM,) * 6,
         [
             pltpu.VMEM((16, B), F32), pltpu.SMEM((1, 2, 4), jnp.int32),
-            pltpu.VMEM((2, 8, B, B), BF16), dma((7,)),
+            pltpu.VMEM((2, 8, B, B), BF16), dma((8,)),
         ],
         1 << 20,
     )(in_hbm(split), in_hbm(diag), in_hbm(face))

time: 34.3 us -> 34.4 us (level)
  no operation moved by 1% of the time
where the time goes in v11:
time: 34.4 us; the launch traced here: 34.2 us
  starting transfers between devices  19.1 us (56%)
  Pallas kernels  7.98 us (23%)
  waiting for transfers between devices  6.26 us (18%)
  between operations  0.79 us (2%)
    ppermute x10, starting transfers between devices, swap(): return lax.ppermute(x, axis, matching(lax.axis_size(axis), start))  19.1 us
    ppermute x10, waiting for transfers between devices, swap(): return lax.ppermute(x, axis, matching(lax.axis_size(axis), start))  6.26 us
    pallas_call x1, Pallas kernels, on_device(): call(inverse_kernel, (sds((6, 4, B, B), F32), sds((48, B), F32), blocks(6...  2.56 us
    pallas_call x1, Pallas kernels, on_device(): call(facts_kernel, (sds((16, B), F32), sds((8, B), jnp.int32), blocks(8),...  1.29 us
    pallas_call x1, Pallas kernels, on_device(): call(near_kernel, (sds((8, B, B), F32), blocks(6, 8), blocks(2, 4)), [VME...  1.28 us
    pallas_call x1, Pallas kernels, on_device(): call(middle_kernel, sds((8, B, B), F32), [VMEM] * 8, VMEM, [], 1 << 30)  0.97 us
    pallas_call x1, Pallas kernels, on_device(): call(coarse_kernel, sds((8, B, B), F32), [VMEM] * 6, HBM, [pltpu.VMEM((8,...  0.93 us
  transfers between devices with their start and end apart: 10, of which 2 were waited for; matrix products, arithmetic and copies ran while one was open for 0% of the time, Pallas kernels for 15%

profile of v11, /device:TPU:98, one launch (start us, length us, event | category | flops | bytes accessed | tf_op | source)
XLA Modules:
  0.0 34.2 jit_solution(15278871558570990710)
XLA Ops:
  0.6 1.3 %shard_map.50 = (f32[16,128]{1,0:T(8,128)S(1)}, s32[8,128]{1,0:T(8,128)S(1)}, bf16[8,128,128]{2,1,0:T(8,128)(2,1)S(1)}, bf16[816,128]{1,0:T(8,128)(2,1)S(1)}, bf...) custom-call(s32[1,2,4]{2,1,0:T(2,128)} %bitcast.14, bf16[8,128,128]{2,1,0:T(8,128)(2,1)} %bitcast.13, ...), custom_call_target="tpu_custom_call" | custom-call | flops 1048576 | bytes 2097152 | tf_op jit(solution)/shard_map/pallas_call | solution.py:477
  1.9 0.1 collective-permute-start.4
  2.0 1.7 %collective-permute-start = (bf16[816,128]{1,0:T(8,128)(2,1)S(1)}, bf16[816,128]{1,0:T(8,128)(2,1)S(1)}, u32[]{:S(2)}, u32[]{:S(2)}) collective-permute-start(bf16[816,128]{1,0:T(8,128)(2,1)S(1)} %get-tuple-element.27), channel_id=1, source_target_pairs={{0,16},{32,48},{64,80},{96,112},{16,0},{48,32},{80,64},{112,96},{1... | collective-permute-start | bytes 626696 | tf_op jit(solution)/shard_map/ppermute | solution.py:453
  3.7 4.1 %collective-permute-start.1 = (bf16[816,128]{1,0:T(8,128)(2,1)S(1)}, bf16[816,128]{1,0:T(8,128)(2,1)S(1)}, u32[]{:S(2)}, u32[]{:S(2)}) collective-permute-start(bf16[816,128]{1,0:T(8,128)(2,1)S(1)} %get-tuple-element.28), channel_id=1, source_target_pairs={{16,32},{48,64},{80,96},{32,16},{64,48},{96,80},{17,33},{49,65},{8... | collective-permute-start | bytes 626696 | tf_op jit(solution)/shard_map/ppermute | solution.py:453
  7.7 2.3 %collective-permute-start.3 = (f32[16,128]{1,0:T(8,128)S(1)}, f32[16,128]{1,0:T(8,128)S(1)}, u32[]{:S(2)}, u32[]{:S(2)}) collective-permute-start(f32[16,128]{1,0:T(8,128)S(1)} %get-tuple-element.26.facts_ref), channel_id=1, source_target_pairs={{2,4},{6,8},{10,12},{4,2},{8,6},{12,10},{3,5},{7,9},{11,13},{5,3},... | collective-permute-start | bytes 24584 | tf_op jit(solution)/shard_map/ppermute | solution.py:453
  10.1 1.6 %collective-permute-start.2 = (f32[16,128]{1,0:T(8,128)S(1)}, f32[16,128]{1,0:T(8,128)S(1)}, u32[]{:S(2)}, u32[]{:S(2)}) collective-permute-start(f32[16,128]{1,0:T(8,128)S(1)} %get-tuple-element.26.facts_ref), channel_id=1, source_target_pairs={{0,2},{4,6},{8,10},{12,14},{2,0},{6,4},{10,8},{14,12},{1,3},{5,7},... | collective-permute-start | bytes 24584 | tf_op jit(solution)/shard_map/ppermute | solution.py:453
  11.7 2.6 %shard_map.51 = (f32[6,4,128,128]{3,2,1,0:T(8,128)S(1)}, f32[48,128]{1,0:T(8,128)S(1)}, bf16[6,4,128,128]{3,2,1,0:T(8,128)(2,1)S(1)}) custom-call(s32[8,128]{1,0:T(8,128)S(1)} %get-tuple-element.21.split_ref, bf16[8,128,128]{2,1,0:T(8,128)(2,1)S(1)} %get-tuple-element.22.diag_ref, bf16[6,8,128,128]{3,2,1,0:T(8,128)(2,1)} %bitcast.8), custom_call_target="tpu_custom_call" | custom-call | flops 1073741824 | bytes 2097152 | tf_op jit(solution)/shard_map/pallas_call | solution.py:493
  14.3 0.0 collective-permute-done.3.hd
  14.3 0.0 collective-permute-done.2.hc
  14.3 0.0 collective-permute-done.ha
  14.3 2.0 %collective-permute-done.1.hb = bf16[816,128]{1,0:T(8,128)(2,1)S(1)} collective-permute-done((bf16[816,128]{1,0:T(8,128)(2,1)S(1)}, bf16[816,128]{1,0:T(8,128)(2,1)S(1)}, u32[]{:S(2)}, u32[]{:S(2)}) %collective-permute-start.1) | collective-permute-done | bytes 208928 | tf_op jit(solution)/shard_map/ppermute | solution.py:453
  16.4 0.0 collective-permute-done.4.hz
  16.4 0.0 copy-start
  16.4 0.5 %shard_map.52 = (s32[8,128]{1,0:T(8,128)S(1)}, bf16[4,128,128]{2,1,0:T(8,128)(2,1)S(1)}, bf16[4,128,128]{2,1,0:T(8,128)(2,1)S(1)}, bf16[2,1,128,128]{3,2,1,0:T(8...) custom-call(s32[8,128]{1,0:T(8,128)S(1)} %get-tuple-element.21.split, ...), custom_call_target="tpu_custom_call" | custom-call | flops 1073741824 | bytes 2097152 | tf_op jit(solution)/shard_map/pallas_call | solution.py:502
  16.9 0.1 collective-permute-start.5
  17.0 0.1 collective-permute-start.6
  17.1 0.5 %collective-permute-start.8 = (bf16[2,1,128,128]{3,2,1,0:T(8,128)(2,1)S(1)}, bf16[2,1,128,128]{3,2,1,0:T(8,128)(2,1)S(1)}, u32[]{:S(2)}, u32[]{:S(2)}) collective-permute-start(bf16[2,1,128,128]{3,2,1,0:T(8,128)(2,1)S(1)} %get-tuple-element.38), channel_id=1, source_target_pairs={{0,2},{4,6},{8,10},{12,14},{2,0},{6,4},{10,8},{14,12},{1,3},{5,7},... | collective-permute-start | bytes 196616 | tf_op jit(solution)/shard_map/ppermute | solution.py:453
  17.6 4.4 %collective-permute-start.9 = (bf16[2,1,128,128]{3,2,1,0:T(8,128)(2,1)S(1)}, bf16[2,1,128,128]{3,2,1,0:T(8,128)(2,1)S(1)}, u32[]{:S(2)}, u32[]{:S(2)}) collective-permute-start(bf16[2,1,128,128]{3,2,1,0:T(8,128)(2,1)S(1)} %get-tuple-element.39), channel_id=1, source_target_pairs={{2,4},{6,8},{10,12},{4,2},{8,6},{12,10},{3,5},{7,9},{11,13},{5,3},... | collective-permute-start | bytes 196616 | tf_op jit(solution)/shard_map/ppermute | solution.py:453
  22.0 4.3 %collective-permute-start.7 = (bf16[4,128,128]{2,1,0:T(8,128)(2,1)S(1)}, bf16[4,128,128]{2,1,0:T(8,128)(2,1)S(1)}, u32[]{:S(2)}, u32[]{:S(2)}) collective-permute-start(bf16[4,128,128]{2,1,0:T(8,128)(2,1)S(1)} %get-tuple-element.37), channel_id=1, source_target_pairs={{16,32},{48,64},{80,96},{32,16},{64,48},{96,80},{17,33},{49,65},{8... | collective-permute-start | bytes 393224 | tf_op jit(solution)/shard_map/ppermute | solution.py:453
  26.3 0.0 copy-done
  26.3 1.3 %shard_map.53 = (f32[8,128,128]{2,1,0:T(8,128)S(1)}, bf16[6,8,128,128]{3,2,1,0:T(8,128)(2,1)}, bf16[2,4,128,128]{3,2,1,0:T(8,128)(2,1)S(1)}) custom-call(s32[8,128]{1,0:T(8,128)S(1)} %get-tuple-element.21.split_ref, bf16[8,128,128]{2,1,0:T(8,128)(2,1)S(1)} %get-tuple-element.22.diag_ref, bf16[6,8,128,128]{3,2,1,0:T(8,128)(2,1)S(1)} %bitcast.9, ...), custom_call_target="tpu_custom_call" | custom-call | flops 1073741824 | bytes 2097152 | tf_op jit(solution)/shard_map/pallas_call | solution.py:513
  27.6 0.0 collective-permute-done.5.xa_ref
  27.6 0.0 collective-permute-done.6.z_ref
  27.6 1.0 %shard_map.54.sum_ref = f32[8,128,128]{2,1,0:T(8,128)S(1)} custom-call(s32[8,128]{1,0:T(8,128)S(1)} %get-tuple-element.32.code_ref, f32[8,128,128]{2,1,0:T(8,128)S(1)} %get-tuple-element.33.sum_ref, bf16[6,8,128,128]{3,2,1,0:T(8,128)(2,1)S(1)} %bitcast.10, bf16[2,4,128,128]{3,2,1,0:T(8,128)(2,1)S(1)} %get-tuple-element.34.far_ref, ...), custom_call_target="tpu_custom_call" | custom-call | flops 1073741824 | bytes 2097152 | tf_op jit(solution)/shard_map/pallas_call | solution.py:517
  28.6 4.2 %collective-permute-done.7.xb_ref = bf16[4,128,128]{2,1,0:T(8,128)(2,1)S(1)} collective-permute-done((bf16[4,128,128]{2,1,0:T(8,128)(2,1)S(1)}, bf16[4,128,128]{2,1,0:T(8,128)(2,1)S(1)}, u32[]{:S(2)}, u32[]{:S(2)}) %collective-permute-start.7) | collective-permute-done | bytes 131104 | tf_op jit(solution)/shard_map/ppermute | solution.py:453
  32.8 0.4 %shard_map.55.sum_ref = f32[8,128,128]{2,1,0:T(8,128)S(1)} custom-call(s32[8,128]{1,0:T(8,128)S(1)} %get-tuple-element.32.code_ref, f32[8,128,128]{2,1,0:T(8,128)S(1)} %shard_map.54.sum_ref, bf16[6,8,128,128]{3,2,1,0:T(8,128)(2,1)S(1)} %bitcast.11, bf16[2,4,128,128]{3,2,1,0:T(8,128)(2,1)S(1)} %get-tuple-element.34.far_ref, ...), custom_call_target="tpu_custom_call" | custom-call | flops 1073741824 | bytes 2097152 | tf_op jit(solution)/shard_map/pallas_call | solution.py:520
  33.2 0.0 collective-permute-done.8.ya_ref
  33.2 0.0 collective-permute-done.9.yb_ref
  33.3 0.9 %shard_map.56 = f32[8,128,128]{2,1,0:T(8,128)} custom-call(s32[8,128]{1,0:T(8,128)S(1)} %get-tuple-element.21.split_ref, s32[8,128]{1,0:T(8,128)S(1)} %get-tuple-element.32.code_ref, f32[8,128,128]{2,1,0:T(8,128)S(1)} %shard_map.55.sum_ref, bf16[6,8,128,128]{3,2,1,0:T(8,128)(2,1)S(1)} %bitcast.12, ...), custom_call_target="tpu_custom_call" | custom-call | flops 1073741824 | bytes 2097152 | tf_op jit(solution)/shard_map/pallas_call | solution.py:523
Async XLA Ops:
  1.9 14.5 %collective-permute-start.4 = (bf16[1056,128]{1,0:T(8,128)(2,1)S(1)}, bf16[1056,128]{1,0:T(8,128)(2,1)S(1)}, u32[]{:S(2)}, u32[]{:S(2)}) collective-permute-start(bf16[1056,128]{1,0:T(8,128)(2,1)S(1)} %get-tuple-element.29), channel_id=1, source_target_pairs={{0,1},{1,0},{2,3},{3,2},{4,5},{5,4},{6,7},{7,6},{8,9},{9,8},{10,11... | collective-permute-start | bytes 811016 | tf_op jit(solution)/shard_map/ppermute | solution.py:453
  2.0 12.3 %collective-permute-start = (bf16[816,128]{1,0:T(8,128)(2,1)S(1)}, bf16[816,128]{1,0:T(8,128)(2,1)S(1)}, u32[]{:S(2)}, u32[]{:S(2)}) collective-permute-start(bf16[816,128]{1,0:T(8,128)(2,1)S(1)} %get-tuple-element.27), channel_id=1, source_target_pairs={{0,16},{32,48},{64,80},{96,112},{16,0},{48,32},{80,64},{112,96},{1... | collective-permute-start | bytes 626696 | tf_op jit(solution)/shard_map/ppermute | solution.py:453
  3.7 12.7 %collective-permute-start.1 = (bf16[816,128]{1,0:T(8,128)(2,1)S(1)}, bf16[816,128]{1,0:T(8,128)(2,1)S(1)}, u32[]{:S(2)}, u32[]{:S(2)}) collective-permute-start(bf16[816,128]{1,0:T(8,128)(2,1)S(1)} %get-tuple-element.28), channel_id=1, source_target_pairs={{16,32},{48,64},{80,96},{32,16},{64,48},{96,80},{17,33},{49,65},{8... | collective-permute-start | bytes 626696 | tf_op jit(solution)/shard_map/ppermute | solution.py:453
  7.7 6.6 %collective-permute-start.3 = (f32[16,128]{1,0:T(8,128)S(1)}, f32[16,128]{1,0:T(8,128)S(1)}, u32[]{:S(2)}, u32[]{:S(2)}) collective-permute-start(f32[16,128]{1,0:T(8,128)S(1)} %get-tuple-element.26.facts_ref), channel_id=1, source_target_pairs={{2,4},{6,8},{10,12},{4,2},{8,6},{12,10},{3,5},{7,9},{11,13},{5,3},... | collective-permute-start | bytes 24584 | tf_op jit(solution)/shard_map/ppermute | solution.py:453
  10.1 4.2 %collective-permute-start.2 = (f32[16,128]{1,0:T(8,128)S(1)}, f32[16,128]{1,0:T(8,128)S(1)}, u32[]{:S(2)}, u32[]{:S(2)}) collective-permute-start(f32[16,128]{1,0:T(8,128)S(1)} %get-tuple-element.26.facts_ref), channel_id=1, source_target_pairs={{0,2},{4,6},{8,10},{12,14},{2,0},{6,4},{10,8},{14,12},{1,3},{5,7},... | collective-permute-start | bytes 24584 | tf_op jit(solution)/shard_map/ppermute | solution.py:453
  16.4 9.9 %copy-start = (bf16[6,1,4,2,128,128]{5,4,3,2,1,0:T(8,128)(2,1)S(1)}, bf16[6,1,4,2,128,128]{5,4,3,2,1,0:T(8,128)(2,1)}, u32[]{:S(2)}) copy-start(bf16[6,1,4,2,128,128]{5,4,3,2,1,0:T(8,128)(2,1)} %param.4) | copy-start | bytes 4718596
  16.9 10.7 %collective-permute-start.5 = (bf16[4,128,128]{2,1,0:T(8,128)(2,1)S(1)}, bf16[4,128,128]{2,1,0:T(8,128)(2,1)S(1)}, u32[]{:S(2)}, u32[]{:S(2)}) collective-permute-start(bf16[4,128,128]{2,1,0:T(8,128)(2,1)S(1)} %get-tuple-element.35), channel_id=1, source_target_pairs={{0,16},{32,48},{64,80},{96,112},{16,0},{48,32},{80,64},{112,96},{1... | collective-permute-start | bytes 393224 | tf_op jit(solution)/shard_map/ppermute | solution.py:453
  17.0 10.6 %collective-permute-start.6 = (bf16[4,128,128]{2,1,0:T(8,128)(2,1)S(1)}, bf16[4,128,128]{2,1,0:T(8,128)(2,1)S(1)}, u32[]{:S(2)}, u32[]{:S(2)}) collective-permute-start(bf16[4,128,128]{2,1,0:T(8,128)(2,1)S(1)} %get-tuple-element.36), channel_id=1, source_target_pairs={{0,1},{1,0},{2,3},{3,2},{4,5},{5,4},{6,7},{7,6},{8,9},{9,8},{10,11... | collective-permute-start | bytes 393224 | tf_op jit(solution)/shard_map/ppermute | solution.py:453
  17.1 16.1 %collective-permute-start.8 = (bf16[2,1,128,128]{3,2,1,0:T(8,128)(2,1)S(1)}, bf16[2,1,128,128]{3,2,1,0:T(8,128)(2,1)S(1)}, u32[]{:S(2)}, u32[]{:S(2)}) collective-permute-start(bf16[2,1,128,128]{3,2,1,0:T(8,128)(2,1)S(1)} %get-tuple-element.38), channel_id=1, source_target_pairs={{0,2},{4,6},{8,10},{12,14},{2,0},{6,4},{10,8},{14,12},{1,3},{5,7},... | collective-permute-start | bytes 196616 | tf_op jit(solution)/shard_map/ppermute | solution.py:453
  17.6 15.7 %collective-permute-start.9 = (bf16[2,1,128,128]{3,2,1,0:T(8,128)(2,1)S(1)}, bf16[2,1,128,128]{3,2,1,0:T(8,128)(2,1)S(1)}, u32[]{:S(2)}, u32[]{:S(2)}) collective-permute-start(bf16[2,1,128,128]{3,2,1,0:T(8,128)(2,1)S(1)} %get-tuple-element.39), channel_id=1, source_target_pairs={{2,4},{6,8},{10,12},{4,2},{8,6},{12,10},{3,5},{7,9},{11,13},{5,3},... | collective-permute-start | bytes 196616 | tf_op jit(solution)/shard_map/ppermute | solution.py:453
  22.0 10.8 %collective-permute-start.7 = (bf16[4,128,128]{2,1,0:T(8,128)(2,1)S(1)}, bf16[4,128,128]{2,1,0:T(8,128)(2,1)S(1)}, u32[]{:S(2)}, u32[]{:S(2)}) collective-permute-start(bf16[4,128,128]{2,1,0:T(8,128)(2,1)S(1)} %get-tuple-element.37), channel_id=1, source_target_pairs={{16,32},{48,64},{80,96},{32,16},{64,48},{96,80},{17,33},{49,65},{8... | collective-permute-start | bytes 393224 | tf_op jit(solution)/shard_map/ppermute | solution.py:453
